TPU v7x, 512 devices: a whole 4x8x8 slice. The times are simulated.
512 devices in a mesh: ctx: 64 (over y, z), tp: 8 (over x, core).
Axes of the slice: x: 4, y: 8, z: 8, core: 2. Of those that a mesh axis runs over, the one named last changes fastest.
Arguments:
- inputs: bfloat16 [8192, 4096], P('ctx', 'tp'), may hold values from -6 to 6
- gate_in: bfloat16 [8192, 4096], P('ctx', 'tp'), may hold values from -6 to 6
- b_proj: bfloat16 [8192, 128], P('ctx'), may hold values from -0.5 to 0.5
- c_proj: bfloat16 [8192, 128], P('ctx'), may hold values from -0.5 to 0.5
- log_decay: float32 [32, 8192], P('tp', 'ctx'), may hold values from -0.75 to 0
- w_out: bfloat16 [4096, 4096], P('tp'), may hold values from -0.09375 to 0.09375
- cotangent: bfloat16 [8192, 4096], P(('ctx', 'tp')), may hold values from -6 to 6
Outputs:
- layer_out: bfloat16 [8192, 4096], P(('ctx', 'tp'))
- grad_inputs: bfloat16 [8192, 4096], P('ctx', 'tp')
- grad_gate: bfloat16 [8192, 4096], P('ctx', 'tp')
- grad_b: float32 [8192, 128], P(('ctx', 'tp'))
- grad_c: float32 [8192, 128], P(('ctx', 'tp'))
- grad_decay: float32 [32, 8192], P('tp', 'ctx')
All inputs are finite; a program needn't handle non-finite values.
Results may differ from a plain program's by a relative error of at most 0.017.
Values may be sent and summed in bfloat16 or wider, within the bound.
No kernel may reach another device: no remote copies, remote signals or barrier semaphores. Data moves between devices by JAX's collectives and lax.ppermute only.
A program may use at most 128 MiB of HBM per device.

v0:
```python
import jax
import jax.numpy as jnp
from jax import lax
from jax.sharding import PartitionSpec as P

BLOCK = 128


def entering(shard, axis, combine, identity, reverse):
    count, place = (lax.axis_size(axis), lax.axis_index(axis))
    everything = jax.tree.map(lambda part: lax.all_gather(part, axis), shard)
    start = jax.tree.map(
        lambda part, zero: jnp.broadcast_to(jnp.asarray(zero, part.dtype), part.shape),
        shard,
        identity,
    )

    def lap(k, before):
        at = count - 1 - k if reverse else k
        reached = at > place if reverse else at < place
        new = combine(before, jax.tree.map(lambda part: part[at], everything))
        return jax.tree.map(lambda a, b: jnp.where(reached, a, b), new, before)

    return lax.fori_loop(0, count, lap, start)


def compose(earlier, later_part):
    return (earlier[0] * later_part[0], later_part[0][:, None, None] * earlier[1] + later_part[1])


def carried(block_decay, block_terms, backward):
    if backward:
        block_decay = jnp.flip(block_decay, 0)
        block_terms = jnp.flip(block_terms, 0)
    head_count = block_decay.shape[1]

    def local_step(running, packed):
        state_level, product = running
        decay_step, term_block = packed
        return (
            (decay_step[:, None, None] * state_level + term_block, decay_step * product),
            (state_level, product),
        )

    initial = (jnp.zeros(block_terms.shape[1:], jnp.float32), jnp.ones((head_count,), jnp.float32))
    (dev_state, dev_decay), (local_in, decay_before) = lax.scan(
        local_step, initial, (block_decay, block_terms)
    )
    identity = (jnp.ones((head_count,), jnp.float32), jnp.zeros(block_terms.shape[1:], jnp.float32))
    if backward:
        incoming = entering((dev_decay, dev_state), "ctx", compose, identity, True)[1]
    else:
        incoming = entering((dev_decay, dev_state), "ctx", compose, identity, False)[1]

    def resume(state_level, packed):
        decay_step, term_block = packed
        return (decay_step[:, None, None] * state_level + term_block, state_level)

    unused, states = lax.scan(resume, incoming, (block_decay, block_terms))
    if backward:
        states = jnp.flip(states, 0)
    return states


def local(inputs, gate_in, b_proj, c_proj, log_decay, w_out, cotangent):
    tok_rows, feature_width = inputs.shape
    head_count = log_decay.shape[0]
    head_dim = feature_width // head_count
    nblocks = tok_rows // BLOCK
    nstate = b_proj.shape[1]
    x_blocks = inputs.reshape(nblocks, BLOCK, head_count, head_dim)
    b_blocks = b_proj.reshape(nblocks, BLOCK, nstate)
    c_blocks = c_proj.reshape(nblocks, BLOCK, nstate)
    d_blocks = jnp.transpose(log_decay.reshape(head_count, nblocks, BLOCK), (1, 2, 0))
    gate_float = gate_in.astype(jnp.float32).reshape(nblocks, BLOCK, head_count, head_dim)
    sigmoid_z = jax.nn.sigmoid(gate_float)
    silu_z = gate_float * sigmoid_z
    position = jnp.arange(BLOCK)
    causal = position[:, None] >= position[None, :]
    lower_ones = causal.astype(jnp.float32)
    cumulative = jnp.einsum("qs,csh->cqh", lower_ones, d_blocks, precision=lax.Precision.HIGHEST)
    final_sum = cumulative[:, -1, :]
    block_decay = jnp.exp(final_sum)
    tail_weight = jnp.exp(final_sum[:, None, :] - cumulative)
    exp_cum = jnp.exp(cumulative)
    column_cum = jnp.transpose(cumulative, (0, 2, 1))
    differ = column_cum[:, :, :, None] - column_cum[:, :, None, :]
    decay_mat = jnp.where(causal, jnp.exp(jnp.minimum(differ, 0.0)), 0.0)
    scores = jnp.einsum("cqn,ckn->cqk", c_blocks, b_blocks, preferred_element_type=jnp.float32)
    mixing_b = (scores[:, None] * decay_mat).astype(jnp.bfloat16)
    y_intra = jnp.einsum("chqk,ckhp->cqhp", mixing_b, x_blocks, preferred_element_type=jnp.float32)
    weighted = (x_blocks.astype(jnp.float32) * tail_weight[..., None]).astype(jnp.bfloat16)
    block_state = jnp.einsum(
        "cqhp,cqn->chpn", weighted, b_blocks, preferred_element_type=jnp.float32
    )
    state_in = carried(block_decay, block_state, False)
    state_b = state_in.astype(jnp.bfloat16)
    y_inter = (
        jnp.einsum("cqn,chpn->cqhp", c_blocks, state_b, preferred_element_type=jnp.float32)
        * exp_cum[..., None]
    )
    y_full = y_intra + y_inter
    gated_out = (y_full * silu_z).astype(jnp.bfloat16).reshape(tok_rows, feature_width)
    layer_out = lax.psum_scatter(
        jnp.dot(gated_out, w_out, preferred_element_type=jnp.float32).astype(jnp.bfloat16),
        "tp",
        scatter_dimension=0,
        tiled=True,
    )
    state_in, state_b, y_inter, y_full, layer_out = (state_in, state_b, y_inter, y_full, layer_out)
    dgated = lax.dot_general(
        lax.all_gather(cotangent, "tp", axis=0, tiled=True),
        w_out,
        (((1,), (1,)), ((), ())),
        preferred_element_type=jnp.float32,
    )
    dgated = dgated.reshape(nblocks, BLOCK, head_count, head_dim)
    grad_y = dgated * silu_z
    grad_w = (grad_y * exp_cum[..., None]).astype(jnp.bfloat16)
    injected = jnp.einsum("cqhp,cqn->chpn", grad_w, c_blocks, preferred_element_type=jnp.float32)
    adjoint_next = carried(block_decay, injected, True)
    dgated, grad_y, grad_w, adjoint_next = (dgated, grad_y, grad_w, adjoint_next)
    grad_gate = (dgated * y_full * (sigmoid_z + gate_float * sigmoid_z * (1.0 - sigmoid_z))).astype(
        jnp.bfloat16
    )
    grad_gate = grad_gate.reshape(tok_rows, feature_width)
    grad_y_b = grad_y.astype(jnp.bfloat16)
    adjoint_b = adjoint_next.astype(jnp.bfloat16)
    pair_dots = jnp.einsum(
        "cqhp,ckhp->chqk", grad_y_b, x_blocks, preferred_element_type=jnp.float32
    )
    dmix = pair_dots * decay_mat
    dmix_b = dmix.astype(jnp.bfloat16)
    state_dx = (
        jnp.einsum("ckn,chpn->ckhp", b_blocks, adjoint_b, preferred_element_type=jnp.float32)
        * tail_weight[..., None]
    )
    grad_inputs = (
        jnp.einsum("chqk,cqhp->ckhp", mixing_b, grad_y_b, preferred_element_type=jnp.float32)
        + state_dx
    )
    grad_inputs = grad_inputs.astype(jnp.bfloat16).reshape(tok_rows, feature_width)
    b_terms = jnp.einsum("chqk,cqn->ckn", dmix_b, c_blocks, preferred_element_type=jnp.float32)
    b_terms = b_terms + jnp.einsum(
        "ckhp,chpn->ckn", weighted, adjoint_b, preferred_element_type=jnp.float32
    )
    c_terms = jnp.einsum("chqk,ckn->cqn", dmix_b, b_blocks, preferred_element_type=jnp.float32)
    c_terms = c_terms + jnp.einsum(
        "cqhp,chpn->cqn", grad_w, state_b, preferred_element_type=jnp.float32
    )
    grad_b, grad_c = (
        lax.psum_scatter(
            b_terms.reshape(tok_rows, nstate).astype(jnp.bfloat16),
            "tp",
            scatter_dimension=0,
            tiled=True,
        ).astype(jnp.float32),
        lax.psum_scatter(
            c_terms.reshape(tok_rows, nstate).astype(jnp.bfloat16),
            "tp",
            scatter_dimension=0,
            tiled=True,
        ).astype(jnp.float32),
    )
    cross_terms = dmix * scores[:, None]
    decay_flow = jnp.transpose(jnp.sum(cross_terms, 3) - jnp.sum(cross_terms, 2), (0, 2, 1))
    outflow = jnp.sum(x_blocks.astype(jnp.float32) * state_dx, 3)
    decay_flow = decay_flow + jnp.sum(grad_y * y_inter, 3) - outflow
    closing = jnp.sum(outflow, 1) + block_decay * jnp.sum(adjoint_next * state_in, (2, 3))
    decay_flow = decay_flow.at[:, -1, :].add(closing)
    grad_decay = jnp.einsum("ut,cuh->cth", lower_ones, decay_flow, precision=lax.Precision.HIGHEST)
    grad_decay = jnp.transpose(grad_decay, (2, 0, 1)).reshape(head_count, tok_rows)
    return (layer_out, grad_inputs, grad_gate, grad_b, grad_c, grad_decay)


def solution(mesh):
    in_specs = (
        P("ctx", "tp"),
        P("ctx", "tp"),
        P("ctx", None),
        P("ctx", None),
        P("tp", "ctx"),
        P("tp", None),
        P(("ctx", "tp"), None),
    )
    out_specs = (
        P(("ctx", "tp"), None),
        P("ctx", "tp"),
        P("ctx", "tp"),
        P(("ctx", "tp"), None),
        P(("ctx", "tp"), None),
        P("tp", "ctx"),
    )
    return jax.shard_map(local, mesh=mesh, in_specs=in_specs, out_specs=out_specs, check_vma=False)
```

profile of v0, /device:TPU:1, one launch (start us, length us, event | category | flops | bytes accessed | tf_op | source)
XLA Modules:
  0.0 478.6 jit_solution(16107612873647827048)
XLA Ops:
  9.3 1.8 convolution_add_fusion.1
  11.4 33.6 %all-gather.7.cloned.1.call-done = bf16[128,4096]{1,0:T(8,128)(2,1)} async-done(((bf16[16,4096]{1,0:T(8,128)(2,1)}), bf16[128,4096]{1,0:T(8,128)(2,1)}) %all-gather.7.cloned.1.call-update) | async-done | bytes 1048592 | tf_op jit(solution)/shard_map/all_gather | solution.py:112
  45.0 4.0 fusion.39
  50.5 37.2 %all-gather = f32[64,1,4]{2,1,0:T(1,128)S(1)} all-gather(f32[1,1,4]{2,1,0:T(1,128)S(1)} %copy.53), channel_id=2, replica_groups=mesh['ctx'=64,'tp'=8] {'ctx'}, dimensions={0}, use_global_device_ids=true | all-gather | bytes 1040 | tf_op jit(solution)/shard_map/all_gather | solution.py:11
  88.6 98.8 %all-gather.9.cloned.1.call-done = f32[256,128,128]{2,1,0:T(8,128)} async-done(((f32[4,128,128]{2,1,0:T(8,128)}), f32[256,128,128]{2,1,0:T(8,128)}) %all-gather.9.cloned.1.call-update) | async-done | bytes 16777232 | tf_op jit(solution)/shard_map/all_gather | solution.py:11
  187.4 70.2 %while.21 = (s32[]{:T(128)}, f32[4,128,128]{2,1,0:T(8,128)S(1)}, s32[]{:T(128)}, f32[64,4]{1,0:T(8,128)S(1)}, f32[64,4,128,128]{3,2,1,0:T(8,128)}, /*index=5*/s32[]{:T(128)}, s32[]{:T(128)}) while((s32[]{:T(128)}, f32[4,128,128]{2,1,0:T(8,128)S(1)}, s32[]{:T(128)}, f32[64,4]{1,0:T(8,128)S(1)}, f32[64,4,128,128]{3,2,1,0:T(8,128)}, ...), condition=%wide.region_1.2_spmd.clone, body=%wide.region_0.1_spmd.clone.sunk | while | flops 262148 | bytes 786585 | solution.py:24
  202.7 1.1 fusion.59
  203.8 1.1 fusion.59
  213.7 1.1 fusion.59
  216.9 1.1 fusion.59
  218.0 1.1 fusion.59
  221.3 1.1 fusion.59
  223.5 1.1 fusion.59
  226.8 1.1 fusion.59
  244.3 1.1 fusion.59
  245.5 1.1 fusion.59
  253.2 1.1 fusion.59
  255.4 1.1 fusion.59
  256.5 1.1 fusion.59
  259.1 69.5 %all-gather.11.cloned.1.call-done = f32[256,128,128]{2,1,0:T(8,128)} async-done(((f32[4,128,128]{2,1,0:T(8,128)}), f32[256,128,128]{2,1,0:T(8,128)}) %all-gather.11.cloned.1.call-update) | async-done | bytes 16777232 | tf_op jit(solution)/shard_map/all_gather | solution.py:11
  328.6 70.8 %while.22 = (s32[]{:T(128)}, f32[4,128,128]{2,1,0:T(8,128)S(1)}, s32[]{:T(128)}, f32[64,4]{1,0:T(8,128)S(1)}, f32[64,4,128,128]{3,2,1,0:T(8,128)}, /*index=5*/s32[]{:T(128)}, s32[]{:T(128)}, s32[]{:T(128)}, s32[]{:T(128)}) while((s32[]{:T(128)}, f32[4,128,128]{2,1,0:T(8,128)S(1)}, s32[]{:T(128)}, f32[64,4]{1,0:T(8,128)S(1)}, ...), condition=%wide.region_4.5_spmd.clone, body=%wide.region_3.4_spmd.clone.sunk | while | flops 262152 | bytes 786647 | solution.py:24
  329.7 1.1 fusion.60
  336.4 1.1 fusion.60
  341.9 1.1 fusion.60
  343.0 1.1 fusion.60
  344.1 1.1 fusion.60
  346.3 1.1 fusion.60
  347.5 1.1 fusion.60
  348.6 1.1 fusion.60
  349.7 1.1 fusion.60
  351.9 1.1 fusion.60
  353.0 1.1 fusion.60
  354.1 1.1 fusion.60
  355.2 1.1 fusion.60
  357.4 1.1 fusion.60
  359.6 1.1 fusion.60
  360.8 1.1 fusion.60
  363.0 1.1 fusion.60
  366.3 1.1 fusion.60
  374.0 1.1 fusion.60
  381.8 1.1 fusion.60
  387.3 1.1 fusion.60
  395.1 1.1 fusion.60
  400.5 3.9 convolution_convert_fusion
  405.2 1.3 convert_element_type.112
  409.2 23.5 %reduce-scatter.6.cloned.1.call-done = bf16[16,128]{1,0:T(8,128)(2,1)} async-done(((bf16[128,128]{1,0:T(8,128)(2,1)}), bf16[16,128]{1,0:T(8,128)(2,1)}) %reduce-scatter.6.cloned.1.call-update) | async-done | bytes 4112 | tf_op jit(solution)/shard_map/reduce_scatter | solution.py:152
  432.7 1.3 convert_element_type.110
  434.0 37.8 %reduce-scatter.4.cloned.1.call-done = bf16[16,4096]{1,0:T(8,128)(2,1)} async-done(((bf16[128,4096]{1,0:T(8,128)(2,1)}), bf16[16,4096]{1,0:T(8,128)(2,1)}) %reduce-scatter.4.cloned.1.call-update) | async-done | bytes 131088 | tf_op jit(solution)/shard_map/reduce_scatter | solution.py:104
  (280 shorter events, 109.7 us)
Async XLA Ops:
  7.2 2.1 copy-start
  7.2 41.8 %copy-start.2 = (bf16[128,512]{1,0:T(8,128)(2,1)S(1)}, bf16[128,512]{1,0:T(8,128)(2,1)}, u32[]{:S(2)}) copy-start(bf16[128,512]{1,0:T(8,128)(2,1)} %param.14) | copy-start | bytes 393220
  7.2 37.8 %all-gather.7.cloned.1.call-start = ((), (), s32[]{:S(2)}) async-start(), calls=%async_computation.4 | async-start | bytes 1179648 | tf_op jit(solution)/shard_map/all_gather | solution.py:112
  7.9 179.5 %all-gather.9.cloned.1.call-start = ((), (), s32[]{:S(2)}) async-start(), calls=%async_computation.7 | async-start | bytes 17039360 | tf_op jit(solution)/shard_map/all_gather | solution.py:11
  9.1 40.0 %copy-start.3 = (bf16[128,128]{1,0:T(8,128)(2,1)S(1)}, bf16[128,128]{1,0:T(8,128)(2,1)}, u32[]{:S(2)}) copy-start(bf16[128,128]{1,0:T(8,128)(2,1)} %param.16) | copy-start | bytes 98308
  11.1 39.0 %copy-start.1 = (bf16[128,512]{1,0:T(8,128)(2,1)S(1)}, bf16[128,512]{1,0:T(8,128)(2,1)}, u32[]{:S(2)}) copy-start(bf16[128,512]{1,0:T(8,128)(2,1)} %param.13) | copy-start | bytes 393220
  11.2 317.5 %all-gather.11.cloned.1.call-start = ((), (), s32[]{:S(2)}) async-start(), calls=%async_computation.8 | async-start | bytes 17039360 | tf_op jit(solution)/shard_map/all_gather | solution.py:11
  50.1 355.2 %reduce-scatter.8.cloned.1.call-start = ((), (), s32[]{:S(2)}) async-start(), calls=%async_computation.6 | async-start | bytes 36864 | tf_op jit(solution)/shard_map/reduce_scatter | solution.py:158
  258.8 173.9 %reduce-scatter.6.cloned.1.call-start = ((), (), s32[]{:S(2)}) async-start(), calls=%async_computation.5 | async-start | bytes 36864 | tf_op jit(solution)/shard_map/reduce_scatter | solution.py:152
  400.5 71.3 %reduce-scatter.4.cloned.1.call-start = ((), (), s32[]{:S(2)}) async-start(), calls=%async_computation.3 | async-start | bytes 1179648 | tf_op jit(solution)/shard_map/reduce_scatter | solution.py:104
Sparse Core Ops, SparseCore 0:
  10.2 34.7 all-gather.6
  48.0 139.3 all-gather.8
  190.4 138.1 all-gather.10
  331.8 32.0 reduce-scatter.7
  400.6 32.0 reduce-scatter.5
  435.9 35.7 reduce-scatter.3
where the time goes:
time: 484 us; the launch traced here: 479 us
  waiting for transfers between devices  264 us (55%)
  other arithmetic  138 us (29%)
  blocking collectives  37.2 us (8%)
  matrix products  15.8 us (3%)
  between operations  14.3 us (3%)
    all_gather x2, waiting for transfers between devices, entering(): everything = jax.tree.map(lambda part: lax.all_gather(part, axis), shard)  168 us
    select_n x128, other arithmetic, lap(): return jax.tree.map(lambda a, b: jnp.where(reached, a, b), new, before)  135 us
    reduce_scatter x1, waiting for transfers between devices, local(): lax.psum_scatter(jnp.dot(gated_out, w_out, preferred_element_type=jnp.flo...  37.8 us
    all_gather x1, blocking collectives, entering(): everything = jax.tree.map(lambda part: lax.all_gather(part, axis), shard)  37.2 us
    all_gather x1, waiting for transfers between devices, local(): lax.all_gather(cotangent, 'tp', axis=0, tiled=True)  33.6 us
    reduce_scatter x1, waiting for transfers between devices, local(): lax.psum_scatter(b_terms.reshape(tok_rows, nstate).astype(jnp.bfloat16),...  23.5 us
  transfers between devices with their start and end apart: 6, of which 5 were waited for; matrix products, arithmetic and copies ran while one was open for 33% of the time, Pallas kernels for 0%

commit v1 on v0

v1 whole, which is shorter than its diff:
```python
import functools

import jax
import jax.numpy as jnp
from jax import lax
from jax.experimental import pallas as pl
from jax.experimental.pallas import tpu as pltpu
from jax.sharding import PartitionSpec as P

BF = jnp.bfloat16
F32 = jnp.float32
NT = (((1,), (1,)), ((), ()))
VMEM_LIMIT = 48 * 1024 * 1024


def mm(a, b):
    return jnp.dot(a, b, preferred_element_type=F32)


def mm_nt(a, b):
    return lax.dot_general(a, b, NT, preferred_element_type=F32)


def flip(a):
    return jnp.transpose(a.astype(F32)).astype(BF)


def split(a):
    hi = a.astype(BF)
    rest = a - hi.astype(F32)
    mid = rest.astype(BF)
    return hi, mid, (rest - mid.astype(F32)).astype(BF)


def sum_by(a, ones):
    hi, mid, lo = split(a)
    return mm(hi, ones) + (mm(mid, ones) + mm(lo, ones))


def grid_of(size):
    return (
        lax.broadcasted_iota(jnp.int32, (size, size), 0),
        lax.broadcasted_iota(jnp.int32, (size, size), 1),
    )


def pre_kernel(heads, x_ref, gate_ref, b_ref, c_ref, ld_ref,
               st_ref, dec_ref, mask_ref, mixt_ref, scores_ref, yi_ref, ec_ref, tail_ref,
               wx_ref, silu_ref, slope_ref):
    size = x_ref.shape[0]
    width = x_ref.shape[1] // heads
    row, col = grid_of(size)
    ld = jnp.concatenate([ld_ref[...], jnp.zeros((8 - heads, size), F32)], axis=0)
    cum = sum_by(ld, (row <= col).astype(BF))
    scores = mm_nt(c_ref[...], b_ref[...])
    scores_ref[...] = scores
    b_t = flip(b_ref[...])
    for h in range(heads):
        at = slice(h * width, (h + 1) * width)
        across = jnp.broadcast_to(cum[h:h + 1, :], (size, size))
        down = jnp.transpose(across)
        mask = jnp.where(row >= col, jnp.exp(jnp.minimum(down - across, 0.0)), 0.0)
        mask_ref[h] = mask
        mixing = scores * mask
        mixt_ref[h] = jnp.transpose(mixing).astype(BF)
        x = x_ref[:, at]
        yi_ref[:, at] = mm(mixing.astype(BF), x)
        last = cum[h:h + 1, size - 1:size]
        ec_ref[:, at] = jnp.exp(down)
        tail = jnp.exp(last - down)
        tail_ref[:, at] = tail
        wx = (x.astype(F32) * tail).astype(BF)
        wx_ref[:, at] = wx
        st_ref[:, at] = mm(b_t, wx)
        decay = jnp.broadcast_to(jnp.exp(last), (8, size))
        hi = decay.astype(BF).astype(F32)
        lo = decay - hi
        dec_ref[h] = jnp.where(lax.broadcasted_iota(jnp.int32, (8, size), 0) < 4, hi, lo)
    v = gate_ref[...].astype(F32)
    g = 1.0 / (1.0 + jnp.exp(-v))
    silu_ref[...] = v * g
    slope_ref[...] = g + v * g * (1.0 - g)


def mid_kernel(heads, piece, near_ref, far_ref, w_ref, c_ref, silu_ref, ec_ref, st_ref, dec_ref,
               msg_ref, dg_ref):
    size = st_ref.shape[0]
    width = st_ref.shape[1] // heads
    me = lax.axis_index("tp")
    core = me % 2
    chip = me // 2
    w = w_ref[...]
    near = mm_nt(near_ref[...], w)
    far = mm_nt(far_ref[...], w)
    chips = near_ref.shape[0] // piece
    for s in range(chips):
        rows = slice(s * piece, (s + 1) * piece)
        src = 2 * ((chip + chips - s) % chips)
        dg_ref[pl.ds(pl.multiple_of(piece * (src + core), piece), piece), :] = near[rows, :]
        dg_ref[pl.ds(pl.multiple_of(piece * (src + 1 - core), piece), piece), :] = far[rows, :]
    gw = (dg_ref[...] * silu_ref[...] * ec_ref[...]).astype(BF)
    inj = mm(flip(c_ref[...]), gw)
    for a in range(size // 8):
        for h in range(heads):
            j = a * heads + h
            at = slice(h * width, (h + 1) * width)
            both = jnp.concatenate([st_ref[8 * a:8 * a + 8, at], inj[8 * a:8 * a + 8, at]], axis=0)
            msg_ref[j, 0:16, :] = both.astype(BF)
            msg_ref[j, 16:24, :] = dec_ref[h].astype(BF)


def scan_kernel(msg_ref, out_ref, dec_ref, state_ref):
    count = msg_ref.shape[0]
    state = jnp.zeros((8, msg_ref.shape[2]), F32)
    for k in range(count):
        pair = msg_ref[k, 16:24, :].astype(F32)
        decay = pair + pltpu.roll(pair, 4, 0)
        dec_ref[k] = decay
        state_ref[k] = state
        state = decay * state + msg_ref[k, 0:8, :].astype(F32)
    adjoint = jnp.zeros((8, msg_ref.shape[2]), F32)
    for k in reversed(range(count)):
        out_ref[k] = jnp.concatenate([state_ref[k], adjoint], axis=0).astype(BF)
        adjoint = dec_ref[k] * adjoint + msg_ref[k, 8:16, :].astype(F32)


def fin_kernel(heads, back_ref, x_ref, b_ref, c_ref, w_ref, dg_ref, silu_ref, slope_ref, mask_ref,
               mixt_ref, scores_ref, yi_ref, ec_ref, tail_ref, wx_ref, dec_ref,
               part_ref, gi_ref, gg_ref, gd_ref, state_ref, adj_ref):
    size, full = x_ref.shape
    width = full // heads
    for a in range(size // 8):
        for h in range(heads):
            both = back_ref[a * heads + h].astype(F32)
            state_ref[8 * a:8 * a + 8, h * width:(h + 1) * width] = both[0:8]
            adj_ref[8 * a:8 * a + 8, h * width:(h + 1) * width] = both[8:16]
    state = state_ref[...]
    adj = adj_ref[...]
    state_b = state.astype(BF)
    adj_b = adj.astype(BF)
    x = x_ref[...]
    b = b_ref[...]
    c = c_ref[...]
    silu = silu_ref[...]
    dg = dg_ref[...]
    ec = ec_ref[...]
    y_inter = mm(c, state_b) * ec
    y = yi_ref[...] + y_inter
    gated = (y * silu).astype(BF)
    out_width = w_ref.shape[1]
    step = 512
    for o in range(0, out_width, step):
        part_ref[:, o:o + step] = mm(gated, w_ref[:, o:o + step]).astype(BF)
    gg_ref[...] = (dg * y * slope_ref[...]).astype(BF)
    gy = dg * silu
    gy_b = gy.astype(BF)
    gw = (gy * ec).astype(BF)
    sdx = mm(b, adj_b) * tail_ref[...]
    through = x.astype(F32) * sdx
    entering = gy * y_inter
    scores = scores_ref[...]
    row, col = grid_of(size)
    sub = lax.broadcasted_iota(jnp.int32, (8, size), 0)
    dmix_sum = jnp.zeros((size, size), F32)
    columns = jnp.zeros((size, size), F32)
    lines = jnp.zeros((8, size), F32)
    closing = jnp.zeros((8, size), F32)
    product = adj * state
    for h in range(heads):
        at = slice(h * width, (h + 1) * width)
        dmix = mm_nt(gy_b[:, at], x[:, at]) * mask_ref[h]
        dmix_sum = dmix_sum + dmix
        cross = dmix * scores
        gi_ref[:, at] = (mm(mixt_ref[h], gy_b[:, at]) + sdx[:, at]).astype(BF)
        down = jnp.sum(cross + entering[:, at] - through[:, at], axis=1, keepdims=True)
        columns = jnp.where(col == h, down, columns)
        lines = jnp.where(sub == h, jnp.sum(cross, axis=0, keepdims=True), lines)
        decay = jnp.max(dec_ref[h][0:1, 0:1] + dec_ref[h][4:5, 0:1], axis=1, keepdims=True)
        end = jnp.sum(jnp.sum(through[:, at], axis=0, keepdims=True), axis=1, keepdims=True)
        dots = jnp.sum(jnp.sum(product[:, at], axis=0, keepdims=True), axis=1, keepdims=True)
        closing = jnp.where(sub == h, end + decay * dots, closing)
    flow = jnp.transpose(columns)[0:8, :] - lines
    total = sum_by(flow, (row >= col).astype(BF)) + closing
    gd_ref[...] = total[0:heads, :]
    dmix_b = dmix_sum.astype(BF)
    n = b.shape[1]
    part_ref[:, out_width:out_width + n] = (
        mm(jnp.transpose(dmix_sum).astype(BF), c) + mm_nt(wx_ref[...], adj_b)
    ).astype(BF)
    part_ref[:, out_width + n:out_width + 2 * n] = (mm(dmix_b, b) + mm_nt(gw, state_b)).astype(BF)


def call(kernel, outs, scratch=()):
    return pl.pallas_call(
        kernel,
        out_shape=tuple(jax.ShapeDtypeStruct(s, d) for s, d in outs),
        scratch_shapes=list(scratch),
        compiler_params=pltpu.CompilerParams(vmem_limit_bytes=VMEM_LIMIT),
    )


def local(inputs, gate_in, b_proj, c_proj, log_decay, w_out, cotangent):
    size, full = inputs.shape
    heads = log_decay.shape[0]
    n = b_proj.shape[1]
    tp = lax.axis_size("tp")
    chips = tp // 2
    workers = lax.axis_size("ctx")
    piece, out_width = cotangent.shape

    def turn(s):
        return [(2 * i + k, 2 * ((i + s) % chips) + k) for i in range(chips) for k in range(2)]

    pieces = [cotangent] + [lax.ppermute(cotangent, "tp", turn(s)) for s in range(1, chips)]
    near = jnp.concatenate(pieces, axis=0)
    far = lax.ppermute(near, "tp", [(i, i ^ 1) for i in range(tp)])

    wide = ((size, full), F32)
    square = (heads, size, size)
    st, dec, mask, mixt, scores, yi, ec, tail, wx, silu, slope = call(
        functools.partial(pre_kernel, heads),
        [((n, full), F32), ((heads, 8, size), F32), (square, F32), (square, BF), ((size, size), F32),
         wide, wide, wide, ((size, full), BF), wide, wide],
    )(inputs, gate_in, b_proj, c_proj, log_decay)
    msg, dg = call(
        functools.partial(mid_kernel, heads, piece),
        [((workers, 24, size), BF), wide],
    )(near, far, w_out, c_proj, silu, ec, st, dec)
    msg = lax.all_to_all(msg, "ctx", 0, 0, tiled=True)
    (back,) = call(
        scan_kernel,
        [((workers, 16, size), BF)],
        [pltpu.VMEM((workers, 8, size), F32), pltpu.VMEM((workers, 8, size), F32)],
    )(msg)
    back = lax.all_to_all(back, "ctx", 0, 0, tiled=True)
    part, grad_inputs, grad_gate, grad_decay = call(
        functools.partial(fin_kernel, heads),
        [((size, out_width + 2 * n), BF), ((size, full), BF), ((size, full), BF), ((heads, size), F32)],
        [pltpu.VMEM((n, full), F32), pltpu.VMEM((n, full), F32)],
    )(back, inputs, b_proj, c_proj, w_out, dg, silu, slope, mask, mixt, scores, yi, ec, tail, wx, dec)
    part = lax.all_to_all(part.reshape(tp, size // tp, out_width + 2 * n), "tp", 0, 0, tiled=True)
    total = jnp.sum(part.astype(F32), axis=0)
    layer_out = total[:, :out_width].astype(BF)
    grad_b = total[:, out_width:out_width + n]
    grad_c = total[:, out_width + n:]
    return (layer_out, grad_inputs, grad_gate, grad_b, grad_c, grad_decay)


def solution(mesh):
    in_specs = (
        P("ctx", "tp"),
        P("ctx", "tp"),
        P("ctx", None),
        P("ctx", None),
        P("tp", "ctx"),
        P("tp", None),
        P(("ctx", "tp"), None),
    )
    out_specs = (
        P(("ctx", "tp"), None),
        P("ctx", "tp"),
        P("ctx", "tp"),
        P(("ctx", "tp"), None),
        P(("ctx", "tp"), None),
        P("tp", "ctx"),
    )
    return jax.shard_map(local, mesh=mesh, in_specs=in_specs, out_specs=out_specs, check_vma=False)
```

time: 484 us -> 108 us (0.22)
  waiting for transfers between devices: 264 us -> 1.26 us
  other arithmetic: 138 us -> 0.14 us
  blocking collectives: 37.2 us -> 71.3 us
  starting transfers between devices: 0.24 us -> 19 us
  matrix products: 15.8 us -> 0 us
  between operations: 14.3 us -> 0.8 us
  Pallas kernels: 0 us -> 10 us
    all_gather x3 -> x0, waiting for transfers between devices: 202 us -> none  [the longest x2 168 us: entering(): everything = jax.tree.map(lambda part: lax.all_gather(part, axis), shard)]
    select_n x128 -> x0, other arithmetic: 135 us -> none  [lap(): return jax.tree.map(lambda a, b: jnp.where(reached, a, b), new, before)]
    all_to_all x0 -> x3, blocking collectives: none -> 71.3 us  [the longest x1 28.6 us: local(): msg = lax.all_to_all(msg, 'ctx', 0, 0, tiled=True)]
    reduce_scatter x3 -> x0, waiting for transfers between devices: 61.3 us -> none  [the longest x1 37.8 us: local(): lax.psum_scatter(jnp.dot(gated_out, w_out, preferred_element_type=jnp.flo...]
    all_gather x1 -> x0, blocking collectives: 37.2 us -> none  [entering(): everything = jax.tree.map(lambda part: lax.all_gather(part, axis), shard)]
    ppermute x0 -> x4, starting transfers between devices: none -> 19 us  [the longest x3 12.1 us: local(): lax.ppermute(cotangent, 'tp', turn(s))]
    dot_general x16 -> x0, matrix products: 15.8 us -> none  [the longest x1 4.04 us: local(): lax.dot_general(lax.all_gather(cotangent, 'tp', axis=0, tiled=True), w_ou...]
    pallas_call x0 -> x4, Pallas kernels: none -> 10 us  [the longest x1 5.03 us: local(): call(functools.partial(mid_kernel, heads, piece), [((workers, 24, size),...]
  transfers between devices with their start and end apart: 6 -> 4, of which waited for: 5 -> 1; matrix products, arithmetic and copies ran while one was open for 33% -> 1% of each run, Pallas kernels for 0% -> 1%
where the time goes in v1:
time: 108 us; the launch traced here: 107 us
  blocking collectives  71.3 us (66%)
  starting transfers between devices  19 us (18%)
  Pallas kernels  10 us (9%)
  local copies, waits for them, and re-layouts  4.45 us (4%)
  waiting for transfers between devices  1.26 us (1%)
    all_to_all x1, blocking collectives, local(): msg = lax.all_to_all(msg, 'ctx', 0, 0, tiled=True)  28.6 us
    all_to_all x1, blocking collectives, local(): lax.all_to_all(part.reshape(tp, size // tp, out_width + 2 * n), 'tp', 0,...  24.2 us
    all_to_all x1, blocking collectives, local(): back = lax.all_to_all(back, 'ctx', 0, 0, tiled=True)  18.5 us
    ppermute x3, starting transfers between devices, local(): lax.ppermute(cotangent, 'tp', turn(s))  12.1 us
    ppermute x1, starting transfers between devices, local(): far = lax.ppermute(near, 'tp', [(i, i ^ 1) for i in range(tp)])  6.93 us
    pallas_call x1, Pallas kernels, local(): call(functools.partial(mid_kernel, heads, piece), [((workers, 24, size),...  5.03 us
    pallas_call x1, Pallas kernels, local(): call(functools.partial(fin_kernel, heads), [((size, out_width + 2 * n), B...  4.2 us
    unnamed x17, local copies, waits for them, and re-layouts  3.16 us
  transfers between devices with their start and end apart: 4, of which 1 were waited for; matrix products, arithmetic and copies ran while one was open for 1% of the time, Pallas kernels for 1%

profile of v1, /device:TPU:1, one launch (start us, length us, event | category | flops | bytes accessed | tf_op | source)
XLA Modules:
  0.0 107.0 jit_solution(16715975469981409521)
XLA Ops:
  0.6 0.0 copy-start.2
  0.6 0.0 copy-start
  0.7 0.0 copy-start.3
  0.7 5.6 %collective-permute-start.1 = (bf16[16,4096]{1,0:T(8,128)(2,1)}, bf16[16,4096]{1,0:T(8,128)(2,1)S(1)}, u32[]{:S(2)}, u32[]{:S(2)}) collective-permute-start(bf16[16,4096]{1,0:T(8,128)(2,1)} %param.13), channel_id=1, source_target_pairs={{0,4},{1,5},{2,6},{3,7},{4,0},{5,1},{6,2},{7,3},{8,12},{9,13},{10,... | collective-permute-start | bytes 393224 | tf_op jit(solution)/shard_map/ppermute | solution.py:214
  6.3 2.2 %collective-permute-start = (bf16[16,4096]{1,0:T(8,128)(2,1)}, bf16[16,4096]{1,0:T(8,128)(2,1)S(1)}, u32[]{:S(2)}, u32[]{:S(2)}) collective-permute-start(bf16[16,4096]{1,0:T(8,128)(2,1)} %param.13), channel_id=1, source_target_pairs={{0,2},{1,3},{2,4},{3,5},{4,6},{5,7},{6,0},{7,1},{8,10},{9,11},{10,... | collective-permute-start | bytes 393224 | tf_op jit(solution)/shard_map/ppermute | solution.py:214
  8.5 4.3 %collective-permute-start.2 = (bf16[16,4096]{1,0:T(8,128)(2,1)}, bf16[16,4096]{1,0:T(8,128)(2,1)S(1)}, u32[]{:S(2)}, u32[]{:S(2)}) collective-permute-start(bf16[16,4096]{1,0:T(8,128)(2,1)} %param.13), channel_id=1, source_target_pairs={{0,6},{1,7},{2,0},{3,1},{4,2},{5,3},{6,4},{7,5},{8,14},{9,15},{10,... | collective-permute-start | bytes 393224 | tf_op jit(solution)/shard_map/ppermute | solution.py:214
  12.8 0.9 constant_dynamic-update-slice_fusion.3
  13.7 0.0 collective-permute-done
  13.7 0.0 collective-permute-done.1
  13.8 1.3 %collective-permute-done.2 = bf16[16,4096]{1,0:T(8,128)(2,1)S(1)} collective-permute-done((bf16[16,4096]{1,0:T(8,128)(2,1)}, bf16[16,4096]{1,0:T(8,128)(2,1)S(1)}, u32[]{:S(2)}, u32[]{:S(2)}) %collective-permute-start.2) | collective-permute-done | bytes 131104 | tf_op jit(solution)/shard_map/ppermute | solution.py:214
  15.0 6.9 %collective-permute-start.3 = (bf16[64,4096]{1,0:T(8,128)(2,1)S(1)}, bf16[64,4096]{1,0:T(8,128)(2,1)S(1)}, u32[]{:S(2)}, u32[]{:S(2)}) collective-permute-start(bf16[64,4096]{1,0:T(8,128)(2,1)S(1)} %constant_dynamic-update-slice_fusion.near_ref), channel_id=1, source_target_pairs={{0,1},{1,0},{2,3},{3,2},{4,5},{5,4},{6,7},{7,6},{8,9},{9,8},{10,11... | collective-permute-start | bytes 1572872 | tf_op jit(solution)/shard_map/ppermute | solution.py:216
  22.0 0.0 copy-done
  22.0 0.0 copy-done.3
  22.0 0.0 copy-start.1
  22.0 0.7 copy-done.1
  22.8 0.0 copy-start.4
  22.8 0.8 copy-done.4
  23.5 0.0 copy-start.6
  23.5 0.7 copy-done.6
  24.2 0.6 shard_map.118
  24.8 0.0 collective-permute-done.3.far_ref
  24.8 0.0 copy-done.2
  24.9 5.0 %shard_map.119 = (bf16[64,24,128]{2,1,0:T(8,128)(2,1)S(1)}, f32[128,512]{1,0:T(8,128)S(1)}) custom-call(bf16[64,4096]{1,0:T(8,128)(2,1)S(1)} %constant_dynamic-update-slice_fusion.near_ref, bf16[64,4096]{1,0:T(8,128)(2,1)S(1)} %collective-permute-done.3.far_ref, bf16[512,4096]{1,0:T(8,128)(2,1)} %w_ref.3, bf16[128,128]{1,0:T(8,128)(2,1)S(1)} %copy-done.2, ...), custom_call_target="tpu_custom_call" | custom-call | tf_op jit(solution)/shard_map/pallas_call | solution.py:225
  29.9 0.0 copy-start.5
  29.9 28.6 %all_to_all.15.msg_ref = bf16[64,24,128]{2,1,0:T(8,128)(2,1)S(1)} all-to-all(bf16[64,24,128]{2,1,0:T(8,128)(2,1)S(1)} %get-tuple-element.27), channel_id=1, replica_groups=mesh['ctx'=64,'tp'=8] {'ctx'}, dimensions={0} | all-to-all | bytes 786432 | tf_op jit(solution)/shard_map/all_to_all | solution.py:229
  58.5 0.2 shard_map.120
  58.7 18.5 %all_to_all.16.back_ref = bf16[64,16,128]{2,1,0:T(8,128)(2,1)S(1)} all-to-all(bf16[64,16,128]{2,1,0:T(8,128)(2,1)S(1)} %shard_map.120), channel_id=1, replica_groups=mesh['ctx'=64,'tp'=8] {'ctx'}, dimensions={0} | all-to-all | bytes 524288 | tf_op jit(solution)/shard_map/all_to_all | solution.py:235
  77.1 0.0 copy-done.5
  77.1 4.2 %shard_map.121 = (bf16[128,4352]{1,0:T(8,128)(2,1)S(1)}, bf16[128,512]{1,0:T(8,128)(2,1)}, bf16[128,512]{1,0:T(8,128)(2,1)}, f32[4,128]{1,0:T(4,128)}) custom-call(bf16[64,16,128]{2,1,0:T(8,128)(2,1)S(1)} %all_to_all.16.back_ref, bf16[128,512]{1,0:T(8,128)(2,1)S(1)} %copy-done, bf16[128,128]{1,0:T(8,128)(2,1)S(1)} %copy-done.5, ...), custom_call_target="tpu_custom_call" | custom-call | tf_op jit(solution)/shard_map/pallas_call | solution.py:236
  81.3 24.2 %all_to_all.17 = bf16[8,16,4352]{2,1,0:T(8,128)(2,1)S(1)} all-to-all(bf16[8,16,4352]{2,1,0:T(8,128)(2,1)S(1)} %bitcast.1), channel_id=1, replica_groups=mesh['ctx'=64,'tp'=8] {'tp'}, dimensions={0} | all-to-all | bytes 2228224 | tf_op jit(solution)/shard_map/all_to_all | solution.py:241
  105.6 0.1 convert_reduce_fusion
  105.7 0.6 fusion
  106.3 0.7 slice.17
  (3 shorter events, 0.0 us)
Async XLA Ops:
  0.6 24.2 %copy-start.2 = (bf16[128,128]{1,0:T(8,128)(2,1)S(1)}, bf16[128,128]{1,0:T(8,128)(2,1)}, u32[]{:S(2)}) copy-start(bf16[128,128]{1,0:T(8,128)(2,1)} %c_ref.5) | copy-start | bytes 98308
  0.6 21.3 %copy-start = (bf16[128,512]{1,0:T(8,128)(2,1)S(1)}, bf16[128,512]{1,0:T(8,128)(2,1)}, u32[]{:S(2)}) copy-start(bf16[128,512]{1,0:T(8,128)(2,1)} %x_ref.3) | copy-start | bytes 393220
  0.7 21.3 %copy-start.3 = (bf16[128,512]{1,0:T(8,128)(2,1)S(1)}, bf16[128,512]{1,0:T(8,128)(2,1)}, u32[]{:S(2)}) copy-start(bf16[128,512]{1,0:T(8,128)(2,1)} %gate_ref.1) | copy-start | bytes 393220
  0.7 13.1 %collective-permute-start.1 = (bf16[16,4096]{1,0:T(8,128)(2,1)}, bf16[16,4096]{1,0:T(8,128)(2,1)S(1)}, u32[]{:S(2)}, u32[]{:S(2)}) collective-permute-start(bf16[16,4096]{1,0:T(8,128)(2,1)} %param.13), channel_id=1, source_target_pairs={{0,4},{1,5},{2,6},{3,7},{4,0},{5,1},{6,2},{7,3},{8,12},{9,13},{10,... | collective-permute-start | bytes 393224 | tf_op jit(solution)/shard_map/ppermute | solution.py:214
  6.3 7.4 %collective-permute-start = (bf16[16,4096]{1,0:T(8,128)(2,1)}, bf16[16,4096]{1,0:T(8,128)(2,1)S(1)}, u32[]{:S(2)}, u32[]{:S(2)}) collective-permute-start(bf16[16,4096]{1,0:T(8,128)(2,1)} %param.13), channel_id=1, source_target_pairs={{0,2},{1,3},{2,4},{3,5},{4,6},{5,7},{6,0},{7,1},{8,10},{9,11},{10,... | collective-permute-start | bytes 393224 | tf_op jit(solution)/shard_map/ppermute | solution.py:214
  8.5 6.5 %collective-permute-start.2 = (bf16[16,4096]{1,0:T(8,128)(2,1)}, bf16[16,4096]{1,0:T(8,128)(2,1)S(1)}, u32[]{:S(2)}, u32[]{:S(2)}) collective-permute-start(bf16[16,4096]{1,0:T(8,128)(2,1)} %param.13), channel_id=1, source_target_pairs={{0,6},{1,7},{2,0},{3,1},{4,2},{5,3},{6,4},{7,5},{8,14},{9,15},{10,... | collective-permute-start | bytes 393224 | tf_op jit(solution)/shard_map/ppermute | solution.py:214
  15.0 9.8 %collective-permute-start.3 = (bf16[64,4096]{1,0:T(8,128)(2,1)S(1)}, bf16[64,4096]{1,0:T(8,128)(2,1)S(1)}, u32[]{:S(2)}, u32[]{:S(2)}) collective-permute-start(bf16[64,4096]{1,0:T(8,128)(2,1)S(1)} %constant_dynamic-update-slice_fusion.near_ref), channel_id=1, source_target_pairs={{0,1},{1,0},{2,3},{3,2},{4,5},{5,4},{6,7},{7,6},{8,9},{9,8},{10,11... | collective-permute-start | bytes 1572872 | tf_op jit(solution)/shard_map/ppermute | solution.py:216
  22.0 0.8 copy-start.1
  22.8 0.8 copy-start.4
  23.5 0.7 copy-start.6
  29.9 47.2 %copy-start.5 = (bf16[128,128]{1,0:T(8,128)(2,1)S(1)}, bf16[128,128]{1,0:T(8,128)(2,1)}, u32[]{:S(2)}) copy-start(bf16[128,128]{1,0:T(8,128)(2,1)} %b_ref.3) | copy-start | bytes 98308

commit v2 on v1

--- a/solution.py
+++ b/solution.py
@@ -44,17 +44,31 @@
     )
 
 
-def pre_kernel(heads, x_ref, gate_ref, b_ref, c_ref, ld_ref,
+def fetch(pairs, sems):
+    copies = [pltpu.make_async_copy(src, dst, sems.at[i]) for i, (src, dst) in enumerate(pairs)]
+    for copy in copies:
+        copy.start()
+    return copies
+
+
+def pre_kernel(heads, x_hbm, gate_hbm, b_hbm, c_hbm, ld_hbm,
                st_ref, dec_ref, mask_ref, mixt_ref, scores_ref, yi_ref, ec_ref, tail_ref,
-               wx_ref, silu_ref, slope_ref):
+               wx_ref, silu_ref, slope_ref, x_ref, b_ref, c_ref, gate_ref, ld_ref, sems):
+    copies = fetch(
+        ((ld_hbm, ld_ref), (b_hbm, b_ref), (c_hbm, c_ref), (x_hbm, x_ref), (gate_hbm, gate_ref)), sems
+    )
     size = x_ref.shape[0]
     width = x_ref.shape[1] // heads
     row, col = grid_of(size)
+    copies[0].wait()
     ld = jnp.concatenate([ld_ref[...], jnp.zeros((8 - heads, size), F32)], axis=0)
     cum = sum_by(ld, (row <= col).astype(BF))
+    copies[1].wait()
+    copies[2].wait()
     scores = mm_nt(c_ref[...], b_ref[...])
     scores_ref[...] = scores
     b_t = flip(b_ref[...])
+    copies[3].wait()
     for h in range(heads):
         at = slice(h * width, (h + 1) * width)
         across = jnp.broadcast_to(cum[h:h + 1, :], (size, size))
@@ -76,37 +90,43 @@
         hi = decay.astype(BF).astype(F32)
         lo = decay - hi
         dec_ref[h] = jnp.where(lax.broadcasted_iota(jnp.int32, (8, size), 0) < 4, hi, lo)
+    copies[4].wait()
     v = gate_ref[...].astype(F32)
     g = 1.0 / (1.0 + jnp.exp(-v))
     silu_ref[...] = v * g
     slope_ref[...] = g + v * g * (1.0 - g)
 
 
-def mid_kernel(heads, piece, near_ref, far_ref, w_ref, c_ref, silu_ref, ec_ref, st_ref, dec_ref,
-               msg_ref, dg_ref):
-    size = st_ref.shape[0]
-    width = st_ref.shape[1] // heads
-    me = lax.axis_index("tp")
-    core = me % 2
-    chip = me // 2
-    w = w_ref[...]
-    near = mm_nt(near_ref[...], w)
-    far = mm_nt(far_ref[...], w)
-    chips = near_ref.shape[0] // piece
+def mid_kernel(heads, near_ref, far_ref, w_hbm, c_hbm, silu_ref, ec_ref, st_ref, dec_ref,
+               msg_ref, dg_ref, w_ref, cot_ref, c_ref, sems):
+    chips, piece = near_ref.shape[:2]
+    size, full = st_ref.shape
+    width = full // heads
+    copies = fetch(
+        [(w_hbm.at[pl.ds(h * width, width), :], w_ref.at[pl.ds(h * width, width), :])
+         for h in range(heads)] + [(c_hbm, c_ref)], sems
+    )
+    core = lax.axis_index("tp") % 2
     for s in range(chips):
-        rows = slice(s * piece, (s + 1) * piece)
-        src = 2 * ((chip + chips - s) % chips)
-        dg_ref[pl.ds(pl.multiple_of(piece * (src + core), piece), piece), :] = near[rows, :]
-        dg_ref[pl.ds(pl.multiple_of(piece * (src + 1 - core), piece), piece), :] = far[rows, :]
-    gw = (dg_ref[...] * silu_ref[...] * ec_ref[...]).astype(BF)
-    inj = mm(flip(c_ref[...]), gw)
-    for a in range(size // 8):
-        for h in range(heads):
+        at = pl.multiple_of(piece * (2 * s + core), piece)
+        cot_ref[pl.ds(at, piece), :] = near_ref[s]
+        at = pl.multiple_of(piece * (2 * s + 1 - core), piece)
+        cot_ref[pl.ds(at, piece), :] = far_ref[s]
+    copies[heads].wait()
+    c_t = flip(c_ref[...])
+    for h in range(heads):
+        at = slice(h * width, (h + 1) * width)
+        copies[h].wait()
+        dg = mm_nt(cot_ref[...], w_ref[at, :])
+        dg_ref[:, at] = dg
+        gw = (dg * silu_ref[:, at] * ec_ref[:, at]).astype(BF)
+        inj = mm(c_t, gw)
+        pair = dec_ref[h].astype(BF)
+        for a in range(size // 8):
             j = a * heads + h
-            at = slice(h * width, (h + 1) * width)
-            both = jnp.concatenate([st_ref[8 * a:8 * a + 8, at], inj[8 * a:8 * a + 8, at]], axis=0)
+            both = jnp.concatenate([st_ref[8 * a:8 * a + 8, at], inj[8 * a:8 * a + 8, :]], axis=0)
             msg_ref[j, 0:16, :] = both.astype(BF)
-            msg_ref[j, 16:24, :] = dec_ref[h].astype(BF)
+            msg_ref[j, 16:24, :] = pair
 
 
 def scan_kernel(msg_ref, out_ref, dec_ref, state_ref):
@@ -124,11 +144,17 @@
         adjoint = dec_ref[k] * adjoint + msg_ref[k, 8:16, :].astype(F32)
 
 
-def fin_kernel(heads, back_ref, x_ref, b_ref, c_ref, w_ref, dg_ref, silu_ref, slope_ref, mask_ref,
+def fin_kernel(heads, piece, back_ref, x_hbm, b_hbm, c_hbm, w_hbm, dg_ref, silu_ref, slope_ref, mask_ref,
                mixt_ref, scores_ref, yi_ref, ec_ref, tail_ref, wx_ref, dec_ref,
-               part_ref, gi_ref, gg_ref, gd_ref, state_ref, adj_ref):
+               mine_ref, theirs_ref, gi_ref, gg_ref, gd_ref,
+               state_ref, adj_ref, gated_ref, terms_ref, x_ref, b_ref, c_ref, w_ref, sems):
     size, full = x_ref.shape
     width = full // heads
+    copies = fetch(
+        [(b_hbm, b_ref), (c_hbm, c_ref), (x_hbm, x_ref)]
+        + [(w_hbm.at[pl.ds(h * width, width), :], w_ref.at[pl.ds(h * width, width), :])
+           for h in range(heads)], sems
+    )
     for a in range(size // 8):
         for h in range(heads):
             both = back_ref[a * heads + h].astype(F32)
@@ -138,7 +164,8 @@
     adj = adj_ref[...]
     state_b = state.astype(BF)
     adj_b = adj.astype(BF)
-    x = x_ref[...]
+    copies[0].wait()
+    copies[1].wait()
     b = b_ref[...]
     c = c_ref[...]
     silu = silu_ref[...]
@@ -147,15 +174,22 @@
     y_inter = mm(c, state_b) * ec
     y = yi_ref[...] + y_inter
     gated = (y * silu).astype(BF)
-    out_width = w_ref.shape[1]
-    step = 512
-    for o in range(0, out_width, step):
-        part_ref[:, o:o + step] = mm(gated, w_ref[:, o:o + step]).astype(BF)
+    core = lax.axis_index("tp") % 2
+    places = []
+    for i in range(size // piece // 2):
+        for k in range(2):
+            away = jnp.where(core == k, 0, 1)
+            places.append((slice(piece * (2 * i + k), piece * (2 * i + k + 1)),
+                           pl.ds(pl.multiple_of(size // 2 * (1 - away) + piece * i, piece), piece)))
+    for src, dst in places:
+        gated_ref[dst, :] = gated[src, :]
     gg_ref[...] = (dg * y * slope_ref[...]).astype(BF)
     gy = dg * silu
     gy_b = gy.astype(BF)
     gw = (gy * ec).astype(BF)
     sdx = mm(b, adj_b) * tail_ref[...]
+    copies[2].wait()
+    x = x_ref[...]
     through = x.astype(F32) * sdx
     entering = gy * y_inter
     scores = scores_ref[...]
@@ -175,25 +209,52 @@
         down = jnp.sum(cross + entering[:, at] - through[:, at], axis=1, keepdims=True)
         columns = jnp.where(col == h, down, columns)
         lines = jnp.where(sub == h, jnp.sum(cross, axis=0, keepdims=True), lines)
-        decay = jnp.max(dec_ref[h][0:1, 0:1] + dec_ref[h][4:5, 0:1], axis=1, keepdims=True)
+        decay = dec_ref[h] + pltpu.roll(dec_ref[h], 4, 0)
         end = jnp.sum(jnp.sum(through[:, at], axis=0, keepdims=True), axis=1, keepdims=True)
         dots = jnp.sum(jnp.sum(product[:, at], axis=0, keepdims=True), axis=1, keepdims=True)
         closing = jnp.where(sub == h, end + decay * dots, closing)
     flow = jnp.transpose(columns)[0:8, :] - lines
     total = sum_by(flow, (row >= col).astype(BF)) + closing
     gd_ref[...] = total[0:heads, :]
-    dmix_b = dmix_sum.astype(BF)
     n = b.shape[1]
-    part_ref[:, out_width:out_width + n] = (
-        mm(jnp.transpose(dmix_sum).astype(BF), c) + mm_nt(wx_ref[...], adj_b)
-    ).astype(BF)
-    part_ref[:, out_width + n:out_width + 2 * n] = (mm(dmix_b, b) + mm_nt(gw, state_b)).astype(BF)
-
-
-def call(kernel, outs, scratch=()):
+    grad_b = mm(jnp.transpose(dmix_sum).astype(BF), c) + mm_nt(wx_ref[...], adj_b)
+    grad_c = mm(dmix_sum.astype(BF), b) + mm_nt(gw, state_b)
+    half = size // 2
+    out_width = w_ref.shape[1]
+    for src, dst in places:
+        terms_ref[dst, 0:n] = grad_b[src, :]
+        terms_ref[dst, n:2 * n] = grad_c[src, :]
+    theirs_ref[:, out_width:out_width + 2 * n] = terms_ref[0:half, :].astype(BF)
+    mine_ref[:, out_width:out_width + 2 * n] = terms_ref[half:size, :].astype(BF)
+    for h in range(heads):
+        copies[3 + h].wait()
+    step = 512
+    gated = gated_ref[...]
+    for o in range(0, out_width, step):
+        part = mm(gated, w_ref[:, o:o + step]).astype(BF)
+        theirs_ref[:, o:o + step] = part[0:half, :]
+        mine_ref[:, o:o + step] = part[half:size, :]
+
+
+def end_kernel(part_ref, out_ref, gb_ref, gc_ref):
+    out_width = out_ref.shape[1]
+    n = gb_ref.shape[1]
+    total = part_ref[0].astype(F32)
+    for i in range(1, part_ref.shape[0]):
+        total = total + part_ref[i].astype(F32)
+    out_ref[...] = total[:, 0:out_width].astype(BF)
+    gb_ref[...] = total[:, out_width:out_width + n]
+    gc_ref[...] = total[:, out_width + n:out_width + 2 * n]
+
+
+def call(kernel, outs, count, remote=(), scratch=()):
     return pl.pallas_call(
         kernel,
         out_shape=tuple(jax.ShapeDtypeStruct(s, d) for s, d in outs),
+        in_specs=[
+            pl.BlockSpec(memory_space=pltpu.HBM if i in remote else pltpu.VMEM)
+            for i in range(count)
+        ],
         scratch_shapes=list(scratch),
         compiler_params=pltpu.CompilerParams(vmem_limit_bytes=VMEM_LIMIT),
     )
@@ -207,42 +268,56 @@
     chips = tp // 2
     workers = lax.axis_size("ctx")
     piece, out_width = cotangent.shape
-
-    def turn(s):
-        return [(2 * i + k, 2 * ((i + s) % chips) + k) for i in range(chips) for k in range(2)]
-
-    pieces = [cotangent] + [lax.ppermute(cotangent, "tp", turn(s)) for s in range(1, chips)]
-    near = jnp.concatenate(pieces, axis=0)
-    far = lax.ppermute(near, "tp", [(i, i ^ 1) for i in range(tp)])
-
     wide = ((size, full), F32)
+    wide_b = ((size, full), BF)
     square = (heads, size, size)
+    small = pltpu.VMEM((size, n), BF)
+    weights = pltpu.VMEM((full, out_width), BF)
+    lanes = pltpu.VMEM((size, full), F32)
+    rows = pltpu.VMEM((size, full), BF)
+    across = [[2 * i + k for i in range(chips)] for k in range(2)]
+    swap = [(i, i ^ 1) for i in range(tp)]
+
+    near = lax.all_to_all(
+        jnp.broadcast_to(cotangent[None], (chips, piece, out_width)),
+        "tp", 0, 0, tiled=True, axis_index_groups=across,
+    )
+    far = lax.ppermute(near, "tp", swap)
     st, dec, mask, mixt, scores, yi, ec, tail, wx, silu, slope = call(
         functools.partial(pre_kernel, heads),
         [((n, full), F32), ((heads, 8, size), F32), (square, F32), (square, BF), ((size, size), F32),
-         wide, wide, wide, ((size, full), BF), wide, wide],
+         wide, wide, wide, wide_b, wide, wide],
+        5, range(5),
+        [rows, small, small, rows, pltpu.VMEM((heads, size), F32), pltpu.SemaphoreType.DMA((5,))],
     )(inputs, gate_in, b_proj, c_proj, log_decay)
     msg, dg = call(
-        functools.partial(mid_kernel, heads, piece),
+        functools.partial(mid_kernel, heads),
         [((workers, 24, size), BF), wide],
+        8, (2, 3),
+        [weights, pltpu.VMEM((size, out_width), BF), small, pltpu.SemaphoreType.DMA((heads + 1,))],
     )(near, far, w_out, c_proj, silu, ec, st, dec)
     msg = lax.all_to_all(msg, "ctx", 0, 0, tiled=True)
     (back,) = call(
-        scan_kernel,
-        [((workers, 16, size), BF)],
+        scan_kernel, [((workers, 16, size), BF)], 1, (),
         [pltpu.VMEM((workers, 8, size), F32), pltpu.VMEM((workers, 8, size), F32)],
     )(msg)
     back = lax.all_to_all(back, "ctx", 0, 0, tiled=True)
-    part, grad_inputs, grad_gate, grad_decay = call(
-        functools.partial(fin_kernel, heads),
-        [((size, out_width + 2 * n), BF), ((size, full), BF), ((size, full), BF), ((heads, size), F32)],
-        [pltpu.VMEM((n, full), F32), pltpu.VMEM((n, full), F32)],
+    half = ((size // 2, out_width + 2 * n), BF)
+    mine, theirs, grad_inputs, grad_gate, grad_decay = call(
+        functools.partial(fin_kernel, heads, piece),
+        [half, half, wide_b, wide_b, ((heads, size), F32)],
+        16, range(1, 5),
+        [lanes, lanes, rows, pltpu.VMEM((size, 2 * n), F32), rows, small, small, weights,
+         pltpu.SemaphoreType.DMA((heads + 3,))],
     )(back, inputs, b_proj, c_proj, w_out, dg, silu, slope, mask, mixt, scores, yi, ec, tail, wx, dec)
-    part = lax.all_to_all(part.reshape(tp, size // tp, out_width + 2 * n), "tp", 0, 0, tiled=True)
-    total = jnp.sum(part.astype(F32), axis=0)
-    layer_out = total[:, :out_width].astype(BF)
-    grad_b = total[:, out_width:out_width + n]
-    grad_c = total[:, out_width + n:]
+    part = (mine.astype(F32) + lax.ppermute(theirs, "tp", swap).astype(F32)).astype(BF)
+    part = lax.all_to_all(
+        part.reshape(chips, piece, out_width + 2 * n),
+        "tp", 0, 0, tiled=True, axis_index_groups=across,
+    )
+    layer_out, grad_b, grad_c = call(
+        end_kernel, [((piece, out_width), BF), ((piece, n), F32), ((piece, n), F32)], 1
+    )(part)
     return (layer_out, grad_inputs, grad_gate, grad_b, grad_c, grad_decay)
 
 

time: 108 us -> 98 us (0.907)
  starting transfers between devices: 19 us -> 13.2 us
  local copies, waits for them, and re-layouts: 4.45 us -> 1.03 us
    ppermute x4 -> x2, starting transfers between devices: 19 us -> 13.2 us  [the longest x1 7.68 us: local(): far = lax.ppermute(near, 'tp', swap)]
    unnamed x17 -> x10, local copies, waits for them, and re-layouts: 3.16 us -> 0.02 us
    slice x2 -> x0, local copies, waits for them, and re-layouts: 1.28 us -> none  [the longest x1 0.67 us: local(): layer_out = total[:, :out_width].astype(BF)]
    all_to_all x1 -> x2, blocking collectives: 24.2 us -> 23.4 us  [the longest x1 11.8 us: local(): lax.all_to_all(part.reshape(chips, piece, out_width + 2 * n), 'tp', 0, 0,...]
    pallas_call x3 -> x4, Pallas kernels: 9.4 us -> 8.71 us  [the longest x1 4.57 us: local(): call(functools.partial(mid_kernel, heads), [((workers, 24, size), BF), wi...]
  transfers between devices with their start and end apart: 4 -> 2, of which waited for: 1 -> 2; matrix products, arithmetic and copies ran while one was open for 1% -> 0% of each run, Pallas kernels for 1% -> 1%
where the time goes in v2:
time: 98 us; the launch traced here: 97.7 us
  blocking collectives  70.9 us (72%)
  starting transfers between devices  13.2 us (13%)
  Pallas kernels  10 us (10%)
  waiting for transfers between devices  1.72 us (2%)
  local copies, waits for them, and re-layouts  1.03 us (1%)
    all_to_all x1, blocking collectives, local(): msg = lax.all_to_all(msg, 'ctx', 0, 0, tiled=True)  28.8 us
    all_to_all x1, blocking collectives, local(): back = lax.all_to_all(back, 'ctx', 0, 0, tiled=True)  18.7 us
    all_to_all x1, blocking collectives, local(): lax.all_to_all(part.reshape(chips, piece, out_width + 2 * n), 'tp', 0, 0,...  11.8 us
    all_to_all x1, blocking collectives, local(): lax.all_to_all(jnp.broadcast_to(cotangent[None], (chips, piece, out_width...  11.6 us
    ppermute x1, starting transfers between devices, local(): far = lax.ppermute(near, 'tp', swap)  7.68 us
    ppermute x1, starting transfers between devices, local(): lax.ppermute(theirs, 'tp', swap).astype(F32)  5.5 us
    pallas_call x1, Pallas kernels, local(): call(functools.partial(mid_kernel, heads), [((workers, 24, size), BF), wi...  4.57 us
    pallas_call x1, Pallas kernels, local(): call(functools.partial(fin_kernel, heads, piece), [half, half, wide_b, wi...  3.25 us
  transfers between devices with their start and end apart: 2, of which 2 were waited for; matrix products, arithmetic and copies ran while one was open for 0% of the time, Pallas kernels for 1%

profile of v2, /device:TPU:1, one launch (start us, length us, event | category | flops | bytes accessed | tf_op | source)
XLA Modules:
  0.0 97.7 jit_solution(5632483669065345557)
XLA Ops:
  0.6 0.0 copy-start.1
  0.6 0.0 copy-start.3
  0.7 0.0 copy-start
  0.7 0.0 copy-start.4
  0.7 0.0 copy-start.2
  0.7 1.0 %broadcast_in_dim.2 = bf16[4,16,4096]{2,1,0:T(8,128)(2,1)S(1)} broadcast(bf16[16,4096]{1,0:T(8,128)(2,1)} %param.13), dimensions={1,2} | broadcast | bytes 655360 | tf_op jit(solution)/shard_map/broadcast_in_dim | solution.py:282
  1.7 11.6 %all_to_all.20.near_ref = bf16[4,16,4096]{2,1,0:T(8,128)(2,1)S(1)} all-to-all(bf16[4,16,4096]{2,1,0:T(8,128)(2,1)S(1)} %broadcast_in_dim.2), channel_id=1, replica_groups={{0,2,4,6},{1,3,5,7},{8,10,12,14},{9,11,13,15},{16,18,20,22},{17,19,21,2..., dimensions={0} | all-to-all | bytes 1048576 | tf_op jit(solution)/shard_map/all_to_all | solution.py:281
  13.3 7.7 %collective-permute-start = (bf16[4,16,4096]{2,1,0:T(8,128)(2,1)S(1)}, bf16[4,16,4096]{2,1,0:T(8,128)(2,1)S(1)}, u32[]{:S(2)}, u32[]{:S(2)}) collective-permute-start(bf16[4,16,4096]{2,1,0:T(8,128)(2,1)S(1)} %all_to_all.20.near_ref), channel_id=1, source_target_pairs={{0,1},{1,0},{2,3},{3,2},{4,5},{5,4},{6,7},{7,6},{8,9},{9,8},{10,11... | collective-permute-start | bytes 1572872 | tf_op jit(solution)/shard_map/ppermute | solution.py:285
  21.0 0.0 copy-done.1
  21.0 0.0 copy-done.3
  21.0 0.0 copy-done
  21.0 0.0 copy-done.4
  21.0 0.0 copy-done.2
  21.0 1.3 %shard_map.118 = (f32[128,512]{1,0:T(8,128)S(1)}, f32[4,8,128]{2,1,0:T(8,128)S(1)}, f32[4,128,128]{2,1,0:T(8,128)S(1)}, bf16[4,128,128]{2,1,0:T(8,128)(2,1)S(1)}...) custom-call(bf16[128,512]{1,0:T(8,128)(2,1)S(1)} %copy-done, ...), custom_call_target="tpu_custom_call" | custom-call | tf_op jit(solution)/shard_map/pallas_call | solution.py:286
  22.3 0.2 collective-permute-done.far_ref
  22.5 4.6 %shard_map.119 = (bf16[64,24,128]{2,1,0:T(8,128)(2,1)S(1)}, f32[128,512]{1,0:T(8,128)S(1)}) custom-call(bf16[4,16,4096]{2,1,0:T(8,128)(2,1)S(1)} %all_to_all.20.near_ref, bf16[4,16,4096]{2,1,0:T(8,128)(2,1)S(1)} %collective-permute-done.far_ref, bf16[512,4096]{1,0:T(8,128)(2,1)} %w_hbm.3, bf16[128,128]{1,0:T(8,128)(2,1)S(1)} %copy-done.1, ...), custom_call_target="tpu_custom_call" | custom-call | tf_op jit(solution)/shard_map/pallas_call | solution.py:293
  27.0 28.8 %all_to_all.21.msg_ref = bf16[64,24,128]{2,1,0:T(8,128)(2,1)S(1)} all-to-all(bf16[64,24,128]{2,1,0:T(8,128)(2,1)S(1)} %get-tuple-element.31), channel_id=1, replica_groups=mesh['ctx'=64,'tp'=8] {'ctx'}, dimensions={0} | all-to-all | bytes 786432 | tf_op jit(solution)/shard_map/all_to_all | solution.py:299
  55.8 0.2 shard_map.120
  56.0 18.7 %all_to_all.22.back_ref = bf16[64,16,128]{2,1,0:T(8,128)(2,1)S(1)} all-to-all(bf16[64,16,128]{2,1,0:T(8,128)(2,1)S(1)} %shard_map.120), channel_id=1, replica_groups=mesh['ctx'=64,'tp'=8] {'ctx'}, dimensions={0} | all-to-all | bytes 524288 | tf_op jit(solution)/shard_map/all_to_all | solution.py:304
  74.7 3.3 %shard_map.121 = (bf16[64,4352]{1,0:T(8,128)(2,1)S(1)}, bf16[64,4352]{1,0:T(8,128)(2,1)S(1)}, bf16[128,512]{1,0:T(8,128)(2,1)}, bf16[128,512]{1,0:T(8,128)(2,1)}, f32[4,128]{1,0:T(4,128)}) custom-call(bf16[64,16,128]{2,1,0:T(8,128)(2,1)S(1)} %all_to_all.22.back_ref, bf16[128,512]{1,0:T(8,128)(2,1)S(1)} %copy-done, bf16[128,128]{1,0:T(8,128)(2,1)S(1)} %copy-done.3, ...), custom_call_target="tpu_custom_call" | custom-call | tf_op jit(solution)/shard_map/pallas_call | solution.py:306
  78.0 5.5 %collective-permute-start.1 = (bf16[64,4352]{1,0:T(8,128)(2,1)S(1)}, bf16[64,4352]{1,0:T(8,128)(2,1)S(1)}, u32[]{:S(2)}, u32[]{:S(2)}) collective-permute-start(bf16[64,4352]{1,0:T(8,128)(2,1)S(1)} %get-tuple-element.41), channel_id=1, source_target_pairs={{0,1},{1,0},{2,3},{3,2},{4,5},{5,4},{6,7},{7,6},{8,9},{9,8},{10,11... | collective-permute-start | bytes 1671176 | tf_op jit(solution)/shard_map/ppermute | solution.py:313
  83.5 1.6 %collective-permute-done.1 = bf16[64,4352]{1,0:T(8,128)(2,1)S(1)} collective-permute-done((bf16[64,4352]{1,0:T(8,128)(2,1)S(1)}, bf16[64,4352]{1,0:T(8,128)(2,1)S(1)}, u32[]{:S(2)}, u32[]{:S(2)}) %collective-permute-start.1) | collective-permute-done | bytes 557088 | tf_op jit(solution)/shard_map/ppermute | solution.py:313
  85.1 0.1 add_convert_fusion
  85.2 11.8 %all_to_all.23.part_ref = bf16[4,16,4352]{2,1,0:T(8,128)(2,1)S(1)} all-to-all(bf16[4,16,4352]{2,1,0:T(8,128)(2,1)S(1)} %bitcast.1), channel_id=1, replica_groups={{0,2,4,6},{1,3,5,7},{8,10,12,14},{9,11,13,15},{16,18,20,22},{17,19,21,2..., dimensions={0} | all-to-all | bytes 1114112 | tf_op jit(solution)/shard_map/all_to_all | solution.py:314
  97.0 0.7 shard_map.122
Async XLA Ops:
  0.6 20.3 %copy-start.1 = (bf16[128,128]{1,0:T(8,128)(2,1)S(1)}, bf16[128,128]{1,0:T(8,128)(2,1)}, u32[]{:S(2)}) copy-start(bf16[128,128]{1,0:T(8,128)(2,1)} %c_hbm.5) | copy-start | bytes 98308
  0.6 20.3 %copy-start.3 = (bf16[128,128]{1,0:T(8,128)(2,1)S(1)}, bf16[128,128]{1,0:T(8,128)(2,1)}, u32[]{:S(2)}) copy-start(bf16[128,128]{1,0:T(8,128)(2,1)} %b_hbm.3) | copy-start | bytes 98308
  0.7 20.3 %copy-start = (bf16[128,512]{1,0:T(8,128)(2,1)S(1)}, bf16[128,512]{1,0:T(8,128)(2,1)}, u32[]{:S(2)}) copy-start(bf16[128,512]{1,0:T(8,128)(2,1)} %x_hbm.3) | copy-start | bytes 393220
  0.7 20.3 %copy-start.4 = (f32[4,128]{1,0:T(4,128)S(1)}, f32[4,128]{1,0:T(4,128)}, u32[]{:S(2)}) copy-start(f32[4,128]{1,0:T(4,128)} %ld_hbm.1) | copy-start | bytes 6148
  0.7 20.3 %copy-start.2 = (bf16[128,512]{1,0:T(8,128)(2,1)S(1)}, bf16[128,512]{1,0:T(8,128)(2,1)}, u32[]{:S(2)}) copy-start(bf16[128,512]{1,0:T(8,128)(2,1)} %gate_hbm.1) | copy-start | bytes 393220
  13.3 9.2 %collective-permute-start = (bf16[4,16,4096]{2,1,0:T(8,128)(2,1)S(1)}, bf16[4,16,4096]{2,1,0:T(8,128)(2,1)S(1)}, u32[]{:S(2)}, u32[]{:S(2)}) collective-permute-start(bf16[4,16,4096]{2,1,0:T(8,128)(2,1)S(1)} %all_to_all.20.near_ref), channel_id=1, source_target_pairs={{0,1},{1,0},{2,3},{3,2},{4,5},{5,4},{6,7},{7,6},{8,9},{9,8},{10,11... | collective-permute-start | bytes 1572872 | tf_op jit(solution)/shard_map/ppermute | solution.py:285
  78.0 7.1 %collective-permute-start.1 = (bf16[64,4352]{1,0:T(8,128)(2,1)S(1)}, bf16[64,4352]{1,0:T(8,128)(2,1)S(1)}, u32[]{:S(2)}, u32[]{:S(2)}) collective-permute-start(bf16[64,4352]{1,0:T(8,128)(2,1)S(1)} %get-tuple-element.41), channel_id=1, source_target_pairs={{0,1},{1,0},{2,3},{3,2},{4,5},{5,4},{6,7},{7,6},{8,9},{9,8},{10,11... | collective-permute-start | bytes 1671176 | tf_op jit(solution)/shard_map/ppermute | solution.py:313

commit v3 on v2

--- a/solution.py
+++ b/solution.py
@@ -11,6 +11,7 @@
 F32 = jnp.float32
 NT = (((1,), (1,)), ((), ()))
 VMEM_LIMIT = 48 * 1024 * 1024
+ROWS = 18
 
 
 def mm(a, b):
@@ -86,10 +87,7 @@
         wx = (x.astype(F32) * tail).astype(BF)
         wx_ref[:, at] = wx
         st_ref[:, at] = mm(b_t, wx)
-        decay = jnp.broadcast_to(jnp.exp(last), (8, size))
-        hi = decay.astype(BF).astype(F32)
-        lo = decay - hi
-        dec_ref[h] = jnp.where(lax.broadcasted_iota(jnp.int32, (8, size), 0) < 4, hi, lo)
+        dec_ref[h] = jnp.broadcast_to(jnp.exp(last), (8, size))
     copies[4].wait()
     v = gate_ref[...].astype(F32)
     g = 1.0 / (1.0 + jnp.exp(-v))
@@ -114,34 +112,42 @@
         cot_ref[pl.ds(at, piece), :] = far_ref[s]
     copies[heads].wait()
     c_t = flip(c_ref[...])
+    sub = lax.broadcasted_iota(jnp.int32, (2, size), 0)
     for h in range(heads):
         at = slice(h * width, (h + 1) * width)
-        copies[h].wait()
-        dg = mm_nt(cot_ref[...], w_ref[at, :])
+        if h % 2 == 0:
+            copies[h].wait()
+            copies[h + 1].wait()
+        dg = jnp.transpose(mm_nt(w_ref[at, :], cot_ref[...]))
         dg_ref[:, at] = dg
         gw = (dg * silu_ref[:, at] * ec_ref[:, at]).astype(BF)
         inj = mm(c_t, gw)
-        pair = dec_ref[h].astype(BF)
+        decay = dec_ref[h][0:2, :]
+        hi = decay.astype(BF).astype(F32)
+        pair = jnp.where(sub == 0, hi, decay - hi).astype(BF)
         for a in range(size // 8):
-            j = a * heads + h
+            j = ROWS * (a * heads + h)
             both = jnp.concatenate([st_ref[8 * a:8 * a + 8, at], inj[8 * a:8 * a + 8, :]], axis=0)
-            msg_ref[j, 0:16, :] = both.astype(BF)
-            msg_ref[j, 16:24, :] = pair
+            msg_ref[j:j + 16, :] = both.astype(BF)
+            msg_ref[j + 16:j + 18, :] = pair
 
 
 def scan_kernel(msg_ref, out_ref, dec_ref, state_ref):
-    count = msg_ref.shape[0]
-    state = jnp.zeros((8, msg_ref.shape[2]), F32)
+    count = out_ref.shape[0]
+    lanes = out_ref.shape[2]
+    state = jnp.zeros((8, lanes), F32)
     for k in range(count):
-        pair = msg_ref[k, 16:24, :].astype(F32)
-        decay = pair + pltpu.roll(pair, 4, 0)
+        at = ROWS * k
+        pair = msg_ref[at + 16:at + 18, :].astype(F32)
+        decay = jnp.broadcast_to(jnp.sum(pair, axis=0, keepdims=True), (8, lanes))
         dec_ref[k] = decay
         state_ref[k] = state
-        state = decay * state + msg_ref[k, 0:8, :].astype(F32)
-    adjoint = jnp.zeros((8, msg_ref.shape[2]), F32)
+        state = decay * state + msg_ref[at:at + 8, :].astype(F32)
+    adjoint = jnp.zeros((8, lanes), F32)
     for k in reversed(range(count)):
+        at = ROWS * k
         out_ref[k] = jnp.concatenate([state_ref[k], adjoint], axis=0).astype(BF)
-        adjoint = dec_ref[k] * adjoint + msg_ref[k, 8:16, :].astype(F32)
+        adjoint = dec_ref[k] * adjoint + msg_ref[at + 8:at + 16, :].astype(F32)
 
 
 def fin_kernel(heads, piece, back_ref, x_hbm, b_hbm, c_hbm, w_hbm, dg_ref, silu_ref, slope_ref, mask_ref,
@@ -209,10 +215,9 @@
         down = jnp.sum(cross + entering[:, at] - through[:, at], axis=1, keepdims=True)
         columns = jnp.where(col == h, down, columns)
         lines = jnp.where(sub == h, jnp.sum(cross, axis=0, keepdims=True), lines)
-        decay = dec_ref[h] + pltpu.roll(dec_ref[h], 4, 0)
         end = jnp.sum(jnp.sum(through[:, at], axis=0, keepdims=True), axis=1, keepdims=True)
         dots = jnp.sum(jnp.sum(product[:, at], axis=0, keepdims=True), axis=1, keepdims=True)
-        closing = jnp.where(sub == h, end + decay * dots, closing)
+        closing = jnp.where(sub == h, end + dec_ref[h] * dots, closing)
     flow = jnp.transpose(columns)[0:8, :] - lines
     total = sum_by(flow, (row >= col).astype(BF)) + closing
     gd_ref[...] = total[0:heads, :]
@@ -292,11 +297,12 @@
     )(inputs, gate_in, b_proj, c_proj, log_decay)
     msg, dg = call(
         functools.partial(mid_kernel, heads),
-        [((workers, 24, size), BF), wide],
+        [((workers * ROWS, size), BF), wide],
         8, (2, 3),
         [weights, pltpu.VMEM((size, out_width), BF), small, pltpu.SemaphoreType.DMA((heads + 1,))],
     )(near, far, w_out, c_proj, silu, ec, st, dec)
-    msg = lax.all_to_all(msg, "ctx", 0, 0, tiled=True)
+    msg = lax.all_to_all(msg.reshape(workers, ROWS // 2, 2, size), "ctx", 0, 0, tiled=True)
+    msg = msg.reshape(workers * ROWS, size)
     (back,) = call(
         scan_kernel, [((workers, 16, size), BF)], 1, (),
         [pltpu.VMEM((workers, 8, size), F32), pltpu.VMEM((workers, 8, size), F32)],

time: 98 us -> 96.3 us (0.983)
  blocking collectives: 70.9 us -> 68.7 us
    all_to_all x1, blocking collectives: 28.8 us -> 27.5 us  [local(): lax.all_to_all(msg.reshape(workers, ROWS // 2, 2, size), 'ctx', 0, 0, til...]
where the time goes in v3:
time: 96.3 us; the launch traced here: 96 us
  blocking collectives  68.7 us (71%)
  starting transfers between devices  13.1 us (14%)
  Pallas kernels  10.5 us (11%)
  waiting for transfers between devices  1.72 us (2%)
  local copies, waits for them, and re-layouts  1.03 us (1%)
    all_to_all x1, blocking collectives, local(): lax.all_to_all(msg.reshape(workers, ROWS // 2, 2, size), 'ctx', 0, 0, til...  27.5 us
    all_to_all x1, blocking collectives, local(): back = lax.all_to_all(back, 'ctx', 0, 0, tiled=True)  17.8 us
    all_to_all x1, blocking collectives, local(): lax.all_to_all(part.reshape(chips, piece, out_width + 2 * n), 'tp', 0, 0,...  11.8 us
    all_to_all x1, blocking collectives, local(): lax.all_to_all(jnp.broadcast_to(cotangent[None], (chips, piece, out_width...  11.6 us
    ppermute x1, starting transfers between devices, local(): far = lax.ppermute(near, 'tp', swap)  7.68 us
    ppermute x1, starting transfers between devices, local(): lax.ppermute(theirs, 'tp', swap).astype(F32)  5.46 us
    pallas_call x1, Pallas kernels, local(): call(functools.partial(mid_kernel, heads), [((workers * ROWS, size), BF),...  4.91 us
    pallas_call x1, Pallas kernels, local(): call(functools.partial(fin_kernel, heads, piece), [half, half, wide_b, wi...  3.26 us
  transfers between devices with their start and end apart: 2, of which 2 were waited for; matrix products, arithmetic and copies ran while one was open for 0% of the time, Pallas kernels for 1%

profile of v3, /device:TPU:1, one launch (start us, length us, event | category | flops | bytes accessed | tf_op | source)
XLA Modules:
  0.0 96.0 jit_solution(3428415427823885459)
XLA Ops:
  0.6 0.0 copy-start.1
  0.6 0.0 copy-start.3
  0.7 0.0 copy-start
  0.7 0.0 copy-start.4
  0.7 0.0 copy-start.2
  0.7 1.0 %broadcast_in_dim.2 = bf16[4,16,4096]{2,1,0:T(8,128)(2,1)S(1)} broadcast(bf16[16,4096]{1,0:T(8,128)(2,1)} %param.13), dimensions={1,2} | broadcast | bytes 655360 | tf_op jit(solution)/shard_map/broadcast_in_dim | solution.py:287
  1.7 11.6 %all_to_all.20.near_ref = bf16[4,16,4096]{2,1,0:T(8,128)(2,1)S(1)} all-to-all(bf16[4,16,4096]{2,1,0:T(8,128)(2,1)S(1)} %broadcast_in_dim.2), channel_id=1, replica_groups={{0,2,4,6},{1,3,5,7},{8,10,12,14},{9,11,13,15},{16,18,20,22},{17,19,21,2..., dimensions={0} | all-to-all | bytes 1048576 | tf_op jit(solution)/shard_map/all_to_all | solution.py:286
  13.3 7.7 %collective-permute-start = (bf16[4,16,4096]{2,1,0:T(8,128)(2,1)S(1)}, bf16[4,16,4096]{2,1,0:T(8,128)(2,1)S(1)}, u32[]{:S(2)}, u32[]{:S(2)}) collective-permute-start(bf16[4,16,4096]{2,1,0:T(8,128)(2,1)S(1)} %all_to_all.20.near_ref), channel_id=1, source_target_pairs={{0,1},{1,0},{2,3},{3,2},{4,5},{5,4},{6,7},{7,6},{8,9},{9,8},{10,11... | collective-permute-start | bytes 1572872 | tf_op jit(solution)/shard_map/ppermute | solution.py:290
  21.0 0.0 copy-done.1
  21.0 0.0 copy-done.3
  21.0 0.0 copy-done
  21.0 0.0 copy-done.4
  21.0 0.0 copy-done.2
  21.0 1.3 %shard_map.118 = (f32[128,512]{1,0:T(8,128)S(1)}, f32[4,8,128]{2,1,0:T(8,128)S(1)}, f32[4,128,128]{2,1,0:T(8,128)S(1)}, bf16[4,128,128]{2,1,0:T(8,128)(2,1)S(1)}...) custom-call(bf16[128,512]{1,0:T(8,128)(2,1)S(1)} %copy-done, ...), custom_call_target="tpu_custom_call" | custom-call | tf_op jit(solution)/shard_map/pallas_call | solution.py:291
  22.3 0.2 collective-permute-done.far_ref
  22.5 4.9 %shard_map.119 = (bf16[1152,128]{1,0:T(8,128)(2,1)S(1)}, f32[128,512]{1,0:T(8,128)S(1)}) custom-call(bf16[4,16,4096]{2,1,0:T(8,128)(2,1)S(1)} %all_to_all.20.near_ref, bf16[4,16,4096]{2,1,0:T(8,128)(2,1)S(1)} %collective-permute-done.far_ref, bf16[512,4096]{1,0:T(8,128)(2,1)} %w_hbm.3, bf16[128,128]{1,0:T(8,128)(2,1)S(1)} %copy-done.1, ...), custom_call_target="tpu_custom_call" | custom-call | tf_op jit(solution)/shard_map/pallas_call | solution.py:298
  27.4 27.5 %all_to_all.21 = bf16[64,9,2,128]{3,2,1,0:T(2,128)(2,1)S(1)} all-to-all(bf16[64,9,2,128]{3,2,1,0:T(2,128)(2,1)S(1)} %bitcast.4), channel_id=1, replica_groups=mesh['ctx'=64,'tp'=8] {'ctx'}, dimensions={0} | all-to-all | bytes 589824 | tf_op jit(solution)/shard_map/all_to_all | solution.py:304
  54.9 0.3 shard_map.120
  55.2 17.8 %all_to_all.22.back_ref = bf16[64,16,128]{2,1,0:T(8,128)(2,1)S(1)} all-to-all(bf16[64,16,128]{2,1,0:T(8,128)(2,1)S(1)} %shard_map.120), channel_id=1, replica_groups=mesh['ctx'=64,'tp'=8] {'ctx'}, dimensions={0} | all-to-all | bytes 524288 | tf_op jit(solution)/shard_map/all_to_all | solution.py:310
  73.0 3.3 %shard_map.121 = (bf16[64,4352]{1,0:T(8,128)(2,1)S(1)}, bf16[64,4352]{1,0:T(8,128)(2,1)S(1)}, bf16[128,512]{1,0:T(8,128)(2,1)}, bf16[128,512]{1,0:T(8,128)(2,1)}, f32[4,128]{1,0:T(4,128)}) custom-call(bf16[64,16,128]{2,1,0:T(8,128)(2,1)S(1)} %all_to_all.22.back_ref, bf16[128,512]{1,0:T(8,128)(2,1)S(1)} %copy-done, bf16[128,128]{1,0:T(8,128)(2,1)S(1)} %copy-done.3, ...), custom_call_target="tpu_custom_call" | custom-call | tf_op jit(solution)/shard_map/pallas_call | solution.py:312
  76.3 5.5 %collective-permute-start.1 = (bf16[64,4352]{1,0:T(8,128)(2,1)S(1)}, bf16[64,4352]{1,0:T(8,128)(2,1)S(1)}, u32[]{:S(2)}, u32[]{:S(2)}) collective-permute-start(bf16[64,4352]{1,0:T(8,128)(2,1)S(1)} %get-tuple-element.41), channel_id=1, source_target_pairs={{0,1},{1,0},{2,3},{3,2},{4,5},{5,4},{6,7},{7,6},{8,9},{9,8},{10,11... | collective-permute-start | bytes 1671176 | tf_op jit(solution)/shard_map/ppermute | solution.py:319
  81.7 1.6 %collective-permute-done.1 = bf16[64,4352]{1,0:T(8,128)(2,1)S(1)} collective-permute-done((bf16[64,4352]{1,0:T(8,128)(2,1)S(1)}, bf16[64,4352]{1,0:T(8,128)(2,1)S(1)}, u32[]{:S(2)}, u32[]{:S(2)}) %collective-permute-start.1) | collective-permute-done | bytes 557088 | tf_op jit(solution)/shard_map/ppermute | solution.py:319
  83.3 0.1 add_convert_fusion
  83.4 11.8 %all_to_all.23.part_ref = bf16[4,16,4352]{2,1,0:T(8,128)(2,1)S(1)} all-to-all(bf16[4,16,4352]{2,1,0:T(8,128)(2,1)S(1)} %bitcast.5), channel_id=1, replica_groups={{0,2,4,6},{1,3,5,7},{8,10,12,14},{9,11,13,15},{16,18,20,22},{17,19,21,2..., dimensions={0} | all-to-all | bytes 1114112 | tf_op jit(solution)/shard_map/all_to_all | solution.py:320
  95.2 0.7 shard_map.122
Async XLA Ops:
  0.6 20.3 %copy-start.1 = (bf16[128,128]{1,0:T(8,128)(2,1)S(1)}, bf16[128,128]{1,0:T(8,128)(2,1)}, u32[]{:S(2)}) copy-start(bf16[128,128]{1,0:T(8,128)(2,1)} %c_hbm.5) | copy-start | bytes 98308
  0.6 20.3 %copy-start.3 = (bf16[128,128]{1,0:T(8,128)(2,1)S(1)}, bf16[128,128]{1,0:T(8,128)(2,1)}, u32[]{:S(2)}) copy-start(bf16[128,128]{1,0:T(8,128)(2,1)} %b_hbm.3) | copy-start | bytes 98308
  0.7 20.3 %copy-start = (bf16[128,512]{1,0:T(8,128)(2,1)S(1)}, bf16[128,512]{1,0:T(8,128)(2,1)}, u32[]{:S(2)}) copy-start(bf16[128,512]{1,0:T(8,128)(2,1)} %x_hbm.3) | copy-start | bytes 393220
  0.7 20.3 %copy-start.4 = (f32[4,128]{1,0:T(4,128)S(1)}, f32[4,128]{1,0:T(4,128)}, u32[]{:S(2)}) copy-start(f32[4,128]{1,0:T(4,128)} %ld_hbm.1) | copy-start | bytes 6148
  0.7 20.3 %copy-start.2 = (bf16[128,512]{1,0:T(8,128)(2,1)S(1)}, bf16[128,512]{1,0:T(8,128)(2,1)}, u32[]{:S(2)}) copy-start(bf16[128,512]{1,0:T(8,128)(2,1)} %gate_hbm.1) | copy-start | bytes 393220
  13.3 9.2 %collective-permute-start = (bf16[4,16,4096]{2,1,0:T(8,128)(2,1)S(1)}, bf16[4,16,4096]{2,1,0:T(8,128)(2,1)S(1)}, u32[]{:S(2)}, u32[]{:S(2)}) collective-permute-start(bf16[4,16,4096]{2,1,0:T(8,128)(2,1)S(1)} %all_to_all.20.near_ref), channel_id=1, source_target_pairs={{0,1},{1,0},{2,3},{3,2},{4,5},{5,4},{6,7},{7,6},{8,9},{9,8},{10,11... | collective-permute-start | bytes 1572872 | tf_op jit(solution)/shard_map/ppermute | solution.py:290
  76.3 7.0 %collective-permute-start.1 = (bf16[64,4352]{1,0:T(8,128)(2,1)S(1)}, bf16[64,4352]{1,0:T(8,128)(2,1)S(1)}, u32[]{:S(2)}, u32[]{:S(2)}) collective-permute-start(bf16[64,4352]{1,0:T(8,128)(2,1)S(1)} %get-tuple-element.41), channel_id=1, source_target_pairs={{0,1},{1,0},{2,3},{3,2},{4,5},{5,4},{6,7},{7,6},{8,9},{9,8},{10,11... | collective-permute-start | bytes 1671176 | tf_op jit(solution)/shard_map/ppermute | solution.py:319

commit v4 on v3

--- a/solution.py
+++ b/solution.py
@@ -12,6 +12,7 @@
 NT = (((1,), (1,)), ((), ()))
 VMEM_LIMIT = 48 * 1024 * 1024
 ROWS = 18
+CHUNKS = 8
 
 
 def mm(a, b):
@@ -50,6 +51,12 @@
     for copy in copies:
         copy.start()
     return copies
+
+
+def strips(src, dst):
+    step = dst.shape[1] // CHUNKS
+    cuts = [pl.ds(i * step, step) for i in range(CHUNKS)]
+    return [(src.at[:, cut], dst.at[:, cut]) for cut in cuts]
 
 
 def pre_kernel(heads, x_hbm, gate_hbm, b_hbm, c_hbm, ld_hbm,
@@ -100,27 +107,27 @@
     chips, piece = near_ref.shape[:2]
     size, full = st_ref.shape
     width = full // heads
-    copies = fetch(
-        [(w_hbm.at[pl.ds(h * width, width), :], w_ref.at[pl.ds(h * width, width), :])
-         for h in range(heads)] + [(c_hbm, c_ref)], sems
-    )
+    chunk = w_ref.shape[1] // CHUNKS
+    copies = fetch(strips(w_hbm, w_ref) + [(c_hbm, c_ref)], sems)
     core = lax.axis_index("tp") % 2
     for s in range(chips):
         at = pl.multiple_of(piece * (2 * s + core), piece)
         cot_ref[pl.ds(at, piece), :] = near_ref[s]
         at = pl.multiple_of(piece * (2 * s + 1 - core), piece)
         cot_ref[pl.ds(at, piece), :] = far_ref[s]
-    copies[heads].wait()
+    copies[CHUNKS].wait()
     c_t = flip(c_ref[...])
+    total = None
+    for i in range(CHUNKS):
+        copies[i].wait()
+        part = slice(i * chunk, (i + 1) * chunk)
+        term = mm_nt(cot_ref[:, part], w_ref[:, part])
+        total = term if total is None else total + term
+    dg_ref[...] = total
     sub = lax.broadcasted_iota(jnp.int32, (2, size), 0)
     for h in range(heads):
         at = slice(h * width, (h + 1) * width)
-        if h % 2 == 0:
-            copies[h].wait()
-            copies[h + 1].wait()
-        dg = jnp.transpose(mm_nt(w_ref[at, :], cot_ref[...]))
-        dg_ref[:, at] = dg
-        gw = (dg * silu_ref[:, at] * ec_ref[:, at]).astype(BF)
+        gw = (total[:, at] * silu_ref[:, at] * ec_ref[:, at]).astype(BF)
         inj = mm(c_t, gw)
         decay = dec_ref[h][0:2, :]
         hi = decay.astype(BF).astype(F32)
@@ -157,9 +164,7 @@
     size, full = x_ref.shape
     width = full // heads
     copies = fetch(
-        [(b_hbm, b_ref), (c_hbm, c_ref), (x_hbm, x_ref)]
-        + [(w_hbm.at[pl.ds(h * width, width), :], w_ref.at[pl.ds(h * width, width), :])
-           for h in range(heads)], sems
+        [(b_hbm, b_ref), (c_hbm, c_ref), (x_hbm, x_ref)] + strips(w_hbm, w_ref), sems
     )
     for a in range(size // 8):
         for h in range(heads):
@@ -231,11 +236,11 @@
         terms_ref[dst, n:2 * n] = grad_c[src, :]
     theirs_ref[:, out_width:out_width + 2 * n] = terms_ref[0:half, :].astype(BF)
     mine_ref[:, out_width:out_width + 2 * n] = terms_ref[half:size, :].astype(BF)
-    for h in range(heads):
-        copies[3 + h].wait()
-    step = 512
+    step = out_width // CHUNKS
     gated = gated_ref[...]
-    for o in range(0, out_width, step):
+    for i in range(CHUNKS):
+        copies[3 + i].wait()
+        o = i * step
         part = mm(gated, w_ref[:, o:o + step]).astype(BF)
         theirs_ref[:, o:o + step] = part[0:half, :]
         mine_ref[:, o:o + step] = part[half:size, :]
@@ -299,7 +304,7 @@
         functools.partial(mid_kernel, heads),
         [((workers * ROWS, size), BF), wide],
         8, (2, 3),
-        [weights, pltpu.VMEM((size, out_width), BF), small, pltpu.SemaphoreType.DMA((heads + 1,))],
+        [weights, pltpu.VMEM((size, out_width), BF), small, pltpu.SemaphoreType.DMA((CHUNKS + 1,))],
     )(near, far, w_out, c_proj, silu, ec, st, dec)
     msg = lax.all_to_all(msg.reshape(workers, ROWS // 2, 2, size), "ctx", 0, 0, tiled=True)
     msg = msg.reshape(workers * ROWS, size)
@@ -314,7 +319,7 @@
         [half, half, wide_b, wide_b, ((heads, size), F32)],
         16, range(1, 5),
         [lanes, lanes, rows, pltpu.VMEM((size, 2 * n), F32), rows, small, small, weights,
-         pltpu.SemaphoreType.DMA((heads + 3,))],
+         pltpu.SemaphoreType.DMA((CHUNKS + 3,))],
     )(back, inputs, b_proj, c_proj, w_out, dg, silu, slope, mask, mixt, scores, yi, ec, tail, wx, dec)
     part = (mine.astype(F32) + lax.ppermute(theirs, "tp", swap).astype(F32)).astype(BF)
     part = lax.all_to_all(

time: 96.3 us -> 95 us (0.987)
  Pallas kernels: 10.5 us -> 9.22 us
    pallas_call x1, Pallas kernels: 4.91 us -> 3.15 us  [local(): call(functools.partial(mid_kernel, heads), [((workers * ROWS, size), BF),...]
where the time goes in v4:
time: 95 us; the launch traced here: 94.7 us
  blocking collectives  68.7 us (72%)
  starting transfers between devices  13.2 us (14%)
  Pallas kernels  9.22 us (10%)
  waiting for transfers between devices  1.72 us (2%)
  local copies, waits for them, and re-layouts  1.03 us (1%)
    all_to_all x1, blocking collectives, local(): lax.all_to_all(msg.reshape(workers, ROWS // 2, 2, size), 'ctx', 0, 0, til...  27.5 us
    all_to_all x1, blocking collectives, local(): back = lax.all_to_all(back, 'ctx', 0, 0, tiled=True)  17.8 us
    all_to_all x1, blocking collectives, local(): lax.all_to_all(part.reshape(chips, piece, out_width + 2 * n), 'tp', 0, 0,...  11.8 us
    all_to_all x1, blocking collectives, local(): lax.all_to_all(jnp.broadcast_to(cotangent[None], (chips, piece, out_width...  11.6 us
    ppermute x1, starting transfers between devices, local(): far = lax.ppermute(near, 'tp', swap)  7.68 us
    ppermute x1, starting transfers between devices, local(): lax.ppermute(theirs, 'tp', swap).astype(F32)  5.48 us
    pallas_call x1, Pallas kernels, local(): call(functools.partial(fin_kernel, heads, piece), [half, half, wide_b, wi...  3.78 us
    pallas_call x1, Pallas kernels, local(): call(functools.partial(mid_kernel, heads), [((workers * ROWS, size), BF),...  3.15 us
  transfers between devices with their start and end apart: 2, of which 2 were waited for; matrix products, arithmetic and copies ran while one was open for 0% of the time, Pallas kernels for 1%

profile of v4, /device:TPU:1, one launch (start us, length us, event | category | flops | bytes accessed | tf_op | source)
XLA Modules:
  0.0 94.7 jit_solution(15664722981845091139)
XLA Ops:
  0.6 0.0 copy-start.1
  0.6 0.0 copy-start.3
  0.7 0.0 copy-start
  0.7 0.0 copy-start.4
  0.7 0.0 copy-start.2
  0.7 1.0 %broadcast_in_dim.2 = bf16[4,16,4096]{2,1,0:T(8,128)(2,1)S(1)} broadcast(bf16[16,4096]{1,0:T(8,128)(2,1)} %param.13), dimensions={1,2} | broadcast | bytes 655360 | tf_op jit(solution)/shard_map/broadcast_in_dim | solution.py:292
  1.7 11.6 %all_to_all.20.near_ref = bf16[4,16,4096]{2,1,0:T(8,128)(2,1)S(1)} all-to-all(bf16[4,16,4096]{2,1,0:T(8,128)(2,1)S(1)} %broadcast_in_dim.2), channel_id=1, replica_groups={{0,2,4,6},{1,3,5,7},{8,10,12,14},{9,11,13,15},{16,18,20,22},{17,19,21,2..., dimensions={0} | all-to-all | bytes 1048576 | tf_op jit(solution)/shard_map/all_to_all | solution.py:291
  13.3 7.7 %collective-permute-start = (bf16[4,16,4096]{2,1,0:T(8,128)(2,1)S(1)}, bf16[4,16,4096]{2,1,0:T(8,128)(2,1)S(1)}, u32[]{:S(2)}, u32[]{:S(2)}) collective-permute-start(bf16[4,16,4096]{2,1,0:T(8,128)(2,1)S(1)} %all_to_all.20.near_ref), channel_id=1, source_target_pairs={{0,1},{1,0},{2,3},{3,2},{4,5},{5,4},{6,7},{7,6},{8,9},{9,8},{10,11... | collective-permute-start | bytes 1572872 | tf_op jit(solution)/shard_map/ppermute | solution.py:295
  21.0 0.0 copy-done.1
  21.0 0.0 copy-done.3
  21.0 0.0 copy-done
  21.0 0.0 copy-done.4
  21.0 0.0 copy-done.2
  21.0 1.3 %shard_map.118 = (f32[128,512]{1,0:T(8,128)S(1)}, f32[4,8,128]{2,1,0:T(8,128)S(1)}, f32[4,128,128]{2,1,0:T(8,128)S(1)}, bf16[4,128,128]{2,1,0:T(8,128)(2,1)S(1)}...) custom-call(bf16[128,512]{1,0:T(8,128)(2,1)S(1)} %copy-done, ...), custom_call_target="tpu_custom_call" | custom-call | tf_op jit(solution)/shard_map/pallas_call | solution.py:296
  22.3 0.2 collective-permute-done.far_ref
  22.5 3.1 %shard_map.119 = (bf16[1152,128]{1,0:T(8,128)(2,1)S(1)}, f32[128,512]{1,0:T(8,128)S(1)}) custom-call(bf16[4,16,4096]{2,1,0:T(8,128)(2,1)S(1)} %all_to_all.20.near_ref, bf16[4,16,4096]{2,1,0:T(8,128)(2,1)S(1)} %collective-permute-done.far_ref, bf16[512,4096]{1,0:T(8,128)(2,1)} %w_hbm.3, bf16[128,128]{1,0:T(8,128)(2,1)S(1)} %copy-done.1, ...), custom_call_target="tpu_custom_call" | custom-call | tf_op jit(solution)/shard_map/pallas_call | solution.py:303
  25.6 27.5 %all_to_all.21 = bf16[64,9,2,128]{3,2,1,0:T(2,128)(2,1)S(1)} all-to-all(bf16[64,9,2,128]{3,2,1,0:T(2,128)(2,1)S(1)} %bitcast.4), channel_id=1, replica_groups=mesh['ctx'=64,'tp'=8] {'ctx'}, dimensions={0} | all-to-all | bytes 589824 | tf_op jit(solution)/shard_map/all_to_all | solution.py:309
  53.1 0.3 shard_map.120
  53.4 17.8 %all_to_all.22.back_ref = bf16[64,16,128]{2,1,0:T(8,128)(2,1)S(1)} all-to-all(bf16[64,16,128]{2,1,0:T(8,128)(2,1)S(1)} %shard_map.120), channel_id=1, replica_groups=mesh['ctx'=64,'tp'=8] {'ctx'}, dimensions={0} | all-to-all | bytes 524288 | tf_op jit(solution)/shard_map/all_to_all | solution.py:315
  71.2 3.8 %shard_map.121 = (bf16[64,4352]{1,0:T(8,128)(2,1)S(1)}, bf16[64,4352]{1,0:T(8,128)(2,1)S(1)}, bf16[128,512]{1,0:T(8,128)(2,1)}, bf16[128,512]{1,0:T(8,128)(2,1)}, f32[4,128]{1,0:T(4,128)}) custom-call(bf16[64,16,128]{2,1,0:T(8,128)(2,1)S(1)} %all_to_all.22.back_ref, bf16[128,512]{1,0:T(8,128)(2,1)S(1)} %copy-done, bf16[128,128]{1,0:T(8,128)(2,1)S(1)} %copy-done.3, ...), custom_call_target="tpu_custom_call" | custom-call | tf_op jit(solution)/shard_map/pallas_call | solution.py:317
  75.0 5.5 %collective-permute-start.1 = (bf16[64,4352]{1,0:T(8,128)(2,1)S(1)}, bf16[64,4352]{1,0:T(8,128)(2,1)S(1)}, u32[]{:S(2)}, u32[]{:S(2)}) collective-permute-start(bf16[64,4352]{1,0:T(8,128)(2,1)S(1)} %get-tuple-element.41), channel_id=1, source_target_pairs={{0,1},{1,0},{2,3},{3,2},{4,5},{5,4},{6,7},{7,6},{8,9},{9,8},{10,11... | collective-permute-start | bytes 1671176 | tf_op jit(solution)/shard_map/ppermute | solution.py:324
  80.5 1.6 %collective-permute-done.1 = bf16[64,4352]{1,0:T(8,128)(2,1)S(1)} collective-permute-done((bf16[64,4352]{1,0:T(8,128)(2,1)S(1)}, bf16[64,4352]{1,0:T(8,128)(2,1)S(1)}, u32[]{:S(2)}, u32[]{:S(2)}) %collective-permute-start.1) | collective-permute-done | bytes 557088 | tf_op jit(solution)/shard_map/ppermute | solution.py:324
  82.1 0.1 add_convert_fusion
  82.2 11.8 %all_to_all.23.part_ref = bf16[4,16,4352]{2,1,0:T(8,128)(2,1)S(1)} all-to-all(bf16[4,16,4352]{2,1,0:T(8,128)(2,1)S(1)} %bitcast.5), channel_id=1, replica_groups={{0,2,4,6},{1,3,5,7},{8,10,12,14},{9,11,13,15},{16,18,20,22},{17,19,21,2..., dimensions={0} | all-to-all | bytes 1114112 | tf_op jit(solution)/shard_map/all_to_all | solution.py:325
  94.0 0.7 shard_map.122
Async XLA Ops:
  0.6 20.3 %copy-start.1 = (bf16[128,128]{1,0:T(8,128)(2,1)S(1)}, bf16[128,128]{1,0:T(8,128)(2,1)}, u32[]{:S(2)}) copy-start(bf16[128,128]{1,0:T(8,128)(2,1)} %c_hbm.5) | copy-start | bytes 98308
  0.6 20.3 %copy-start.3 = (bf16[128,128]{1,0:T(8,128)(2,1)S(1)}, bf16[128,128]{1,0:T(8,128)(2,1)}, u32[]{:S(2)}) copy-start(bf16[128,128]{1,0:T(8,128)(2,1)} %b_hbm.3) | copy-start | bytes 98308
  0.7 20.3 %copy-start = (bf16[128,512]{1,0:T(8,128)(2,1)S(1)}, bf16[128,512]{1,0:T(8,128)(2,1)}, u32[]{:S(2)}) copy-start(bf16[128,512]{1,0:T(8,128)(2,1)} %x_hbm.3) | copy-start | bytes 393220
  0.7 20.3 %copy-start.4 = (f32[4,128]{1,0:T(4,128)S(1)}, f32[4,128]{1,0:T(4,128)}, u32[]{:S(2)}) copy-start(f32[4,128]{1,0:T(4,128)} %ld_hbm.1) | copy-start | bytes 6148
  0.7 20.3 %copy-start.2 = (bf16[128,512]{1,0:T(8,128)(2,1)S(1)}, bf16[128,512]{1,0:T(8,128)(2,1)}, u32[]{:S(2)}) copy-start(bf16[128,512]{1,0:T(8,128)(2,1)} %gate_hbm.1) | copy-start | bytes 393220
  13.3 9.2 %collective-permute-start = (bf16[4,16,4096]{2,1,0:T(8,128)(2,1)S(1)}, bf16[4,16,4096]{2,1,0:T(8,128)(2,1)S(1)}, u32[]{:S(2)}, u32[]{:S(2)}) collective-permute-start(bf16[4,16,4096]{2,1,0:T(8,128)(2,1)S(1)} %all_to_all.20.near_ref), channel_id=1, source_target_pairs={{0,1},{1,0},{2,3},{3,2},{4,5},{5,4},{6,7},{7,6},{8,9},{9,8},{10,11... | collective-permute-start | bytes 1572872 | tf_op jit(solution)/shard_map/ppermute | solution.py:295
  75.0 7.0 %collective-permute-start.1 = (bf16[64,4352]{1,0:T(8,128)(2,1)S(1)}, bf16[64,4352]{1,0:T(8,128)(2,1)S(1)}, u32[]{:S(2)}, u32[]{:S(2)}) collective-permute-start(bf16[64,4352]{1,0:T(8,128)(2,1)S(1)} %get-tuple-element.41), channel_id=1, source_target_pairs={{0,1},{1,0},{2,3},{3,2},{4,5},{5,4},{6,7},{7,6},{8,9},{9,8},{10,11... | collective-permute-start | bytes 1671176 | tf_op jit(solution)/shard_map/ppermute | solution.py:324

commit v5 on v4

--- a/solution.py
+++ b/solution.py
@@ -13,6 +13,7 @@
 VMEM_LIMIT = 48 * 1024 * 1024
 ROWS = 18
 CHUNKS = 8
+KEPT = 4
 
 
 def mm(a, b):
@@ -53,17 +54,31 @@
     return copies
 
 
-def strips(src, dst):
-    step = dst.shape[1] // CHUNKS
-    cuts = [pl.ds(i * step, step) for i in range(CHUNKS)]
-    return [(src.at[:, cut], dst.at[:, cut]) for cut in cuts]
-
-
-def pre_kernel(heads, x_hbm, gate_hbm, b_hbm, c_hbm, ld_hbm,
-               st_ref, dec_ref, mask_ref, mixt_ref, scores_ref, yi_ref, ec_ref, tail_ref,
-               wx_ref, silu_ref, slope_ref, x_ref, b_ref, c_ref, gate_ref, ld_ref, sems):
+def strips(src, dst, first, last):
+    step = src.shape[1] // CHUNKS
+    return [
+        (src.at[:, pl.ds(i * step, step)], dst.at[:, pl.ds((i - first) * step, step)])
+        for i in range(first, last)
+    ]
+
+
+def downward(cum_ref, h):
+    size = cum_ref.shape[1]
+    return jnp.transpose(jnp.broadcast_to(cum_ref[h:h + 1, :], (size, size)))
+
+
+def gates(gate_ref):
+    v = gate_ref[...].astype(F32)
+    g = 1.0 / (1.0 + jnp.exp(-v))
+    return v * g, g
+
+
+def pre_kernel(heads, x_hbm, b_hbm, c_hbm, ld_hbm, w_hbm,
+               st_ref, dec_ref, cum_ref, mixt_ref, scores_ref, yi_ref, wx_ref, kept_ref,
+               x_ref, b_ref, c_ref, ld_ref, sems):
     copies = fetch(
-        ((ld_hbm, ld_ref), (b_hbm, b_ref), (c_hbm, c_ref), (x_hbm, x_ref), (gate_hbm, gate_ref)), sems
+        [(ld_hbm, ld_ref), (b_hbm, b_ref), (c_hbm, c_ref), (x_hbm, x_ref)]
+        + strips(w_hbm, kept_ref, 0, KEPT), sems
     )
     size = x_ref.shape[0]
     width = x_ref.shape[1] // heads
@@ -71,6 +86,7 @@
     copies[0].wait()
     ld = jnp.concatenate([ld_ref[...], jnp.zeros((8 - heads, size), F32)], axis=0)
     cum = sum_by(ld, (row <= col).astype(BF))
+    cum_ref[...] = cum
     copies[1].wait()
     copies[2].wait()
     scores = mm_nt(c_ref[...], b_ref[...])
@@ -82,52 +98,50 @@
         across = jnp.broadcast_to(cum[h:h + 1, :], (size, size))
         down = jnp.transpose(across)
         mask = jnp.where(row >= col, jnp.exp(jnp.minimum(down - across, 0.0)), 0.0)
-        mask_ref[h] = mask
         mixing = scores * mask
         mixt_ref[h] = jnp.transpose(mixing).astype(BF)
         x = x_ref[:, at]
         yi_ref[:, at] = mm(mixing.astype(BF), x)
         last = cum[h:h + 1, size - 1:size]
-        ec_ref[:, at] = jnp.exp(down)
         tail = jnp.exp(last - down)
-        tail_ref[:, at] = tail
         wx = (x.astype(F32) * tail).astype(BF)
         wx_ref[:, at] = wx
         st_ref[:, at] = mm(b_t, wx)
         dec_ref[h] = jnp.broadcast_to(jnp.exp(last), (8, size))
-    copies[4].wait()
-    v = gate_ref[...].astype(F32)
-    g = 1.0 / (1.0 + jnp.exp(-v))
-    silu_ref[...] = v * g
-    slope_ref[...] = g + v * g * (1.0 - g)
-
-
-def mid_kernel(heads, near_ref, far_ref, w_hbm, c_hbm, silu_ref, ec_ref, st_ref, dec_ref,
-               msg_ref, dg_ref, w_ref, cot_ref, c_ref, sems):
+    for copy in copies[4:]:
+        copy.wait()
+
+
+def mid_kernel(heads, near_ref, far_ref, w_hbm, c_hbm, gate_hbm, kept_ref, cum_ref, st_ref, dec_ref,
+               msg_ref, dg_ref, w_ref, cot_ref, c_ref, gate_ref, sems):
     chips, piece = near_ref.shape[:2]
     size, full = st_ref.shape
     width = full // heads
-    chunk = w_ref.shape[1] // CHUNKS
-    copies = fetch(strips(w_hbm, w_ref) + [(c_hbm, c_ref)], sems)
+    chunk = w_hbm.shape[1] // CHUNKS
+    copies = fetch(
+        [(c_hbm, c_ref), (gate_hbm, gate_ref)] + strips(w_hbm, w_ref, KEPT, CHUNKS), sems
+    )
     core = lax.axis_index("tp") % 2
     for s in range(chips):
         at = pl.multiple_of(piece * (2 * s + core), piece)
         cot_ref[pl.ds(at, piece), :] = near_ref[s]
         at = pl.multiple_of(piece * (2 * s + 1 - core), piece)
         cot_ref[pl.ds(at, piece), :] = far_ref[s]
-    copies[CHUNKS].wait()
+    copies[0].wait()
+    copies[1].wait()
     c_t = flip(c_ref[...])
-    total = None
-    for i in range(CHUNKS):
-        copies[i].wait()
-        part = slice(i * chunk, (i + 1) * chunk)
-        term = mm_nt(cot_ref[:, part], w_ref[:, part])
-        total = term if total is None else total + term
+    silu, g = gates(gate_ref)
+    held = KEPT * chunk
+    total = mm_nt(cot_ref[:, 0:held], kept_ref[...])
+    for i in range(KEPT, CHUNKS):
+        copies[2 + i - KEPT].wait()
+        own = slice((i - KEPT) * chunk, (i - KEPT + 1) * chunk)
+        total = total + mm_nt(cot_ref[:, i * chunk:(i + 1) * chunk], w_ref[:, own])
     dg_ref[...] = total
     sub = lax.broadcasted_iota(jnp.int32, (2, size), 0)
     for h in range(heads):
         at = slice(h * width, (h + 1) * width)
-        gw = (total[:, at] * silu_ref[:, at] * ec_ref[:, at]).astype(BF)
+        gw = (total[:, at] * silu[:, at] * jnp.exp(downward(cum_ref, h))).astype(BF)
         inj = mm(c_t, gw)
         decay = dec_ref[h][0:2, :]
         hi = decay.astype(BF).astype(F32)
@@ -157,14 +171,15 @@
         adjoint = dec_ref[k] * adjoint + msg_ref[at + 8:at + 16, :].astype(F32)
 
 
-def fin_kernel(heads, piece, back_ref, x_hbm, b_hbm, c_hbm, w_hbm, dg_ref, silu_ref, slope_ref, mask_ref,
-               mixt_ref, scores_ref, yi_ref, ec_ref, tail_ref, wx_ref, dec_ref,
+def fin_kernel(heads, piece, back_ref, x_hbm, b_hbm, c_hbm, w_hbm, gate_hbm, kept_ref, dg_ref, cum_ref,
+               mixt_ref, scores_ref, yi_ref, wx_ref, dec_ref,
                mine_ref, theirs_ref, gi_ref, gg_ref, gd_ref,
-               state_ref, adj_ref, gated_ref, terms_ref, x_ref, b_ref, c_ref, w_ref, sems):
+               state_ref, adj_ref, gated_ref, terms_ref, x_ref, b_ref, c_ref, gate_ref, w_ref, sems):
     size, full = x_ref.shape
     width = full // heads
     copies = fetch(
-        [(b_hbm, b_ref), (c_hbm, c_ref), (x_hbm, x_ref)] + strips(w_hbm, w_ref), sems
+        [(b_hbm, b_ref), (c_hbm, c_ref), (gate_hbm, gate_ref), (x_hbm, x_ref)]
+        + strips(w_hbm, w_ref, KEPT, CHUNKS), sems
     )
     for a in range(size // 8):
         for h in range(heads):
@@ -179,9 +194,14 @@
     copies[1].wait()
     b = b_ref[...]
     c = c_ref[...]
-    silu = silu_ref[...]
+    copies[2].wait()
+    silu, g = gates(gate_ref)
     dg = dg_ref[...]
-    ec = ec_ref[...]
+    downs = [downward(cum_ref, h) for h in range(heads)]
+    ec = jnp.concatenate([jnp.exp(down) for down in downs], axis=1)
+    tail = jnp.concatenate(
+        [jnp.exp(cum_ref[h:h + 1, size - 1:size] - downs[h]) for h in range(heads)], axis=1
+    )
     y_inter = mm(c, state_b) * ec
     y = yi_ref[...] + y_inter
     gated = (y * silu).astype(BF)
@@ -194,12 +214,12 @@
                            pl.ds(pl.multiple_of(size // 2 * (1 - away) + piece * i, piece), piece)))
     for src, dst in places:
         gated_ref[dst, :] = gated[src, :]
-    gg_ref[...] = (dg * y * slope_ref[...]).astype(BF)
+    gg_ref[...] = (dg * y * (g + silu * (1.0 - g))).astype(BF)
     gy = dg * silu
     gy_b = gy.astype(BF)
     gw = (gy * ec).astype(BF)
-    sdx = mm(b, adj_b) * tail_ref[...]
-    copies[2].wait()
+    sdx = mm(b, adj_b) * tail
+    copies[3].wait()
     x = x_ref[...]
     through = x.astype(F32) * sdx
     entering = gy * y_inter
@@ -213,7 +233,9 @@
     product = adj * state
     for h in range(heads):
         at = slice(h * width, (h + 1) * width)
-        dmix = mm_nt(gy_b[:, at], x[:, at]) * mask_ref[h]
+        gap = downs[h] - jnp.broadcast_to(cum_ref[h:h + 1, :], (size, size))
+        mask = jnp.where(row >= col, jnp.exp(jnp.minimum(gap, 0.0)), 0.0)
+        dmix = mm_nt(gy_b[:, at], x[:, at]) * mask
         dmix_sum = dmix_sum + dmix
         cross = dmix * scores
         gi_ref[:, at] = (mm(mixt_ref[h], gy_b[:, at]) + sdx[:, at]).astype(BF)
@@ -230,7 +252,7 @@
     grad_b = mm(jnp.transpose(dmix_sum).astype(BF), c) + mm_nt(wx_ref[...], adj_b)
     grad_c = mm(dmix_sum.astype(BF), b) + mm_nt(gw, state_b)
     half = size // 2
-    out_width = w_ref.shape[1]
+    out_width = w_hbm.shape[1]
     for src, dst in places:
         terms_ref[dst, 0:n] = grad_b[src, :]
         terms_ref[dst, n:2 * n] = grad_c[src, :]
@@ -239,11 +261,14 @@
     step = out_width // CHUNKS
     gated = gated_ref[...]
     for i in range(CHUNKS):
-        copies[3 + i].wait()
-        o = i * step
-        part = mm(gated, w_ref[:, o:o + step]).astype(BF)
-        theirs_ref[:, o:o + step] = part[0:half, :]
-        mine_ref[:, o:o + step] = part[half:size, :]
+        if i == KEPT or i == (KEPT + CHUNKS) // 2:
+            for k in range(i, (KEPT + CHUNKS) // 2 if i == KEPT else CHUNKS):
+                copies[4 + k - KEPT].wait()
+        own = kept_ref if i < KEPT else w_ref
+        at = (i if i < KEPT else i - KEPT) * step
+        part = mm(gated, own[:, at:at + step]).astype(BF)
+        theirs_ref[:, i * step:(i + 1) * step] = part[0:half, :]
+        mine_ref[:, i * step:(i + 1) * step] = part[half:size, :]
 
 
 def end_kernel(part_ref, out_ref, gb_ref, gc_ref):
@@ -282,7 +307,8 @@
     wide_b = ((size, full), BF)
     square = (heads, size, size)
     small = pltpu.VMEM((size, n), BF)
-    weights = pltpu.VMEM((full, out_width), BF)
+    kept_width = out_width // CHUNKS * KEPT
+    weights = pltpu.VMEM((full, out_width - kept_width), BF)
     lanes = pltpu.VMEM((size, full), F32)
     rows = pltpu.VMEM((size, full), BF)
     across = [[2 * i + k for i in range(chips)] for k in range(2)]
@@ -293,19 +319,20 @@
         "tp", 0, 0, tiled=True, axis_index_groups=across,
     )
     far = lax.ppermute(near, "tp", swap)
-    st, dec, mask, mixt, scores, yi, ec, tail, wx, silu, slope = call(
+    st, dec, cum, mixt, scores, yi, wx, kept = call(
         functools.partial(pre_kernel, heads),
-        [((n, full), F32), ((heads, 8, size), F32), (square, F32), (square, BF), ((size, size), F32),
-         wide, wide, wide, wide_b, wide, wide],
+        [((n, full), F32), ((heads, 8, size), F32), ((8, size), F32), (square, BF), ((size, size), F32),
+         wide, wide_b, ((full, kept_width), BF)],
         5, range(5),
-        [rows, small, small, rows, pltpu.VMEM((heads, size), F32), pltpu.SemaphoreType.DMA((5,))],
-    )(inputs, gate_in, b_proj, c_proj, log_decay)
+        [rows, small, small, pltpu.VMEM((heads, size), F32), pltpu.SemaphoreType.DMA((4 + KEPT,))],
+    )(inputs, b_proj, c_proj, log_decay, w_out)
     msg, dg = call(
         functools.partial(mid_kernel, heads),
         [((workers * ROWS, size), BF), wide],
-        8, (2, 3),
-        [weights, pltpu.VMEM((size, out_width), BF), small, pltpu.SemaphoreType.DMA((CHUNKS + 1,))],
-    )(near, far, w_out, c_proj, silu, ec, st, dec)
+        9, (2, 3, 4),
+        [weights, pltpu.VMEM((size, out_width), BF), small, rows,
+         pltpu.SemaphoreType.DMA((2 + CHUNKS - KEPT,))],
+    )(near, far, w_out, c_proj, gate_in, kept, cum, st, dec)
     msg = lax.all_to_all(msg.reshape(workers, ROWS // 2, 2, size), "ctx", 0, 0, tiled=True)
     msg = msg.reshape(workers * ROWS, size)
     (back,) = call(
@@ -317,10 +344,10 @@
     mine, theirs, grad_inputs, grad_gate, grad_decay = call(
         functools.partial(fin_kernel, heads, piece),
         [half, half, wide_b, wide_b, ((heads, size), F32)],
-        16, range(1, 5),
-        [lanes, lanes, rows, pltpu.VMEM((size, 2 * n), F32), rows, small, small, weights,
-         pltpu.SemaphoreType.DMA((CHUNKS + 3,))],
-    )(back, inputs, b_proj, c_proj, w_out, dg, silu, slope, mask, mixt, scores, yi, ec, tail, wx, dec)
+        14, range(1, 6),
+        [lanes, lanes, rows, pltpu.VMEM((size, 2 * n), F32), rows, small, small, rows, weights,
+         pltpu.SemaphoreType.DMA((4 + CHUNKS - KEPT,))],
+    )(back, inputs, b_proj, c_proj, w_out, gate_in, kept, dg, cum, mixt, scores, yi, wx, dec)
     part = (mine.astype(F32) + lax.ppermute(theirs, "tp", swap).astype(F32)).astype(BF)
     part = lax.all_to_all(
         part.reshape(chips, piece, out_width + 2 * n),

time: 95 us -> 94.9 us (level)
  transfers between devices with their start and end apart: 2 -> 2, of which waited for: 2 -> 1; matrix products, arithmetic and copies ran while one was open for 0% -> 0% of each run, Pallas kernels for 1% -> 2%
where the time goes in v5:
time: 94.9 us; the launch traced here: 94.6 us
  blocking collectives  68.9 us (73%)
  starting transfers between devices  13.3 us (14%)
  Pallas kernels  8.91 us (9%)
  waiting for transfers between devices  1.56 us (2%)
  local copies, waits for them, and re-layouts  1 us (1%)
    all_to_all x1, blocking collectives, local(): lax.all_to_all(msg.reshape(workers, ROWS // 2, 2, size), 'ctx', 0, 0, til...  27.8 us
    all_to_all x1, blocking collectives, local(): back = lax.all_to_all(back, 'ctx', 0, 0, tiled=True)  17.8 us
    all_to_all x1, blocking collectives, local(): lax.all_to_all(part.reshape(chips, piece, out_width + 2 * n), 'tp', 0, 0,...  11.8 us
    all_to_all x1, blocking collectives, local(): lax.all_to_all(jnp.broadcast_to(cotangent[None], (chips, piece, out_width...  11.6 us
    ppermute x1, starting transfers between devices, local(): far = lax.ppermute(near, 'tp', swap)  7.81 us
    ppermute x1, starting transfers between devices, local(): lax.ppermute(theirs, 'tp', swap).astype(F32)  5.46 us
    pallas_call x1, Pallas kernels, local(): call(functools.partial(mid_kernel, heads), [((workers * ROWS, size), BF),...  3.14 us
    pallas_call x1, Pallas kernels, local(): call(functools.partial(fin_kernel, heads, piece), [half, half, wide_b, wi...  2.93 us
  transfers between devices with their start and end apart: 2, of which 1 were waited for; matrix products, arithmetic and copies ran while one was open for 0% of the time, Pallas kernels for 2%

profile of v5, /device:TPU:1, one launch (start us, length us, event | category | flops | bytes accessed | tf_op | source)
XLA Modules:
  0.0 94.6 jit_solution(8800186382741396770)
XLA Ops:
  0.6 0.0 copy-start.2
  0.6 0.0 copy-start.3
  0.7 0.0 copy-start.1
  0.7 0.0 copy-start.4
  0.7 1.0 %broadcast_in_dim.2 = bf16[4,16,4096]{2,1,0:T(8,128)(2,1)S(1)} broadcast(bf16[16,4096]{1,0:T(8,128)(2,1)} %param.13), dimensions={1,2} | broadcast | bytes 655360 | tf_op jit(solution)/shard_map/broadcast_in_dim | solution.py:318
  1.7 11.6 %all_to_all.20.near_ref = bf16[4,16,4096]{2,1,0:T(8,128)(2,1)S(1)} all-to-all(bf16[4,16,4096]{2,1,0:T(8,128)(2,1)S(1)} %broadcast_in_dim.2), channel_id=1, replica_groups={{0,2,4,6},{1,3,5,7},{8,10,12,14},{9,11,13,15},{16,18,20,22},{17,19,21,2..., dimensions={0} | all-to-all | bytes 1048576 | tf_op jit(solution)/shard_map/all_to_all | solution.py:317
  13.2 0.0 copy-start
  13.2 7.8 %collective-permute-start = (bf16[4,16,4096]{2,1,0:T(8,128)(2,1)S(1)}, bf16[4,16,4096]{2,1,0:T(8,128)(2,1)S(1)}, u32[]{:S(2)}, u32[]{:S(2)}) collective-permute-start(bf16[4,16,4096]{2,1,0:T(8,128)(2,1)S(1)} %all_to_all.20.near_ref), channel_id=1, source_target_pairs={{0,1},{1,0},{2,3},{3,2},{4,5},{5,4},{6,7},{7,6},{8,9},{9,8},{10,11... | collective-permute-start | bytes 1572872 | tf_op jit(solution)/shard_map/ppermute | solution.py:321
  21.1 0.0 copy-done.2
  21.1 0.0 copy-done.3
  21.1 0.0 copy-done.1
  21.1 0.0 copy-done.4
  21.1 1.9 %shard_map.118 = (f32[128,512]{1,0:T(8,128)S(1)}, f32[4,8,128]{2,1,0:T(8,128)S(1)}, f32[8,128]{1,0:T(8,128)S(1)}, bf16[4,128,128]{2,1,0:T(8,128)(2,1)S(1)}, f32[...) custom-call(bf16[128,512]{1,0:T(8,128)(2,1)S(1)} %copy-done.1, ...), custom_call_target="tpu_custom_call" | custom-call | tf_op jit(solution)/shard_map/pallas_call | solution.py:322
  23.0 0.0 collective-permute-done.far_ref
  23.0 0.0 copy-done
  23.0 3.1 %shard_map.119 = (bf16[1152,128]{1,0:T(8,128)(2,1)S(1)}, f32[128,512]{1,0:T(8,128)S(1)}) custom-call(bf16[4,16,4096]{2,1,0:T(8,128)(2,1)S(1)} %all_to_all.20.near_ref, bf16[4,16,4096]{2,1,0:T(8,128)(2,1)S(1)} %collective-permute-done.far_ref, bf16[512,4096]{1,0:T(8,128)(2,1)} %w_hbm.5, bf16[128,128]{1,0:T(8,128)(2,1)S(1)} %copy-done.2, ...), custom_call_target="tpu_custom_call" | custom-call | tf_op jit(solution)/shard_map/pallas_call | solution.py:329
  26.1 27.8 %all_to_all.21 = bf16[64,9,2,128]{3,2,1,0:T(2,128)(2,1)S(1)} all-to-all(bf16[64,9,2,128]{3,2,1,0:T(2,128)(2,1)S(1)} %bitcast.4), channel_id=1, replica_groups=mesh['ctx'=64,'tp'=8] {'ctx'}, dimensions={0} | all-to-all | bytes 589824 | tf_op jit(solution)/shard_map/all_to_all | solution.py:336
  53.9 0.3 shard_map.120
  54.2 17.8 %all_to_all.22.back_ref = bf16[64,16,128]{2,1,0:T(8,128)(2,1)S(1)} all-to-all(bf16[64,16,128]{2,1,0:T(8,128)(2,1)S(1)} %shard_map.120), channel_id=1, replica_groups=mesh['ctx'=64,'tp'=8] {'ctx'}, dimensions={0} | all-to-all | bytes 524288 | tf_op jit(solution)/shard_map/all_to_all | solution.py:342
  71.9 2.9 %shard_map.121 = (bf16[64,4352]{1,0:T(8,128)(2,1)S(1)}, bf16[64,4352]{1,0:T(8,128)(2,1)S(1)}, bf16[128,512]{1,0:T(8,128)(2,1)}, bf16[128,512]{1,0:T(8,128)(2,1)}, f32[4,128]{1,0:T(4,128)}) custom-call(bf16[64,16,128]{2,1,0:T(8,128)(2,1)S(1)} %all_to_all.22.back_ref, bf16[128,512]{1,0:T(8,128)(2,1)S(1)} %copy-done.1, bf16[128,128]{1,0:T(8,128)(2,1)S(1)} %copy-done.3, ...), custom_call_target="tpu_custom_call" | custom-call | tf_op jit(solution)/shard_map/pallas_call | solution.py:344
  74.9 5.5 %collective-permute-start.1 = (bf16[64,4352]{1,0:T(8,128)(2,1)S(1)}, bf16[64,4352]{1,0:T(8,128)(2,1)S(1)}, u32[]{:S(2)}, u32[]{:S(2)}) collective-permute-start(bf16[64,4352]{1,0:T(8,128)(2,1)S(1)} %get-tuple-element.35), channel_id=1, source_target_pairs={{0,1},{1,0},{2,3},{3,2},{4,5},{5,4},{6,7},{7,6},{8,9},{9,8},{10,11... | collective-permute-start | bytes 1671176 | tf_op jit(solution)/shard_map/ppermute | solution.py:351
  80.3 1.6 %collective-permute-done.1 = bf16[64,4352]{1,0:T(8,128)(2,1)S(1)} collective-permute-done((bf16[64,4352]{1,0:T(8,128)(2,1)S(1)}, bf16[64,4352]{1,0:T(8,128)(2,1)S(1)}, u32[]{:S(2)}, u32[]{:S(2)}) %collective-permute-start.1) | collective-permute-done | bytes 557088 | tf_op jit(solution)/shard_map/ppermute | solution.py:351
  81.9 0.1 add_convert_fusion
  82.0 11.8 %all_to_all.23.part_ref = bf16[4,16,4352]{2,1,0:T(8,128)(2,1)S(1)} all-to-all(bf16[4,16,4352]{2,1,0:T(8,128)(2,1)S(1)} %bitcast.5), channel_id=1, replica_groups={{0,2,4,6},{1,3,5,7},{8,10,12,14},{9,11,13,15},{16,18,20,22},{17,19,21,2..., dimensions={0} | all-to-all | bytes 1114112 | tf_op jit(solution)/shard_map/all_to_all | solution.py:352
  93.8 0.7 shard_map.122
Async XLA Ops:
  0.6 20.4 %copy-start.2 = (bf16[128,128]{1,0:T(8,128)(2,1)S(1)}, bf16[128,128]{1,0:T(8,128)(2,1)}, u32[]{:S(2)}) copy-start(bf16[128,128]{1,0:T(8,128)(2,1)} %c_hbm.5) | copy-start | bytes 98308
  0.6 20.4 %copy-start.3 = (bf16[128,128]{1,0:T(8,128)(2,1)S(1)}, bf16[128,128]{1,0:T(8,128)(2,1)}, u32[]{:S(2)}) copy-start(bf16[128,128]{1,0:T(8,128)(2,1)} %b_hbm.3) | copy-start | bytes 98308
  0.7 20.4 %copy-start.1 = (bf16[128,512]{1,0:T(8,128)(2,1)S(1)}, bf16[128,512]{1,0:T(8,128)(2,1)}, u32[]{:S(2)}) copy-start(bf16[128,512]{1,0:T(8,128)(2,1)} %x_hbm.3) | copy-start | bytes 393220
  0.7 20.4 %copy-start.4 = (f32[4,128]{1,0:T(4,128)S(1)}, f32[4,128]{1,0:T(4,128)}, u32[]{:S(2)}) copy-start(f32[4,128]{1,0:T(4,128)} %ld_hbm.1) | copy-start | bytes 6148
  13.2 9.7 %copy-start = (bf16[128,512]{1,0:T(8,128)(2,1)S(1)}, bf16[128,512]{1,0:T(8,128)(2,1)}, u32[]{:S(2)}) copy-start(bf16[128,512]{1,0:T(8,128)(2,1)} %gate_hbm.3) | copy-start | bytes 393220
  13.2 9.7 %collective-permute-start = (bf16[4,16,4096]{2,1,0:T(8,128)(2,1)S(1)}, bf16[4,16,4096]{2,1,0:T(8,128)(2,1)S(1)}, u32[]{:S(2)}, u32[]{:S(2)}) collective-permute-start(bf16[4,16,4096]{2,1,0:T(8,128)(2,1)S(1)} %all_to_all.20.near_ref), channel_id=1, source_target_pairs={{0,1},{1,0},{2,3},{3,2},{4,5},{5,4},{6,7},{7,6},{8,9},{9,8},{10,11... | collective-permute-start | bytes 1572872 | tf_op jit(solution)/shard_map/ppermute | solution.py:321
  74.9 7.0 %collective-permute-start.1 = (bf16[64,4352]{1,0:T(8,128)(2,1)S(1)}, bf16[64,4352]{1,0:T(8,128)(2,1)S(1)}, u32[]{:S(2)}, u32[]{:S(2)}) collective-permute-start(bf16[64,4352]{1,0:T(8,128)(2,1)S(1)} %get-tuple-element.35), channel_id=1, source_target_pairs={{0,1},{1,0},{2,3},{3,2},{4,5},{5,4},{6,7},{7,6},{8,9},{9,8},{10,11... | collective-permute-start | bytes 1671176 | tf_op jit(solution)/shard_map/ppermute | solution.py:351

commit v6 on v5

--- a/solution.py
+++ b/solution.py
@@ -131,8 +131,11 @@
     copies[1].wait()
     c_t = flip(c_ref[...])
     silu, g = gates(gate_ref)
-    held = KEPT * chunk
-    total = mm_nt(cot_ref[:, 0:held], kept_ref[...])
+    total = None
+    for i in range(KEPT):
+        own = slice(i * chunk, (i + 1) * chunk)
+        term = mm_nt(cot_ref[:, own], kept_ref[:, own])
+        total = term if total is None else total + term
     for i in range(KEPT, CHUNKS):
         copies[2 + i - KEPT].wait()
         own = slice((i - KEPT) * chunk, (i - KEPT + 1) * chunk)

time: 94.9 us -> 94.3 us (level)
  no operation moved by 1% of the time
where the time goes in v6:
time: 94.3 us; the launch traced here: 93.9 us
  blocking collectives  68.9 us (73%)
  starting transfers between devices  13.3 us (14%)
  Pallas kernels  8.25 us (9%)
  waiting for transfers between devices  1.56 us (2%)
  local copies, waits for them, and re-layouts  1 us (1%)
    all_to_all x1, blocking collectives, local(): lax.all_to_all(msg.reshape(workers, ROWS // 2, 2, size), 'ctx', 0, 0, til...  27.8 us
    all_to_all x1, blocking collectives, local(): back = lax.all_to_all(back, 'ctx', 0, 0, tiled=True)  17.8 us
    all_to_all x1, blocking collectives, local(): lax.all_to_all(part.reshape(chips, piece, out_width + 2 * n), 'tp', 0, 0,...  11.8 us
    all_to_all x1, blocking collectives, local(): lax.all_to_all(jnp.broadcast_to(cotangent[None], (chips, piece, out_width...  11.6 us
    ppermute x1, starting transfers between devices, local(): far = lax.ppermute(near, 'tp', swap)  7.81 us
    ppermute x1, starting transfers between devices, local(): lax.ppermute(theirs, 'tp', swap).astype(F32)  5.44 us
    pallas_call x1, Pallas kernels, local(): call(functools.partial(fin_kernel, heads, piece), [half, half, wide_b, wi...  2.93 us
    pallas_call x1, Pallas kernels, local(): call(functools.partial(mid_kernel, heads), [((workers * ROWS, size), BF),...  2.47 us
  transfers between devices with their start and end apart: 2, of which 1 were waited for; matrix products, arithmetic and copies ran while one was open for 0% of the time, Pallas kernels for 2%

profile of v6, /device:TPU:1, one launch (start us, length us, event | category | flops | bytes accessed | tf_op | source)
XLA Modules:
  0.0 93.9 jit_solution(5611151700264790017)
XLA Ops:
  0.6 0.0 copy-start.2
  0.6 0.0 copy-start.3
  0.7 0.0 copy-start.1
  0.7 0.0 copy-start.4
  0.7 1.0 %broadcast_in_dim.2 = bf16[4,16,4096]{2,1,0:T(8,128)(2,1)S(1)} broadcast(bf16[16,4096]{1,0:T(8,128)(2,1)} %param.13), dimensions={1,2} | broadcast | bytes 655360 | tf_op jit(solution)/shard_map/broadcast_in_dim | solution.py:321
  1.7 11.6 %all_to_all.20.near_ref = bf16[4,16,4096]{2,1,0:T(8,128)(2,1)S(1)} all-to-all(bf16[4,16,4096]{2,1,0:T(8,128)(2,1)S(1)} %broadcast_in_dim.2), channel_id=1, replica_groups={{0,2,4,6},{1,3,5,7},{8,10,12,14},{9,11,13,15},{16,18,20,22},{17,19,21,2..., dimensions={0} | all-to-all | bytes 1048576 | tf_op jit(solution)/shard_map/all_to_all | solution.py:320
  13.2 0.0 copy-start
  13.2 7.8 %collective-permute-start = (bf16[4,16,4096]{2,1,0:T(8,128)(2,1)S(1)}, bf16[4,16,4096]{2,1,0:T(8,128)(2,1)S(1)}, u32[]{:S(2)}, u32[]{:S(2)}) collective-permute-start(bf16[4,16,4096]{2,1,0:T(8,128)(2,1)S(1)} %all_to_all.20.near_ref), channel_id=1, source_target_pairs={{0,1},{1,0},{2,3},{3,2},{4,5},{5,4},{6,7},{7,6},{8,9},{9,8},{10,11... | collective-permute-start | bytes 1572872 | tf_op jit(solution)/shard_map/ppermute | solution.py:324
  21.1 0.0 copy-done.2
  21.1 0.0 copy-done.3
  21.1 0.0 copy-done.1
  21.1 0.0 copy-done.4
  21.1 1.9 %shard_map.118 = (f32[128,512]{1,0:T(8,128)S(1)}, f32[4,8,128]{2,1,0:T(8,128)S(1)}, f32[8,128]{1,0:T(8,128)S(1)}, bf16[4,128,128]{2,1,0:T(8,128)(2,1)S(1)}, f32[...) custom-call(bf16[128,512]{1,0:T(8,128)(2,1)S(1)} %copy-done.1, ...), custom_call_target="tpu_custom_call" | custom-call | tf_op jit(solution)/shard_map/pallas_call | solution.py:325
  23.0 0.0 collective-permute-done.far_ref
  23.0 0.0 copy-done
  23.0 2.5 %shard_map.119 = (bf16[1152,128]{1,0:T(8,128)(2,1)S(1)}, f32[128,512]{1,0:T(8,128)S(1)}) custom-call(bf16[4,16,4096]{2,1,0:T(8,128)(2,1)S(1)} %all_to_all.20.near_ref, bf16[4,16,4096]{2,1,0:T(8,128)(2,1)S(1)} %collective-permute-done.far_ref, bf16[512,4096]{1,0:T(8,128)(2,1)} %w_hbm.5, bf16[128,128]{1,0:T(8,128)(2,1)S(1)} %copy-done.2, ...), custom_call_target="tpu_custom_call" | custom-call | tf_op jit(solution)/shard_map/pallas_call | solution.py:332
  25.5 27.8 %all_to_all.21 = bf16[64,9,2,128]{3,2,1,0:T(2,128)(2,1)S(1)} all-to-all(bf16[64,9,2,128]{3,2,1,0:T(2,128)(2,1)S(1)} %bitcast.4), channel_id=1, replica_groups=mesh['ctx'=64,'tp'=8] {'ctx'}, dimensions={0} | all-to-all | bytes 589824 | tf_op jit(solution)/shard_map/all_to_all | solution.py:339
  53.2 0.3 shard_map.120
  53.5 17.8 %all_to_all.22.back_ref = bf16[64,16,128]{2,1,0:T(8,128)(2,1)S(1)} all-to-all(bf16[64,16,128]{2,1,0:T(8,128)(2,1)S(1)} %shard_map.120), channel_id=1, replica_groups=mesh['ctx'=64,'tp'=8] {'ctx'}, dimensions={0} | all-to-all | bytes 524288 | tf_op jit(solution)/shard_map/all_to_all | solution.py:345
  71.3 2.9 %shard_map.121 = (bf16[64,4352]{1,0:T(8,128)(2,1)S(1)}, bf16[64,4352]{1,0:T(8,128)(2,1)S(1)}, bf16[128,512]{1,0:T(8,128)(2,1)}, bf16[128,512]{1,0:T(8,128)(2,1)}, f32[4,128]{1,0:T(4,128)}) custom-call(bf16[64,16,128]{2,1,0:T(8,128)(2,1)S(1)} %all_to_all.22.back_ref, bf16[128,512]{1,0:T(8,128)(2,1)S(1)} %copy-done.1, bf16[128,128]{1,0:T(8,128)(2,1)S(1)} %copy-done.3, ...), custom_call_target="tpu_custom_call" | custom-call | tf_op jit(solution)/shard_map/pallas_call | solution.py:347
  74.2 5.4 %collective-permute-start.1 = (bf16[64,4352]{1,0:T(8,128)(2,1)S(1)}, bf16[64,4352]{1,0:T(8,128)(2,1)S(1)}, u32[]{:S(2)}, u32[]{:S(2)}) collective-permute-start(bf16[64,4352]{1,0:T(8,128)(2,1)S(1)} %get-tuple-element.35), channel_id=1, source_target_pairs={{0,1},{1,0},{2,3},{3,2},{4,5},{5,4},{6,7},{7,6},{8,9},{9,8},{10,11... | collective-permute-start | bytes 1671176 | tf_op jit(solution)/shard_map/ppermute | solution.py:354
  79.7 1.6 %collective-permute-done.1 = bf16[64,4352]{1,0:T(8,128)(2,1)S(1)} collective-permute-done((bf16[64,4352]{1,0:T(8,128)(2,1)S(1)}, bf16[64,4352]{1,0:T(8,128)(2,1)S(1)}, u32[]{:S(2)}, u32[]{:S(2)}) %collective-permute-start.1) | collective-permute-done | bytes 557088 | tf_op jit(solution)/shard_map/ppermute | solution.py:354
  81.2 0.1 add_convert_fusion
  81.4 11.8 %all_to_all.23.part_ref = bf16[4,16,4352]{2,1,0:T(8,128)(2,1)S(1)} all-to-all(bf16[4,16,4352]{2,1,0:T(8,128)(2,1)S(1)} %bitcast.5), channel_id=1, replica_groups={{0,2,4,6},{1,3,5,7},{8,10,12,14},{9,11,13,15},{16,18,20,22},{17,19,21,2..., dimensions={0} | all-to-all | bytes 1114112 | tf_op jit(solution)/shard_map/all_to_all | solution.py:355
  93.2 0.7 shard_map.122
Async XLA Ops:
  0.6 20.4 %copy-start.2 = (bf16[128,128]{1,0:T(8,128)(2,1)S(1)}, bf16[128,128]{1,0:T(8,128)(2,1)}, u32[]{:S(2)}) copy-start(bf16[128,128]{1,0:T(8,128)(2,1)} %c_hbm.5) | copy-start | bytes 98308
  0.6 20.4 %copy-start.3 = (bf16[128,128]{1,0:T(8,128)(2,1)S(1)}, bf16[128,128]{1,0:T(8,128)(2,1)}, u32[]{:S(2)}) copy-start(bf16[128,128]{1,0:T(8,128)(2,1)} %b_hbm.3) | copy-start | bytes 98308
  0.7 20.4 %copy-start.1 = (bf16[128,512]{1,0:T(8,128)(2,1)S(1)}, bf16[128,512]{1,0:T(8,128)(2,1)}, u32[]{:S(2)}) copy-start(bf16[128,512]{1,0:T(8,128)(2,1)} %x_hbm.3) | copy-start | bytes 393220
  0.7 20.4 %copy-start.4 = (f32[4,128]{1,0:T(4,128)S(1)}, f32[4,128]{1,0:T(4,128)}, u32[]{:S(2)}) copy-start(f32[4,128]{1,0:T(4,128)} %ld_hbm.1) | copy-start | bytes 6148
  13.2 9.7 %copy-start = (bf16[128,512]{1,0:T(8,128)(2,1)S(1)}, bf16[128,512]{1,0:T(8,128)(2,1)}, u32[]{:S(2)}) copy-start(bf16[128,512]{1,0:T(8,128)(2,1)} %gate_hbm.3) | copy-start | bytes 393220
  13.2 9.7 %collective-permute-start = (bf16[4,16,4096]{2,1,0:T(8,128)(2,1)S(1)}, bf16[4,16,4096]{2,1,0:T(8,128)(2,1)S(1)}, u32[]{:S(2)}, u32[]{:S(2)}) collective-permute-start(bf16[4,16,4096]{2,1,0:T(8,128)(2,1)S(1)} %all_to_all.20.near_ref), channel_id=1, source_target_pairs={{0,1},{1,0},{2,3},{3,2},{4,5},{5,4},{6,7},{7,6},{8,9},{9,8},{10,11... | collective-permute-start | bytes 1572872 | tf_op jit(solution)/shard_map/ppermute | solution.py:324
  74.2 7.0 %collective-permute-start.1 = (bf16[64,4352]{1,0:T(8,128)(2,1)S(1)}, bf16[64,4352]{1,0:T(8,128)(2,1)S(1)}, u32[]{:S(2)}, u32[]{:S(2)}) collective-permute-start(bf16[64,4352]{1,0:T(8,128)(2,1)S(1)} %get-tuple-element.35), channel_id=1, source_target_pairs={{0,1},{1,0},{2,3},{3,2},{4,5},{5,4},{6,7},{7,6},{8,9},{9,8},{10,11... | collective-permute-start | bytes 1671176 | tf_op jit(solution)/shard_map/ppermute | solution.py:354

commit v7 on v6

--- a/solution.py
+++ b/solution.py
@@ -174,40 +174,41 @@
         adjoint = dec_ref[k] * adjoint + msg_ref[at + 8:at + 16, :].astype(F32)
 
 
+def unpack(heads, back_ref, state_ref, adj_ref):
+    width = state_ref.shape[1] // heads
+    for a in range(state_ref.shape[0] // 8):
+        for h in range(heads):
+            both = back_ref[a * heads + h].astype(F32)
+            state_ref[8 * a:8 * a + 8, h * width:(h + 1) * width] = both[0:8]
+            adj_ref[8 * a:8 * a + 8, h * width:(h + 1) * width] = both[8:16]
+
+
+def mask_of(cum_ref, down, h, row, col):
+    gap = down - jnp.broadcast_to(cum_ref[h:h + 1, :], down.shape)
+    return jnp.where(row >= col, jnp.exp(jnp.minimum(gap, 0.0)), 0.0)
+
+
 def fin_kernel(heads, piece, back_ref, x_hbm, b_hbm, c_hbm, w_hbm, gate_hbm, kept_ref, dg_ref, cum_ref,
-               mixt_ref, scores_ref, yi_ref, wx_ref, dec_ref,
-               mine_ref, theirs_ref, gi_ref, gg_ref, gd_ref,
-               state_ref, adj_ref, gated_ref, terms_ref, x_ref, b_ref, c_ref, gate_ref, w_ref, sems):
+               yi_ref, wx_ref, mine_ref, theirs_ref, state_ref, adj_ref,
+               gated_ref, terms_ref, x_ref, b_ref, c_ref, gate_ref, w_ref, sems):
     size, full = x_ref.shape
     width = full // heads
     copies = fetch(
         [(b_hbm, b_ref), (c_hbm, c_ref), (gate_hbm, gate_ref), (x_hbm, x_ref)]
         + strips(w_hbm, w_ref, KEPT, CHUNKS), sems
     )
-    for a in range(size // 8):
-        for h in range(heads):
-            both = back_ref[a * heads + h].astype(F32)
-            state_ref[8 * a:8 * a + 8, h * width:(h + 1) * width] = both[0:8]
-            adj_ref[8 * a:8 * a + 8, h * width:(h + 1) * width] = both[8:16]
-    state = state_ref[...]
-    adj = adj_ref[...]
-    state_b = state.astype(BF)
-    adj_b = adj.astype(BF)
-    copies[0].wait()
-    copies[1].wait()
+    unpack(heads, back_ref, state_ref, adj_ref)
+    state_b = state_ref[...].astype(BF)
+    adj_b = adj_ref[...].astype(BF)
+    for copy in copies[0:4]:
+        copy.wait()
+    x = x_ref[...]
     b = b_ref[...]
     c = c_ref[...]
-    copies[2].wait()
     silu, g = gates(gate_ref)
-    dg = dg_ref[...]
     downs = [downward(cum_ref, h) for h in range(heads)]
     ec = jnp.concatenate([jnp.exp(down) for down in downs], axis=1)
-    tail = jnp.concatenate(
-        [jnp.exp(cum_ref[h:h + 1, size - 1:size] - downs[h]) for h in range(heads)], axis=1
-    )
-    y_inter = mm(c, state_b) * ec
-    y = yi_ref[...] + y_inter
-    gated = (y * silu).astype(BF)
+    gated = ((yi_ref[...] + mm(c, state_b) * ec) * silu).astype(BF)
     core = lax.axis_index("tp") % 2
     places = []
     for i in range(size // piece // 2):
@@ -217,40 +218,15 @@
                            pl.ds(pl.multiple_of(size // 2 * (1 - away) + piece * i, piece), piece)))
     for src, dst in places:
         gated_ref[dst, :] = gated[src, :]
-    gg_ref[...] = (dg * y * (g + silu * (1.0 - g))).astype(BF)
-    gy = dg * silu
+    gy = dg_ref[...] * silu
     gy_b = gy.astype(BF)
     gw = (gy * ec).astype(BF)
-    sdx = mm(b, adj_b) * tail
-    copies[3].wait()
-    x = x_ref[...]
-    through = x.astype(F32) * sdx
-    entering = gy * y_inter
-    scores = scores_ref[...]
     row, col = grid_of(size)
-    sub = lax.broadcasted_iota(jnp.int32, (8, size), 0)
     dmix_sum = jnp.zeros((size, size), F32)
-    columns = jnp.zeros((size, size), F32)
-    lines = jnp.zeros((8, size), F32)
-    closing = jnp.zeros((8, size), F32)
-    product = adj * state
     for h in range(heads):
         at = slice(h * width, (h + 1) * width)
-        gap = downs[h] - jnp.broadcast_to(cum_ref[h:h + 1, :], (size, size))
-        mask = jnp.where(row >= col, jnp.exp(jnp.minimum(gap, 0.0)), 0.0)
-        dmix = mm_nt(gy_b[:, at], x[:, at]) * mask
-        dmix_sum = dmix_sum + dmix
-        cross = dmix * scores
-        gi_ref[:, at] = (mm(mixt_ref[h], gy_b[:, at]) + sdx[:, at]).astype(BF)
-        down = jnp.sum(cross + entering[:, at] - through[:, at], axis=1, keepdims=True)
-        columns = jnp.where(col == h, down, columns)
-        lines = jnp.where(sub == h, jnp.sum(cross, axis=0, keepdims=True), lines)
-        end = jnp.sum(jnp.sum(through[:, at], axis=0, keepdims=True), axis=1, keepdims=True)
-        dots = jnp.sum(jnp.sum(product[:, at], axis=0, keepdims=True), axis=1, keepdims=True)
-        closing = jnp.where(sub == h, end + dec_ref[h] * dots, closing)
-    flow = jnp.transpose(columns)[0:8, :] - lines
-    total = sum_by(flow, (row >= col).astype(BF)) + closing
-    gd_ref[...] = total[0:heads, :]
+        mask = mask_of(cum_ref, downs[h], h, row, col)
+        dmix_sum = dmix_sum + mm_nt(gy_b[:, at], x[:, at]) * mask
     n = b.shape[1]
     grad_b = mm(jnp.transpose(dmix_sum).astype(BF), c) + mm_nt(wx_ref[...], adj_b)
     grad_c = mm(dmix_sum.astype(BF), b) + mm_nt(gw, state_b)
@@ -272,6 +248,55 @@
         part = mm(gated, own[:, at:at + step]).astype(BF)
         theirs_ref[:, i * step:(i + 1) * step] = part[0:half, :]
         mine_ref[:, i * step:(i + 1) * step] = part[half:size, :]
+
+
+def rest_kernel(heads, back_ref, x_hbm, b_hbm, c_hbm, gate_hbm, dg_ref, cum_ref,
+                mixt_ref, scores_ref, yi_ref, dec_ref,
+                gi_ref, gg_ref, gd_ref, state_ref, adj_ref, x_ref, b_ref, c_ref, gate_ref, sems):
+    size, full = x_ref.shape
+    width = full // heads
+    copies = fetch([(b_hbm, b_ref), (c_hbm, c_ref), (gate_hbm, gate_ref), (x_hbm, x_ref)], sems)
+    unpack(heads, back_ref, state_ref, adj_ref)
+    state = state_ref[...]
+    adj = adj_ref[...]
+    for copy in copies:
+        copy.wait()
+    x = x_ref[...]
+    silu, g = gates(gate_ref)
+    dg = dg_ref[...]
+    downs = [downward(cum_ref, h) for h in range(heads)]
+    ec = jnp.concatenate([jnp.exp(down) for down in downs], axis=1)
+    tail = jnp.concatenate(
+        [jnp.exp(cum_ref[h:h + 1, size - 1:size] - downs[h]) for h in range(heads)], axis=1
+    )
+    y_inter = mm(c_ref[...], state.astype(BF)) * ec
+    gg_ref[...] = (dg * (yi_ref[...] + y_inter) * (g + silu * (1.0 - g))).astype(BF)
+    gy = dg * silu
+    gy_b = gy.astype(BF)
+    sdx = mm(b_ref[...], adj.astype(BF)) * tail
+    through = x.astype(F32) * sdx
+    entering = gy * y_inter
+    scores = scores_ref[...]
+    row, col = grid_of(size)
+    sub = lax.broadcasted_iota(jnp.int32, (8, size), 0)
+    columns = jnp.zeros((size, size), F32)
+    lines = jnp.zeros((8, size), F32)
+    closing = jnp.zeros((8, size), F32)
+    product = adj * state
+    for h in range(heads):
+        at = slice(h * width, (h + 1) * width)
+        mask = mask_of(cum_ref, downs[h], h, row, col)
+        cross = mm_nt(gy_b[:, at], x[:, at]) * mask * scores
+        gi_ref[:, at] = (mm(mixt_ref[h], gy_b[:, at]) + sdx[:, at]).astype(BF)
+        down = jnp.sum(cross + entering[:, at] - through[:, at], axis=1, keepdims=True)
+        columns = jnp.where(col == h, down, columns)
+        lines = jnp.where(sub == h, jnp.sum(cross, axis=0, keepdims=True), lines)
+        end = jnp.sum(jnp.sum(through[:, at], axis=0, keepdims=True), axis=1, keepdims=True)
+        dots = jnp.sum(jnp.sum(product[:, at], axis=0, keepdims=True), axis=1, keepdims=True)
+        closing = jnp.where(sub == h, end + dec_ref[h] * dots, closing)
+    flow = jnp.transpose(columns)[0:8, :] - lines
+    total = sum_by(flow, (row >= col).astype(BF)) + closing
+    gd_ref[...] = total[0:heads, :]
 
 
 def end_kernel(part_ref, out_ref, gb_ref, gc_ref):
@@ -344,14 +369,21 @@
     )(msg)
     back = lax.all_to_all(back, "ctx", 0, 0, tiled=True)
     half = ((size // 2, out_width + 2 * n), BF)
-    mine, theirs, grad_inputs, grad_gate, grad_decay = call(
+    mine, theirs = call(
         functools.partial(fin_kernel, heads, piece),
-        [half, half, wide_b, wide_b, ((heads, size), F32)],
-        14, range(1, 6),
+        [half, half],
+        11, range(1, 6),
         [lanes, lanes, rows, pltpu.VMEM((size, 2 * n), F32), rows, small, small, rows, weights,
          pltpu.SemaphoreType.DMA((4 + CHUNKS - KEPT,))],
-    )(back, inputs, b_proj, c_proj, w_out, gate_in, kept, dg, cum, mixt, scores, yi, wx, dec)
-    part = (mine.astype(F32) + lax.ppermute(theirs, "tp", swap).astype(F32)).astype(BF)
+    )(back, inputs, b_proj, c_proj, w_out, gate_in, kept, dg, cum, yi, wx)
+    grad_inputs, grad_gate, grad_decay = call(
+        functools.partial(rest_kernel, heads),
+        [wide_b, wide_b, ((heads, size), F32)],
+        11, range(1, 5),
+        [lanes, lanes, rows, small, small, rows, pltpu.SemaphoreType.DMA((4,))],
+    )(back, inputs, b_proj, c_proj, gate_in, dg, cum, mixt, scores, yi, dec)
+    other, grad_inputs = lax.optimization_barrier((lax.ppermute(theirs, "tp", swap), grad_inputs))
+    part = (mine.astype(F32) + other.astype(F32)).astype(BF)
     part = lax.all_to_all(
         part.reshape(chips, piece, out_width + 2 * n),
         "tp", 0, 0, tiled=True, axis_index_groups=across,

time: 94.3 us -> 94.5 us (level)
  waiting for transfers between devices: 1.56 us -> 0.01 us
  Pallas kernels: 8.25 us -> 9.42 us
    ppermute x1, waiting for transfers between devices: 1.56 us -> 0.01 us  [local(): lax.ppermute(theirs, 'tp', swap)]
    pallas_call x1 -> x2, Pallas kernels: 2.93 us -> 4.11 us  [the longest x1 2.31 us: local(): call(functools.partial(fin_kernel, heads, piece), [half, half], 11, range...]
  transfers between devices with their start and end apart: 2 -> 2, of which waited for: 1 -> 0; matrix products, arithmetic and copies ran while one was open for 0% -> 0% of each run, Pallas kernels for 2% -> 4%
where the time goes in v7:
time: 94.5 us; the launch traced here: 94 us
  blocking collectives  69.5 us (74%)
  starting transfers between devices  13.3 us (14%)
  Pallas kernels  9.42 us (10%)
  local copies, waits for them, and re-layouts  1 us (1%)
    all_to_all x1, blocking collectives, local(): lax.all_to_all(msg.reshape(workers, ROWS // 2, 2, size), 'ctx', 0, 0, til...  27.8 us
    all_to_all x1, blocking collectives, local(): back = lax.all_to_all(back, 'ctx', 0, 0, tiled=True)  17.8 us
    all_to_all x1, blocking collectives, local(): lax.all_to_all(part.reshape(chips, piece, out_width + 2 * n), 'tp', 0, 0,...  12.3 us
    all_to_all x1, blocking collectives, local(): lax.all_to_all(jnp.broadcast_to(cotangent[None], (chips, piece, out_width...  11.6 us
    ppermute x1, starting transfers between devices, local(): far = lax.ppermute(near, 'tp', swap)  7.81 us
    ppermute x1, starting transfers between devices, local(): lax.ppermute(theirs, 'tp', swap)  5.44 us
    pallas_call x1, Pallas kernels, local(): call(functools.partial(mid_kernel, heads), [((workers * ROWS, size), BF),...  2.47 us
    pallas_call x1, Pallas kernels, local(): call(functools.partial(fin_kernel, heads, piece), [half, half], 11, range...  2.31 us
  transfers between devices with their start and end apart: 2, of which 0 were waited for; matrix products, arithmetic and copies ran while one was open for 0% of the time, Pallas kernels for 4%

profile of v7, /device:TPU:1, one launch (start us, length us, event | category | flops | bytes accessed | tf_op | source)
XLA Modules:
  0.0 94.0 jit_solution(17469812679901346591)
XLA Ops:
  0.6 0.0 copy-start.2
  0.6 0.0 copy-start.3
  0.7 0.0 copy-start.1
  0.7 0.0 copy-start.4
  0.7 1.0 %broadcast_in_dim.2 = bf16[4,16,4096]{2,1,0:T(8,128)(2,1)S(1)} broadcast(bf16[16,4096]{1,0:T(8,128)(2,1)} %param.13), dimensions={1,2} | broadcast | bytes 655360 | tf_op jit(solution)/shard_map/broadcast_in_dim | solution.py:346
  1.7 11.6 %all_to_all.20.near_ref = bf16[4,16,4096]{2,1,0:T(8,128)(2,1)S(1)} all-to-all(bf16[4,16,4096]{2,1,0:T(8,128)(2,1)S(1)} %broadcast_in_dim.2), channel_id=1, replica_groups={{0,2,4,6},{1,3,5,7},{8,10,12,14},{9,11,13,15},{16,18,20,22},{17,19,21,2..., dimensions={0} | all-to-all | bytes 1048576 | tf_op jit(solution)/shard_map/all_to_all | solution.py:345
  13.2 0.0 copy-start
  13.2 7.8 %collective-permute-start = (bf16[4,16,4096]{2,1,0:T(8,128)(2,1)S(1)}, bf16[4,16,4096]{2,1,0:T(8,128)(2,1)S(1)}, u32[]{:S(2)}, u32[]{:S(2)}) collective-permute-start(bf16[4,16,4096]{2,1,0:T(8,128)(2,1)S(1)} %all_to_all.20.near_ref), channel_id=1, source_target_pairs={{0,1},{1,0},{2,3},{3,2},{4,5},{5,4},{6,7},{7,6},{8,9},{9,8},{10,11... | collective-permute-start | bytes 1572872 | tf_op jit(solution)/shard_map/ppermute | solution.py:349
  21.1 0.0 copy-done.2
  21.1 0.0 copy-done.3
  21.1 0.0 copy-done.1
  21.1 0.0 copy-done.4
  21.1 1.9 %shard_map.118 = (f32[128,512]{1,0:T(8,128)S(1)}, f32[4,8,128]{2,1,0:T(8,128)S(1)}, f32[8,128]{1,0:T(8,128)S(1)}, bf16[4,128,128]{2,1,0:T(8,128)(2,1)S(1)}, f32[...) custom-call(bf16[128,512]{1,0:T(8,128)(2,1)S(1)} %copy-done.1, ...), custom_call_target="tpu_custom_call" | custom-call | tf_op jit(solution)/shard_map/pallas_call | solution.py:350
  23.0 0.0 collective-permute-done.far_ref
  23.0 0.0 copy-done
  23.0 2.5 %shard_map.119 = (bf16[1152,128]{1,0:T(8,128)(2,1)S(1)}, f32[128,512]{1,0:T(8,128)S(1)}) custom-call(bf16[4,16,4096]{2,1,0:T(8,128)(2,1)S(1)} %all_to_all.20.near_ref, bf16[4,16,4096]{2,1,0:T(8,128)(2,1)S(1)} %collective-permute-done.far_ref, bf16[512,4096]{1,0:T(8,128)(2,1)} %w_hbm.5, bf16[128,128]{1,0:T(8,128)(2,1)S(1)} %copy-done.2, ...), custom_call_target="tpu_custom_call" | custom-call | tf_op jit(solution)/shard_map/pallas_call | solution.py:357
  25.5 27.8 %all_to_all.21 = bf16[64,9,2,128]{3,2,1,0:T(2,128)(2,1)S(1)} all-to-all(bf16[64,9,2,128]{3,2,1,0:T(2,128)(2,1)S(1)} %bitcast.4), channel_id=1, replica_groups=mesh['ctx'=64,'tp'=8] {'ctx'}, dimensions={0} | all-to-all | bytes 589824 | tf_op jit(solution)/shard_map/all_to_all | solution.py:364
  53.2 0.3 shard_map.120
  53.5 17.8 %all_to_all.22.back_ref = bf16[64,16,128]{2,1,0:T(8,128)(2,1)S(1)} all-to-all(bf16[64,16,128]{2,1,0:T(8,128)(2,1)S(1)} %shard_map.120), channel_id=1, replica_groups=mesh['ctx'=64,'tp'=8] {'ctx'}, dimensions={0} | all-to-all | bytes 524288 | tf_op jit(solution)/shard_map/all_to_all | solution.py:370
  71.3 2.3 %shard_map.121 = (bf16[64,4352]{1,0:T(8,128)(2,1)S(1)}, bf16[64,4352]{1,0:T(8,128)(2,1)S(1)}) custom-call(bf16[64,16,128]{2,1,0:T(8,128)(2,1)S(1)} %all_to_all.22.back_ref, bf16[128,512]{1,0:T(8,128)(2,1)S(1)} %copy-done.1, bf16[128,128]{1,0:T(8,128)(2,1)S(1)} %copy-done.3, bf16[128,128]{1,0:T(8,128)(2,1)S(1)} %copy-done.2, bf16[512,4096]{1,0:T(8,128)(2,1)} %w_hbm.5, ...), custom_call_target="tpu_custom_call" | custom-call | tf_op jit(solution)/shard_map/pallas_call | solution.py:372
  73.6 5.4 %collective-permute-start.1 = (bf16[64,4352]{1,0:T(8,128)(2,1)S(1)}, bf16[64,4352]{1,0:T(8,128)(2,1)S(1)}, u32[]{:S(2)}, u32[]{:S(2)}) collective-permute-start(bf16[64,4352]{1,0:T(8,128)(2,1)S(1)} %get-tuple-element.35), channel_id=1, source_target_pairs={{0,1},{1,0},{2,3},{3,2},{4,5},{5,4},{6,7},{7,6},{8,9},{9,8},{10,11... | collective-permute-start | bytes 1671176 | tf_op jit(solution)/shard_map/ppermute | solution.py:385
  79.1 1.8 %shard_map.122 = (bf16[128,512]{1,0:T(8,128)(2,1)}, bf16[128,512]{1,0:T(8,128)(2,1)}, f32[4,128]{1,0:T(4,128)}) custom-call(bf16[64,16,128]{2,1,0:T(8,128)(2,1)S(1)} %all_to_all.22.back_ref, bf16[128,512]{1,0:T(8,128)(2,1)S(1)} %copy-done.1, bf16[128,128]{1,0:T(8,128)(2,1)S(1)} %copy-done.3, bf16[128,128]{1,0:T(8,128)(2,1)S(1)} %copy-done.2, ...), custom_call_target="tpu_custom_call" | custom-call | tf_op jit(solution)/shard_map/pallas_call | solution.py:379
  80.9 0.0 collective-permute-done.1
  80.9 0.1 add_convert_fusion
  81.0 12.3 %all_to_all.23.part_ref = bf16[4,16,4352]{2,1,0:T(8,128)(2,1)S(1)} all-to-all(bf16[4,16,4352]{2,1,0:T(8,128)(2,1)S(1)} %bitcast.5), channel_id=1, replica_groups={{0,2,4,6},{1,3,5,7},{8,10,12,14},{9,11,13,15},{16,18,20,22},{17,19,21,2..., dimensions={0} | all-to-all | bytes 1114112 | tf_op jit(solution)/shard_map/all_to_all | solution.py:387
  93.3 0.7 shard_map.123
Async XLA Ops:
  0.6 20.4 %copy-start.2 = (bf16[128,128]{1,0:T(8,128)(2,1)S(1)}, bf16[128,128]{1,0:T(8,128)(2,1)}, u32[]{:S(2)}) copy-start(bf16[128,128]{1,0:T(8,128)(2,1)} %c_hbm.7) | copy-start | bytes 98308
  0.6 20.4 %copy-start.3 = (bf16[128,128]{1,0:T(8,128)(2,1)S(1)}, bf16[128,128]{1,0:T(8,128)(2,1)}, u32[]{:S(2)}) copy-start(bf16[128,128]{1,0:T(8,128)(2,1)} %b_hbm.5) | copy-start | bytes 98308
  0.7 20.4 %copy-start.1 = (bf16[128,512]{1,0:T(8,128)(2,1)S(1)}, bf16[128,512]{1,0:T(8,128)(2,1)}, u32[]{:S(2)}) copy-start(bf16[128,512]{1,0:T(8,128)(2,1)} %x_hbm.5) | copy-start | bytes 393220
  0.7 20.4 %copy-start.4 = (f32[4,128]{1,0:T(4,128)S(1)}, f32[4,128]{1,0:T(4,128)}, u32[]{:S(2)}) copy-start(f32[4,128]{1,0:T(4,128)} %ld_hbm.1) | copy-start | bytes 6148
  13.2 9.7 %copy-start = (bf16[128,512]{1,0:T(8,128)(2,1)S(1)}, bf16[128,512]{1,0:T(8,128)(2,1)}, u32[]{:S(2)}) copy-start(bf16[128,512]{1,0:T(8,128)(2,1)} %gate_hbm.5) | copy-start | bytes 393220
  13.2 9.7 %collective-permute-start = (bf16[4,16,4096]{2,1,0:T(8,128)(2,1)S(1)}, bf16[4,16,4096]{2,1,0:T(8,128)(2,1)S(1)}, u32[]{:S(2)}, u32[]{:S(2)}) collective-permute-start(bf16[4,16,4096]{2,1,0:T(8,128)(2,1)S(1)} %all_to_all.20.near_ref), channel_id=1, source_target_pairs={{0,1},{1,0},{2,3},{3,2},{4,5},{5,4},{6,7},{7,6},{8,9},{9,8},{10,11... | collective-permute-start | bytes 1572872 | tf_op jit(solution)/shard_map/ppermute | solution.py:349
  73.6 7.3 %collective-permute-start.1 = (bf16[64,4352]{1,0:T(8,128)(2,1)S(1)}, bf16[64,4352]{1,0:T(8,128)(2,1)S(1)}, u32[]{:S(2)}, u32[]{:S(2)}) collective-permute-start(bf16[64,4352]{1,0:T(8,128)(2,1)S(1)} %get-tuple-element.35), channel_id=1, source_target_pairs={{0,1},{1,0},{2,3},{3,2},{4,5},{5,4},{6,7},{7,6},{8,9},{9,8},{10,11... | collective-permute-start | bytes 1671176 | tf_op jit(solution)/shard_map/ppermute | solution.py:385

commit v8 on v7

v8 whole, which is shorter than its diff:
```python
import functools

import jax
import jax.numpy as jnp
from jax import lax
from jax.experimental import pallas as pl
from jax.experimental.pallas import tpu as pltpu
from jax.sharding import PartitionSpec as P

BF = jnp.bfloat16
F32 = jnp.float32
NT = (((1,), (1,)), ((), ()))
VMEM_LIMIT = 48 * 1024 * 1024
ROWS = 10
CHUNKS = 8
KEPT = 4


def mm(a, b):
    return jnp.dot(a, b, preferred_element_type=F32)


def mm_nt(a, b):
    return lax.dot_general(a, b, NT, preferred_element_type=F32)


def flip(a):
    return jnp.transpose(a.astype(F32)).astype(BF)


def split(a):
    hi = a.astype(BF)
    rest = a - hi.astype(F32)
    mid = rest.astype(BF)
    return hi, mid, (rest - mid.astype(F32)).astype(BF)


def sum_by(a, ones):
    hi, mid, lo = split(a)
    return mm(hi, ones) + (mm(mid, ones) + mm(lo, ones))


def grid_of(size):
    return (
        lax.broadcasted_iota(jnp.int32, (size, size), 0),
        lax.broadcasted_iota(jnp.int32, (size, size), 1),
    )


def fetch(pairs, sems):
    copies = [pltpu.make_async_copy(src, dst, sems.at[i]) for i, (src, dst) in enumerate(pairs)]
    for copy in copies:
        copy.start()
    return copies


def strips(src, dst, first, last):
    step = src.shape[1] // CHUNKS
    return [
        (src.at[:, pl.ds(i * step, step)], dst.at[:, pl.ds((i - first) * step, step)])
        for i in range(first, last)
    ]


def downward(cum_ref, h):
    size = cum_ref.shape[1]
    return jnp.transpose(jnp.broadcast_to(cum_ref[h:h + 1, :], (size, size)))


def gates(gate_ref):
    v = gate_ref[...].astype(F32)
    g = 1.0 / (1.0 + jnp.exp(-v))
    return v * g, g


def send_kernel(heads, x_hbm, b_hbm, ld_hbm, msg_ref, cum_ref, wx_ref, dec_ref, x_ref, b_ref, ld_ref, sems):
    copies = fetch([(ld_hbm, ld_ref), (b_hbm, b_ref), (x_hbm, x_ref)], sems)
    size = x_ref.shape[0]
    width = x_ref.shape[1] // heads
    row, col = grid_of(size)
    copies[0].wait()
    ld = jnp.concatenate([ld_ref[...], jnp.zeros((8 - heads, size), F32)], axis=0)
    cum_ref[...] = sum_by(ld, (row <= col).astype(BF))
    copies[1].wait()
    b_t = flip(b_ref[...])
    copies[2].wait()
    sub = lax.broadcasted_iota(jnp.int32, (2, size), 0)
    for h in range(heads):
        at = slice(h * width, (h + 1) * width)
        last = cum_ref[h:h + 1, size - 1:size]
        wx = (x_ref[:, at].astype(F32) * jnp.exp(last - downward(cum_ref, h))).astype(BF)
        wx_ref[:, at] = wx
        state = mm(b_t, wx).astype(BF)
        decay = jnp.broadcast_to(jnp.exp(last), (8, size))
        dec_ref[h] = decay
        hi = decay[0:2, :].astype(BF).astype(F32)
        pair = jnp.where(sub == 0, hi, decay[0:2, :] - hi).astype(BF)
        for a in range(size // 8):
            j = ROWS * (a * heads + h)
            msg_ref[j:j + 8, :] = state[8 * a:8 * a + 8, :]
            msg_ref[j + 8:j + 10, :] = pair


def join_kernel(a_ref, b_ref, c_ref, d_ref, out_ref):
    piece = a_ref.shape[0]
    for i, ref in enumerate((a_ref, b_ref, c_ref, d_ref)):
        out_ref[i * piece:(i + 1) * piece, :] = ref[...]


def pre_kernel(heads, x_hbm, b_hbm, c_hbm, w_hbm, cum_ref,
               mixt_ref, scores_ref, yi_ref, kept_ref, x_ref, b_ref, c_ref, sems):
    copies = fetch(
        [(b_hbm, b_ref), (c_hbm, c_ref), (x_hbm, x_ref)] + strips(w_hbm, kept_ref, 0, KEPT), sems
    )
    size = x_ref.shape[0]
    width = x_ref.shape[1] // heads
    row, col = grid_of(size)
    for copy in copies[0:3]:
        copy.wait()
    scores = mm_nt(c_ref[...], b_ref[...])
    scores_ref[...] = scores
    for h in range(heads):
        at = slice(h * width, (h + 1) * width)
        mixing = scores * mask_of(cum_ref, downward(cum_ref, h), h, row, col)
        mixt_ref[h] = jnp.transpose(mixing).astype(BF)
        yi_ref[:, at] = mm(mixing.astype(BF), x_ref[:, at])
    for copy in copies[3:]:
        copy.wait()


def mid_kernel(heads, piece, near_ref, far_ref, w_hbm, c_hbm, gate_hbm, kept_ref, cum_ref,
               inj_ref, dg_ref, w_ref, cot_ref, c_ref, gate_ref, sems):
    chips = near_ref.shape[0] // piece
    size, full = gate_ref.shape
    width = full // heads
    chunk = w_hbm.shape[1] // CHUNKS
    copies = fetch(
        [(c_hbm, c_ref), (gate_hbm, gate_ref)] + strips(w_hbm, w_ref, KEPT, CHUNKS), sems
    )
    me = lax.axis_index("tp")
    core = me % 2
    for s in range(chips):
        src = 2 * ((me // 2 + chips - s) % chips)
        rows = slice(s * piece, (s + 1) * piece)
        cot_ref[pl.ds(pl.multiple_of(piece * (src + core), piece), piece), :] = near_ref[rows, :]
        cot_ref[pl.ds(pl.multiple_of(piece * (src + 1 - core), piece), piece), :] = far_ref[rows, :]
    copies[0].wait()
    copies[1].wait()
    c_t = flip(c_ref[...])
    silu, g = gates(gate_ref)
    total = None
    for i in range(KEPT):
        own = slice(i * chunk, (i + 1) * chunk)
        term = mm_nt(cot_ref[:, own], kept_ref[:, own])
        total = term if total is None else total + term
    for i in range(KEPT, CHUNKS):
        copies[2 + i - KEPT].wait()
        own = slice((i - KEPT) * chunk, (i - KEPT + 1) * chunk)
        total = total + mm_nt(cot_ref[:, i * chunk:(i + 1) * chunk], w_ref[:, own])
    dg_ref[...] = total
    for h in range(heads):
        at = slice(h * width, (h + 1) * width)
        gw = (total[:, at] * silu[:, at] * jnp.exp(downward(cum_ref, h))).astype(BF)
        inj_ref[:, at] = mm(c_t, gw)


def ahead_kernel(heads, msg_ref, inj_ref, out_ref, dec_ref):
    count = out_ref.shape[0]
    lanes = out_ref.shape[2]
    width = inj_ref.shape[1] // heads
    state = jnp.zeros((8, lanes), F32)
    for k in range(count):
        at = ROWS * k
        pair = msg_ref[at + 8:at + 10, :].astype(F32)
        decay = jnp.broadcast_to(jnp.sum(pair, axis=0, keepdims=True), (8, lanes))
        dec_ref[k] = decay
        a, h = k // heads, k % heads
        inj = inj_ref[8 * a:8 * a + 8, h * width:(h + 1) * width]
        out_ref[k] = jnp.concatenate([state, inj], axis=0).astype(BF)
        state = decay * state + msg_ref[at:at + 8, :].astype(F32)


def turn_kernel(heads, piece, both_ref, decays_ref, c_hbm, w_hbm, gate_hbm, kept_ref, cum_ref, yi_ref,
                mine_ref, theirs_ref, back_ref, state_ref,
                gated_ref, c_ref, gate_ref, w_ref, sems):
    size, full = yi_ref.shape
    width = full // heads
    copies = fetch([(c_hbm, c_ref), (gate_hbm, gate_ref)] + strips(w_hbm, w_ref, KEPT, CHUNKS), sems)
    adjoint = jnp.zeros((8, both_ref.shape[2]), F32)
    for k in reversed(range(both_ref.shape[0])):
        both = both_ref[k].astype(F32)
        a, h = k // heads, k % heads
        state_ref[8 * a:8 * a + 8, h * width:(h + 1) * width] = both[0:8]
        back_ref[k] = adjoint.astype(BF)
        adjoint = decays_ref[k] * adjoint + both[8:16]
    copies[0].wait()
    copies[1].wait()
    silu, g = gates(gate_ref)
    ec = jnp.concatenate([jnp.exp(downward(cum_ref, h)) for h in range(heads)], axis=1)
    state_b = state_ref[...].astype(BF)
    gated = ((yi_ref[...] + mm(c_ref[...], state_b) * ec) * silu).astype(BF)
    core = lax.axis_index("tp") % 2
    half = size // 2
    for i in range(half // piece):
        for k in range(2):
            away = jnp.where(core == k, 0, 1)
            dst = pl.ds(pl.multiple_of(half * (1 - away) + piece * i, piece), piece)
            gated_ref[dst, :] = gated[piece * (2 * i + k):piece * (2 * i + k + 1), :]
    step = w_hbm.shape[1] // CHUNKS
    gated = gated_ref[...]
    for i in range(CHUNKS):
        if i == KEPT:
            for copy in copies[2:]:
                copy.wait()
        own = kept_ref if i < KEPT else w_ref
        at = (i if i < KEPT else i - KEPT) * step
        part = mm(gated, own[:, at:at + step]).astype(BF)
        theirs_ref[:, i * step:(i + 1) * step] = part[0:half, :]
        mine_ref[:, i * step:(i + 1) * step] = part[half:size, :]


def pair_kernel(piece, mine_ref, other_ref, own_ref, one_ref, two_ref, three_ref):
    chips = mine_ref.shape[0] // piece
    chip = lax.axis_index("tp") // 2
    for s, ref in enumerate((own_ref, one_ref, two_ref, three_ref)):
        at = pl.ds(pl.multiple_of(piece * ((chip + s) % chips), piece), piece)
        ref[...] = (mine_ref[at, :].astype(F32) + other_ref[at, :].astype(F32)).astype(BF)


def total_kernel(a_ref, b_ref, c_ref, d_ref, out_ref):
    total = a_ref[...].astype(F32) + b_ref[...].astype(F32)
    out_ref[...] = (total + (c_ref[...].astype(F32) + d_ref[...].astype(F32))).astype(BF)


def unpack(heads, back_ref, adj_ref):
    width = adj_ref.shape[1] // heads
    for a in range(adj_ref.shape[0] // 8):
        for h in range(heads):
            tile = back_ref[a * heads + h].astype(F32)
            adj_ref[8 * a:8 * a + 8, h * width:(h + 1) * width] = tile


def mask_of(cum_ref, down, h, row, col):
    gap = down - jnp.broadcast_to(cum_ref[h:h + 1, :], down.shape)
    return jnp.where(row >= col, jnp.exp(jnp.minimum(gap, 0.0)), 0.0)


def fin_kernel(heads, back_ref, x_hbm, b_hbm, c_hbm, gate_hbm, dg_ref, cum_ref, wx_ref, state_ref,
               terms_ref, adj_ref, x_ref, b_ref, c_ref, gate_ref, sems):
    size, full = x_ref.shape
    width = full // heads
    copies = fetch([(b_hbm, b_ref), (c_hbm, c_ref), (gate_hbm, gate_ref), (x_hbm, x_ref)], sems)
    unpack(heads, back_ref, adj_ref)
    state_b = state_ref[...].astype(BF)
    adj_b = adj_ref[...].astype(BF)
    for copy in copies:
        copy.wait()
    x = x_ref[...]
    silu, g = gates(gate_ref)
    gy = dg_ref[...] * silu
    gy_b = gy.astype(BF)
    row, col = grid_of(size)
    dmix_sum = jnp.zeros((size, size), F32)
    ecs = []
    for h in range(heads):
        at = slice(h * width, (h + 1) * width)
        down = downward(cum_ref, h)
        ecs.append(jnp.exp(down))
        dmix_sum = dmix_sum + mm_nt(gy_b[:, at], x[:, at]) * mask_of(cum_ref, down, h, row, col)
    gw = (gy * jnp.concatenate(ecs, axis=1)).astype(BF)
    n = b_ref.shape[1]
    grad_b = mm(jnp.transpose(dmix_sum).astype(BF), c_ref[...]) + mm_nt(wx_ref[...], adj_b)
    grad_c = mm(dmix_sum.astype(BF), b_ref[...]) + mm_nt(gw, state_b)
    terms_ref[:, 0:n] = grad_b.astype(BF)
    terms_ref[:, n:2 * n] = grad_c.astype(BF)


def rest_kernel(heads, back_ref, x_hbm, b_hbm, c_hbm, gate_hbm, dg_ref, cum_ref,
                mixt_ref, scores_ref, yi_ref, dec_ref, state_ref,
                gi_ref, gg_ref, gd_ref, adj_ref, x_ref, b_ref, c_ref, gate_ref, sems):
    size, full = x_ref.shape
    width = full // heads
    copies = fetch([(b_hbm, b_ref), (c_hbm, c_ref), (gate_hbm, gate_ref), (x_hbm, x_ref)], sems)
    unpack(heads, back_ref, adj_ref)
    state = state_ref[...]
    adj = adj_ref[...]
    for copy in copies:
        copy.wait()
    x = x_ref[...]
    silu, g = gates(gate_ref)
    dg = dg_ref[...]
    downs = [downward(cum_ref, h) for h in range(heads)]
    ec = jnp.concatenate([jnp.exp(down) for down in downs], axis=1)
    tail = jnp.concatenate(
        [jnp.exp(cum_ref[h:h + 1, size - 1:size] - downs[h]) for h in range(heads)], axis=1
    )
    y_inter = mm(c_ref[...], state.astype(BF)) * ec
    gg_ref[...] = (dg * (yi_ref[...] + y_inter) * (g + silu * (1.0 - g))).astype(BF)
    gy = dg * silu
    gy_b = gy.astype(BF)
    sdx = mm(b_ref[...], adj.astype(BF)) * tail
    through = x.astype(F32) * sdx
    entering = gy * y_inter
    scores = scores_ref[...]
    row, col = grid_of(size)
    sub = lax.broadcasted_iota(jnp.int32, (8, size), 0)
    columns = jnp.zeros((size, size), F32)
    lines = jnp.zeros((8, size), F32)
    closing = jnp.zeros((8, size), F32)
    product = adj * state
    for h in range(heads):
        at = slice(h * width, (h + 1) * width)
        mask = mask_of(cum_ref, downs[h], h, row, col)
        cross = mm_nt(gy_b[:, at], x[:, at]) * mask * scores
        gi_ref[:, at] = (mm(mixt_ref[h], gy_b[:, at]) + sdx[:, at]).astype(BF)
        down = jnp.sum(cross + entering[:, at] - through[:, at], axis=1, keepdims=True)
        columns = jnp.where(col == h, down, columns)
        lines = jnp.where(sub == h, jnp.sum(cross, axis=0, keepdims=True), lines)
        end = jnp.sum(jnp.sum(through[:, at], axis=0, keepdims=True), axis=1, keepdims=True)
        dots = jnp.sum(jnp.sum(product[:, at], axis=0, keepdims=True), axis=1, keepdims=True)
        closing = jnp.where(sub == h, end + dec_ref[h] * dots, closing)
    flow = jnp.transpose(columns)[0:8, :] - lines
    total = sum_by(flow, (row >= col).astype(BF)) + closing
    gd_ref[...] = total[0:heads, :]


def end_kernel(part_ref, gb_ref, gc_ref):
    n = gb_ref.shape[1]
    total = part_ref[0].astype(F32)
    for i in range(1, part_ref.shape[0]):
        total = total + part_ref[i].astype(F32)
    gb_ref[...] = total[:, 0:n]
    gc_ref[...] = total[:, n:2 * n]


def call(kernel, outs, count, remote=(), scratch=()):
    return pl.pallas_call(
        kernel,
        out_shape=tuple(jax.ShapeDtypeStruct(s, d) for s, d in outs),
        in_specs=[
            pl.BlockSpec(memory_space=pltpu.HBM if i in remote else pltpu.VMEM)
            for i in range(count)
        ],
        scratch_shapes=list(scratch),
        compiler_params=pltpu.CompilerParams(vmem_limit_bytes=VMEM_LIMIT),
    )


def local(inputs, gate_in, b_proj, c_proj, log_decay, w_out, cotangent):
    size, full = inputs.shape
    heads = log_decay.shape[0]
    n = b_proj.shape[1]
    tp = lax.axis_size("tp")
    chips = tp // 2
    workers = lax.axis_size("ctx")
    piece, out_width = cotangent.shape
    wide = ((size, full), F32)
    wide_b = ((size, full), BF)
    square = (heads, size, size)
    small = pltpu.VMEM((size, n), BF)
    kept_width = out_width // CHUNKS * KEPT
    weights = pltpu.VMEM((full, out_width - kept_width), BF)
    lanes = pltpu.VMEM((size, full), F32)
    rows = pltpu.VMEM((size, full), BF)
    swap = [(i, i ^ 1) for i in range(tp)]
    strip_sems = pltpu.SemaphoreType.DMA((4 + CHUNKS - KEPT,))
    slab = ((piece, out_width), BF)

    def turn(s):
        return [(2 * i + k, 2 * ((i + s) % chips) + k) for i in range(chips) for k in range(2)]

    def spread(a):
        return lax.all_to_all(a, "ctx", 0, 0, tiled=True)

    pieces = [cotangent] + [lax.ppermute(cotangent, "tp", turn(s)) for s in range(1, chips)]
    msg, cum, wx, dec = call(
        functools.partial(send_kernel, heads),
        [((workers * ROWS, size), BF), ((8, size), F32), wide_b, ((heads, 8, size), F32)],
        3, range(3), [rows, small, pltpu.VMEM((heads, size), F32), strip_sems],
    )(inputs, b_proj, log_decay)
    pieces, msg = lax.optimization_barrier((pieces, msg))
    msg = spread(msg.reshape(workers, ROWS // 2, 2, size)).reshape(workers * ROWS, size)
    (near,) = call(join_kernel, [((size // 2, out_width), BF)], 4)(*pieces)
    far = lax.ppermute(near, "tp", swap)
    mixt, scores, yi, kept = call(
        functools.partial(pre_kernel, heads),
        [(square, BF), ((size, size), F32), wide, ((full, kept_width), BF)],
        5, range(4), [rows, small, small, pltpu.SemaphoreType.DMA((3 + KEPT,))],
    )(inputs, b_proj, c_proj, w_out, cum)
    inj, dg = call(
        functools.partial(mid_kernel, heads, piece),
        [((n, full), F32), wide],
        7, (2, 3, 4), [weights, pltpu.VMEM((size, out_width), BF), small, rows, strip_sems],
    )(near, far, w_out, c_proj, gate_in, kept, cum)
    both, decays = call(
        functools.partial(ahead_kernel, heads),
        [((workers, 16, size), BF), ((workers, 8, size), F32)], 2,
    )(msg, inj)
    both = spread(both)
    half = ((size // 2, out_width), BF)
    mine, theirs, back, state = call(
        functools.partial(turn_kernel, heads, piece),
        [half, half, ((workers, 8, size), BF), wide],
        8, (2, 3, 4), [rows, small, rows, weights, strip_sems],
    )(both, decays, c_proj, w_out, gate_in, kept, cum, yi)
    other = lax.ppermute(theirs, "tp", swap)
    back = spread(back)
    sums = call(functools.partial(pair_kernel, piece), [slab] * chips, 2)(mine, other)
    sums = [sums[0]] + [lax.ppermute(sums[s], "tp", turn(s)) for s in range(1, chips)]
    (layer_out,) = call(total_kernel, [slab], 4)(*sums)
    (terms,) = call(
        functools.partial(fin_kernel, heads), [((size, 2 * n), BF)],
        9, range(1, 5), [lanes, rows, small, small, rows, strip_sems],
    )(back, inputs, b_proj, c_proj, gate_in, dg, cum, wx, state)
    terms = lax.all_to_all(terms.reshape(tp, piece, 2 * n), "tp", 0, 0, tiled=True)
    grad_inputs, grad_gate, grad_decay = call(
        functools.partial(rest_kernel, heads),
        [wide_b, wide_b, ((heads, size), F32)],
        12, range(1, 5), [lanes, rows, small, small, rows, strip_sems],
    )(back, inputs, b_proj, c_proj, gate_in, dg, cum, mixt, scores, yi, dec, state)
    grad_b, grad_c = call(end_kernel, [((piece, n), F32), ((piece, n), F32)], 1)(terms)
    return (layer_out, grad_inputs, grad_gate, grad_b, grad_c, grad_decay)


def solution(mesh):
    in_specs = (
        P("ctx", "tp"),
        P("ctx", "tp"),
        P("ctx", None),
        P("ctx", None),
        P("tp", "ctx"),
        P("tp", None),
        P(("ctx", "tp"), None),
    )
    out_specs = (
        P(("ctx", "tp"), None),
        P("ctx", "tp"),
        P("ctx", "tp"),
        P(("ctx", "tp"), None),
        P(("ctx", "tp"), None),
        P("tp", "ctx"),
    )
    return jax.shard_map(local, mesh=mesh, in_specs=in_specs, out_specs=out_specs, check_vma=False)
```

time: 94.5 us -> 112 us (1.19)
  blocking collectives: 69.5 us -> 21.8 us
  starting transfers between devices: 13.3 us -> 54.9 us
  local copies, waits for them, and re-layouts: 1 us -> 11.4 us
  waiting for transfers between devices: 0.01 us -> 7.42 us
  Pallas kernels: 9.42 us -> 14.9 us
    all_to_all x4 -> x1, blocking collectives: 69.5 us -> 21.8 us  [spread(): return lax.all_to_all(a, 'ctx', 0, 0, tiled=True)]
    all_to_all x0 -> x3, starting transfers between devices: none -> 23.6 us  [the longest x2 18.6 us: spread(): return lax.all_to_all(a, 'ctx', 0, 0, tiled=True)]
    ppermute x1 -> x7, starting transfers between devices: 5.44 us -> 25.5 us  [the longest x3 12.1 us: local(): lax.ppermute(cotangent, 'tp', turn(s))]
    unnamed x10 -> x44, local copies, waits for them, and re-layouts: 0.02 us -> 11.4 us
    all_to_all x0 -> x3, waiting for transfers between devices: none -> 7.39 us  [the longest x2 5.22 us: spread(): return lax.all_to_all(a, 'ctx', 0, 0, tiled=True)]
    pallas_call x5 -> x10, Pallas kernels: 7.62 us -> 13.1 us  [the longest x1 3.49 us: local(): call(functools.partial(mid_kernel, heads, piece), [((n, full), F32), wide...]
    ppermute x1, starting transfers between devices: 7.81 us -> 5.79 us  [local(): far = lax.ppermute(near, 'tp', swap)]
  transfers between devices with their start and end apart: 2 -> 11, of which waited for: 0 -> 3; matrix products, arithmetic and copies ran while one was open for 0% -> 0% of each run, Pallas kernels for 4% -> 10%
where the time goes in v8:
time: 112 us; the launch traced here: 111 us
  starting transfers between devices  54.9 us (49%)
  blocking collectives  21.8 us (19%)
  Pallas kernels  14.9 us (13%)
  local copies, waits for them, and re-layouts  11.4 us (10%)
  waiting for transfers between devices  7.42 us (7%)
    all_to_all x1, blocking collectives, spread(): return lax.all_to_all(a, 'ctx', 0, 0, tiled=True)  21.8 us
    all_to_all x2, starting transfers between devices, spread(): return lax.all_to_all(a, 'ctx', 0, 0, tiled=True)  18.6 us
    ppermute x3, starting transfers between devices, local(): lax.ppermute(cotangent, 'tp', turn(s))  12.1 us
    unnamed x44, local copies, waits for them, and re-layouts  11.4 us
    ppermute x3, starting transfers between devices, local(): lax.ppermute(sums[s], 'tp', turn(s))  8.46 us
    ppermute x1, starting transfers between devices, local(): far = lax.ppermute(near, 'tp', swap)  5.79 us
    all_to_all x2, waiting for transfers between devices, spread(): return lax.all_to_all(a, 'ctx', 0, 0, tiled=True)  5.22 us
    all_to_all x1, starting transfers between devices, local(): lax.all_to_all(terms.reshape(tp, piece, 2 * n), 'tp', 0, 0, tiled=True)  5.04 us
  transfers between devices with their start and end apart: 11, of which 3 were waited for; matrix products, arithmetic and copies ran while one was open for 0% of the time, Pallas kernels for 10%

profile of v8, /device:TPU:1, one launch (start us, length us, event | category | flops | bytes accessed | tf_op | source)
XLA Modules:
  0.0 111.3 jit_solution(3369207600205893759)
XLA Ops:
  0.6 5.6 %collective-permute-start.1 = (bf16[16,4096]{1,0:T(8,128)(2,1)}, bf16[16,4096]{1,0:T(8,128)(2,1)S(1)}, u32[]{:S(2)}, u32[]{:S(2)}) collective-permute-start(bf16[16,4096]{1,0:T(8,128)(2,1)} %a_ref), channel_id=1, source_target_pairs={{0,4},{1,5},{2,6},{3,7},{4,0},{5,1},{6,2},{7,3},{8,12},{9,13},{10,... | collective-permute-start | bytes 393224 | tf_op jit(solution)/shard_map/ppermute | solution.py:375
  6.3 2.2 %collective-permute-start = (bf16[16,4096]{1,0:T(8,128)(2,1)}, bf16[16,4096]{1,0:T(8,128)(2,1)S(1)}, u32[]{:S(2)}, u32[]{:S(2)}) collective-permute-start(bf16[16,4096]{1,0:T(8,128)(2,1)} %a_ref), channel_id=1, source_target_pairs={{0,2},{1,3},{2,4},{3,5},{4,6},{5,7},{6,0},{7,1},{8,10},{9,11},{10,... | collective-permute-start | bytes 393224 | tf_op jit(solution)/shard_map/ppermute | solution.py:375
  8.5 4.3 %collective-permute-start.2 = (bf16[16,4096]{1,0:T(8,128)(2,1)}, bf16[16,4096]{1,0:T(8,128)(2,1)S(1)}, u32[]{:S(2)}, u32[]{:S(2)}) collective-permute-start(bf16[16,4096]{1,0:T(8,128)(2,1)} %a_ref), channel_id=1, source_target_pairs={{0,6},{1,7},{2,0},{3,1},{4,2},{5,3},{6,4},{7,5},{8,14},{9,15},{10,... | collective-permute-start | bytes 393224 | tf_op jit(solution)/shard_map/ppermute | solution.py:375
  12.8 0.0 copy-start.1
  12.8 0.9 copy-done.1
  13.7 0.8 copy-done.6
  14.4 0.7 copy-done.21
  15.1 1.5 %shard_map.118 = (bf16[640,128]{1,0:T(8,128)(2,1)}, f32[8,128]{1,0:T(8,128)S(1)}, bf16[128,512]{1,0:T(8,128)(2,1)S(1)}, f32[4,8,128]{2,1,0:T(8,128)S(1)}) custom-call(bf16[128,512]{1,0:T(8,128)(2,1)S(1)} %copy-done.1, bf16[128,128]{1,0:T(8,128)(2,1)S(1)} %copy-done.6, f32[4,128]{1,0:T(4,128)S(1)} %copy-done.21), custom_call_target="tpu_custom_call" | custom-call | tf_op jit(solution)/shard_map/pallas_call | solution.py:376
  16.6 0.0 copy-start.13
  16.7 0.6 copy-done.13
  17.3 0.0 collective-permute-done.1.c_ref
  17.3 0.0 collective-permute-done.b_ref
  17.3 0.0 copy-start.18
  17.3 0.9 copy-done.18
  18.3 5.8 %collective-permute-start.3 = (bf16[64,4096]{1,0:T(8,128)(2,1)S(1)}, bf16[64,4096]{1,0:T(8,128)(2,1)}, u32[]{:S(2)}, u32[]{:S(2)}) collective-permute-start(bf16[64,4096]{1,0:T(8,128)(2,1)S(1)} %shard_map.119.near_ref), channel_id=1, source_target_pairs={{0,1},{1,0},{2,3},{3,2},{4,5},{5,4},{6,7},{7,6},{8,9},{9,8},{10,11... | collective-permute-start | bytes 1572872 | tf_op jit(solution)/shard_map/ppermute | solution.py:384
  24.1 14.0 %all-to-all-start = ((bf16[64,5,2,128]{3,2,1,0:T(2,128)(2,1)}), bf16[64,5,2,128]{3,2,1,0:T(2,128)(2,1)S(1)}, u32[]{:S(2)}, u32[]{:S(2)}) async-start(bf16[64,5,2,128]{3,2,1,0:T(2,128)(2,1)} %bitcast), calls=%async_computation | async-start | bytes 327680 | tf_op jit(solution)/shard_map/all_to_all | solution.py:373
  38.0 0.0 copy-start.2
  38.0 0.9 copy-done.2
  38.9 0.8 copy-done.4
  39.7 0.8 copy-done.7
  40.5 1.8 %shard_map.120 = (bf16[4,128,128]{2,1,0:T(8,128)(2,1)S(1)}, f32[128,128]{1,0:T(8,128)S(1)}, f32[128,512]{1,0:T(8,128)S(1)}, bf16[512,2048]{1,0:T(8,128)(2,1)S(1)}) custom-call(bf16[128,512]{1,0:T(8,128)(2,1)S(1)} %copy-done.2, bf16[128,128]{1,0:T(8,128)(2,1)S(1)} %copy-done.7, bf16[128,128]{1,0:T(8,128)(2,1)S(1)} %copy-done.4, bf16[512,4096]{1,0:T(8,128)(2,1)} %w_hbm.5, ...), custom_call_target="tpu_custom_call" | custom-call | tf_op jit(solution)/shard_map/pallas_call | solution.py:385
  42.3 0.0 copy-start.15
  42.3 0.6 copy-done.15
  42.9 3.5 %shard_map.121 = (f32[128,512]{1,0:T(8,128)S(1)}, f32[128,512]{1,0:T(8,128)S(1)}) custom-call(bf16[64,4096]{1,0:T(8,128)(2,1)S(1)} %shard_map.119.near_ref, bf16[64,4096]{1,0:T(8,128)(2,1)} %collective-permute-done.3.far_ref, bf16[512,4096]{1,0:T(8,128)(2,1)} %w_hbm.5, bf16[128,128]{1,0:T(8,128)(2,1)S(1)} %copy-done.4, bf16[128,512]{1,0:T(8,128)(2,1)S(1)} %copy-done, ...), custom_call_target="tpu_custom_call" | custom-call | tf_op jit(solution)/shard_map/pallas_call | solution.py:390
  46.5 0.7 copy-done.11
  47.1 2.9 %all-to-all-done = bf16[64,5,2,128]{3,2,1,0:T(2,128)(2,1)S(1)} async-done(((bf16[64,5,2,128]{3,2,1,0:T(2,128)(2,1)}), bf16[64,5,2,128]{3,2,1,0:T(2,128)(2,1)S(1)}, u32[]{:S(2)}, u32[]{:S(2)}) %all-to-all-start) | async-done | bytes 163872 | tf_op jit(solution)/shard_map/all_to_all | solution.py:373
  50.1 0.9 copy-done.12
  51.0 0.1 shard_map.122
  51.2 21.8 %all_to_all.20.both_ref = bf16[64,16,128]{2,1,0:T(8,128)(2,1)S(1)} all-to-all(bf16[64,16,128]{2,1,0:T(8,128)(2,1)S(1)} %get-tuple-element.45), channel_id=1, replica_groups=mesh['ctx'=64,'tp'=8] {'ctx'}, dimensions={0} | all-to-all | bytes 524288 | tf_op jit(solution)/shard_map/all_to_all | solution.py:373
  73.0 3.0 %shard_map.123 = (bf16[64,4096]{1,0:T(8,128)(2,1)S(1)}, bf16[64,4096]{1,0:T(8,128)(2,1)}, bf16[64,8,128]{2,1,0:T(8,128)(2,1)S(1)}, f32[128,512]{1,0:T(8,128)S(1)}) custom-call(bf16[64,16,128]{2,1,0:T(8,128)(2,1)S(1)} %all_to_all.20.both_ref, f32[64,8,128]{2,1,0:T(8,128)S(1)} %get-tuple-element.46.decays_ref, bf16[128,128]{1,0:T(8,128)(2,1)S(1)} %copy-done.5, ...), custom_call_target="tpu_custom_call" | custom-call | tf_op jit(solution)/shard_map/pallas_call | solution.py:401
  76.1 0.8 copy-done.9
  76.9 4.9 %collective-permute-start.4 = (bf16[64,4096]{1,0:T(8,128)(2,1)}, bf16[64,4096]{1,0:T(8,128)(2,1)S(1)}, u32[]{:S(2)}, u32[]{:S(2)}) collective-permute-start(bf16[64,4096]{1,0:T(8,128)(2,1)} %get-tuple-element.49), channel_id=1, source_target_pairs={{0,1},{1,0},{2,3},{3,2},{4,5},{5,4},{6,7},{7,6},{8,9},{9,8},{10,11... | collective-permute-start | bytes 1572872 | tf_op jit(solution)/shard_map/ppermute | solution.py:406
  81.9 4.6 %all-to-all-start.2 = ((bf16[64,8,128]{2,1,0:T(8,128)(2,1)}), bf16[64,8,128]{2,1,0:T(8,128)(2,1)S(1)}, u32[]{:S(2)}, u32[]{:S(2)}) async-start(bf16[64,8,128]{2,1,0:T(8,128)(2,1)} %copy-done.17), calls=%async_computation.2 | async-start | bytes 262144 | tf_op jit(solution)/shard_map/all_to_all | solution.py:373
  86.5 0.0 collective-permute-done.4.other_ref
  86.5 1.0 copy-done.10
  87.5 0.1 shard_map.124
  87.7 1.9 %collective-permute-start.5 = (bf16[16,4096]{1,0:T(8,128)(2,1)S(1)}, bf16[16,4096]{1,0:T(8,128)(2,1)S(1)}, u32[]{:S(2)}, u32[]{:S(2)}) collective-permute-start(bf16[16,4096]{1,0:T(8,128)(2,1)S(1)} %get-tuple-element.51), channel_id=1, source_target_pairs={{0,2},{1,3},{2,4},{3,5},{4,6},{5,7},{6,0},{7,1},{8,10},{9,11},{10,... | collective-permute-start | bytes 393224 | tf_op jit(solution)/shard_map/ppermute | solution.py:409
  89.6 4.6 %collective-permute-start.6 = (bf16[16,4096]{1,0:T(8,128)(2,1)S(1)}, bf16[16,4096]{1,0:T(8,128)(2,1)S(1)}, u32[]{:S(2)}, u32[]{:S(2)}) collective-permute-start(bf16[16,4096]{1,0:T(8,128)(2,1)S(1)} %get-tuple-element.52), channel_id=1, source_target_pairs={{0,4},{1,5},{2,6},{3,7},{4,0},{5,1},{6,2},{7,3},{8,12},{9,13},{10,... | collective-permute-start | bytes 393224 | tf_op jit(solution)/shard_map/ppermute | solution.py:409
  94.2 1.9 %collective-permute-start.7 = (bf16[16,4096]{1,0:T(8,128)(2,1)S(1)}, bf16[16,4096]{1,0:T(8,128)(2,1)S(1)}, u32[]{:S(2)}, u32[]{:S(2)}) collective-permute-start(bf16[16,4096]{1,0:T(8,128)(2,1)S(1)} %get-tuple-element.53), channel_id=1, source_target_pairs={{0,6},{1,7},{2,0},{3,1},{4,2},{5,3},{6,4},{7,5},{8,14},{9,15},{10,... | collective-permute-start | bytes 393224 | tf_op jit(solution)/shard_map/ppermute | solution.py:409
  96.1 2.3 %all-to-all-done.2.back_ref = bf16[64,8,128]{2,1,0:T(8,128)(2,1)S(1)} async-done(((bf16[64,8,128]{2,1,0:T(8,128)(2,1)}), bf16[64,8,128]{2,1,0:T(8,128)(2,1)S(1)}, u32[]{:S(2)}, u32[]{:S(2)}) %all-to-all-start.2) | async-done | bytes 131104 | tf_op jit(solution)/shard_map/all_to_all | solution.py:373
  98.4 1.6 %shard_map.127 = bf16[128,256]{1,0:T(8,128)(2,1)} custom-call(bf16[64,8,128]{2,1,0:T(8,128)(2,1)S(1)} %all-to-all-done.2.back_ref, bf16[128,512]{1,0:T(8,128)(2,1)S(1)} %copy-done.3, bf16[128,128]{1,0:T(8,128)(2,1)S(1)} %copy-done.8, bf16[128,128]{1,0:T(8,128)(2,1)S(1)} %copy-done.5, bf16[128,512]{1,0:T(8,128)(2,1)S(1)} %copy-done, ...), custom_call_target="tpu_custom_call" | custom-call | tf_op jit(solution)/shard_map/pallas_call | solution.py:411
  100.1 5.0 %all-to-all-start.3 = ((bf16[8,16,256]{2,1,0:T(8,128)(2,1)}), bf16[8,16,256]{2,1,0:T(8,128)(2,1)S(1)}, u32[]{:S(2)}, u32[]{:S(2)}) async-start(bf16[8,16,256]{2,1,0:T(8,128)(2,1)} %bitcast.2), calls=%async_computation.3 | async-start | bytes 131072 | tf_op jit(solution)/shard_map/all_to_all | solution.py:415
  105.1 0.9 copy-done.16
  106.0 1.8 %shard_map.126 = (bf16[128,512]{1,0:T(8,128)(2,1)}, bf16[128,512]{1,0:T(8,128)(2,1)}, f32[4,128]{1,0:T(4,128)}) custom-call(bf16[64,8,128]{2,1,0:T(8,128)(2,1)S(1)} %all-to-all-done.2.back_ref, bf16[128,512]{1,0:T(8,128)(2,1)S(1)} %copy-done.3, bf16[128,128]{1,0:T(8,128)(2,1)S(1)} %copy-done.8, bf16[128,128]{1,0:T(8,128)(2,1)S(1)} %copy-done.5, ...), custom_call_target="tpu_custom_call" | custom-call | tf_op jit(solution)/shard_map/pallas_call | solution.py:416
  107.8 2.2 %all-to-all-done.3.part_ref = bf16[8,16,256]{2,1,0:T(8,128)(2,1)S(1)} async-done(((bf16[8,16,256]{2,1,0:T(8,128)(2,1)}), bf16[8,16,256]{2,1,0:T(8,128)(2,1)S(1)}, u32[]{:S(2)}, u32[]{:S(2)}) %all-to-all-start.3) | async-done | bytes 65568 | tf_op jit(solution)/shard_map/all_to_all | solution.py:415
  110.0 0.6 shard_map.128
  110.6 0.0 collective-permute-done.5.b_ref
  110.6 0.7 shard_map.125
  (30 shorter events, 0.1 us)
Async XLA Ops:
  0.6 42.3 %copy-start = (bf16[128,512]{1,0:T(8,128)(2,1)S(1)}, bf16[128,512]{1,0:T(8,128)(2,1)}, u32[]{:S(2)}) copy-start(bf16[128,512]{1,0:T(8,128)(2,1)} %gate_hbm.7) | copy-start | bytes 393220
  0.6 16.7 %collective-permute-start.1 = (bf16[16,4096]{1,0:T(8,128)(2,1)}, bf16[16,4096]{1,0:T(8,128)(2,1)S(1)}, u32[]{:S(2)}, u32[]{:S(2)}) collective-permute-start(bf16[16,4096]{1,0:T(8,128)(2,1)} %a_ref), channel_id=1, source_target_pairs={{0,4},{1,5},{2,6},{3,7},{4,0},{5,1},{6,2},{7,3},{8,12},{9,13},{10,... | collective-permute-start | bytes 393224 | tf_op jit(solution)/shard_map/ppermute | solution.py:375
  6.3 11.0 %collective-permute-start = (bf16[16,4096]{1,0:T(8,128)(2,1)}, bf16[16,4096]{1,0:T(8,128)(2,1)S(1)}, u32[]{:S(2)}, u32[]{:S(2)}) collective-permute-start(bf16[16,4096]{1,0:T(8,128)(2,1)} %a_ref), channel_id=1, source_target_pairs={{0,2},{1,3},{2,4},{3,5},{4,6},{5,7},{6,0},{7,1},{8,10},{9,11},{10,... | collective-permute-start | bytes 393224 | tf_op jit(solution)/shard_map/ppermute | solution.py:375
  8.5 8.8 %collective-permute-start.2 = (bf16[16,4096]{1,0:T(8,128)(2,1)}, bf16[16,4096]{1,0:T(8,128)(2,1)S(1)}, u32[]{:S(2)}, u32[]{:S(2)}) collective-permute-start(bf16[16,4096]{1,0:T(8,128)(2,1)} %a_ref), channel_id=1, source_target_pairs={{0,6},{1,7},{2,0},{3,1},{4,2},{5,3},{6,4},{7,5},{8,14},{9,15},{10,... | collective-permute-start | bytes 393224 | tf_op jit(solution)/shard_map/ppermute | solution.py:375
  12.8 0.9 copy-start.1
  13.7 0.8 copy-start.6
  14.4 0.7 copy-start.21
  16.6 0.7 copy-start.13
  17.3 1.0 copy-start.19
  17.3 0.9 copy-start.18
  18.3 24.7 %collective-permute-start.3 = (bf16[64,4096]{1,0:T(8,128)(2,1)S(1)}, bf16[64,4096]{1,0:T(8,128)(2,1)}, u32[]{:S(2)}, u32[]{:S(2)}) collective-permute-start(bf16[64,4096]{1,0:T(8,128)(2,1)S(1)} %shard_map.119.near_ref), channel_id=1, source_target_pairs={{0,1},{1,0},{2,3},{3,2},{4,5},{5,4},{6,7},{7,6},{8,9},{9,8},{10,11... | collective-permute-start | bytes 1572872 | tf_op jit(solution)/shard_map/ppermute | solution.py:384
  24.1 26.0 %all-to-all-start = ((bf16[64,5,2,128]{3,2,1,0:T(2,128)(2,1)}), bf16[64,5,2,128]{3,2,1,0:T(2,128)(2,1)S(1)}, u32[]{:S(2)}, u32[]{:S(2)}) async-start(bf16[64,5,2,128]{3,2,1,0:T(2,128)(2,1)} %bitcast), calls=%async_computation | async-start | bytes 327680 | tf_op jit(solution)/shard_map/all_to_all | solution.py:373
  38.0 0.9 copy-start.2
  38.9 0.8 copy-start.4
  39.7 0.8 copy-start.7
  42.3 0.7 copy-start.15
  42.9 30.1 %copy-start.5 = (bf16[128,128]{1,0:T(8,128)(2,1)S(1)}, bf16[128,128]{1,0:T(8,128)(2,1)}, u32[]{:S(2)}) copy-start(bf16[128,128]{1,0:T(8,128)(2,1)} %c_hbm.9) | copy-start | bytes 98308
  46.4 0.7 copy-start.11
  50.1 1.0 copy-start.12
  73.0 25.4 %copy-start.3 = (bf16[128,512]{1,0:T(8,128)(2,1)S(1)}, bf16[128,512]{1,0:T(8,128)(2,1)}, u32[]{:S(2)}) copy-start(bf16[128,512]{1,0:T(8,128)(2,1)} %x_hbm.7) | copy-start | bytes 393220
  73.0 25.4 %copy-start.8 = (bf16[128,128]{1,0:T(8,128)(2,1)S(1)}, bf16[128,128]{1,0:T(8,128)(2,1)}, u32[]{:S(2)}) copy-start(bf16[128,128]{1,0:T(8,128)(2,1)} %b_hbm.7) | copy-start | bytes 98308
  73.0 25.4 %copy-start.14 = (bf16[128,512]{1,0:T(8,128)(2,1)S(1)}, bf16[128,512]{1,0:T(8,128)(2,1)}, u32[]{:S(2)}) copy-start(bf16[128,512]{1,0:T(8,128)(2,1)} %copy-done.13) | copy-start | bytes 393220
  73.0 32.1 %copy-start.20 = (f32[4,8,128]{2,1,0:T(8,128)S(1)}, f32[4,8,128]{2,1,0:T(8,128)}, u32[]{:S(2)}) copy-start(f32[4,8,128]{2,1,0:T(8,128)} %copy-done.19) | copy-start | bytes 49156
  76.1 0.8 copy-start.9
  76.9 4.9 %copy-start.17 = (bf16[64,8,128]{2,1,0:T(8,128)(2,1)}, bf16[64,8,128]{2,1,0:T(8,128)(2,1)S(1)}, u32[]{:S(2)}) copy-start(bf16[64,8,128]{2,1,0:T(8,128)(2,1)S(1)} %get-tuple-element.54) | copy-start | bytes 393220
  76.9 9.6 %collective-permute-start.4 = (bf16[64,4096]{1,0:T(8,128)(2,1)}, bf16[64,4096]{1,0:T(8,128)(2,1)S(1)}, u32[]{:S(2)}, u32[]{:S(2)}) collective-permute-start(bf16[64,4096]{1,0:T(8,128)(2,1)} %get-tuple-element.49), channel_id=1, source_target_pairs={{0,1},{1,0},{2,3},{3,2},{4,5},{5,4},{6,7},{7,6},{8,9},{9,8},{10,11... | collective-permute-start | bytes 1572872 | tf_op jit(solution)/shard_map/ppermute | solution.py:406
  81.9 16.6 %all-to-all-start.2 = ((bf16[64,8,128]{2,1,0:T(8,128)(2,1)}), bf16[64,8,128]{2,1,0:T(8,128)(2,1)S(1)}, u32[]{:S(2)}, u32[]{:S(2)}) async-start(bf16[64,8,128]{2,1,0:T(8,128)(2,1)} %copy-done.17), calls=%async_computation.2 | async-start | bytes 262144 | tf_op jit(solution)/shard_map/all_to_all | solution.py:373
  86.5 1.0 copy-start.10
  87.7 22.9 %collective-permute-start.5 = (bf16[16,4096]{1,0:T(8,128)(2,1)S(1)}, bf16[16,4096]{1,0:T(8,128)(2,1)S(1)}, u32[]{:S(2)}, u32[]{:S(2)}) collective-permute-start(bf16[16,4096]{1,0:T(8,128)(2,1)S(1)} %get-tuple-element.51), channel_id=1, source_target_pairs={{0,2},{1,3},{2,4},{3,5},{4,6},{5,7},{6,0},{7,1},{8,10},{9,11},{10,... | collective-permute-start | bytes 393224 | tf_op jit(solution)/shard_map/ppermute | solution.py:409
  89.6 21.0 %collective-permute-start.6 = (bf16[16,4096]{1,0:T(8,128)(2,1)S(1)}, bf16[16,4096]{1,0:T(8,128)(2,1)S(1)}, u32[]{:S(2)}, u32[]{:S(2)}) collective-permute-start(bf16[16,4096]{1,0:T(8,128)(2,1)S(1)} %get-tuple-element.52), channel_id=1, source_target_pairs={{0,4},{1,5},{2,6},{3,7},{4,0},{5,1},{6,2},{7,3},{8,12},{9,13},{10,... | collective-permute-start | bytes 393224 | tf_op jit(solution)/shard_map/ppermute | solution.py:409
  94.2 16.4 %collective-permute-start.7 = (bf16[16,4096]{1,0:T(8,128)(2,1)S(1)}, bf16[16,4096]{1,0:T(8,128)(2,1)S(1)}, u32[]{:S(2)}, u32[]{:S(2)}) collective-permute-start(bf16[16,4096]{1,0:T(8,128)(2,1)S(1)} %get-tuple-element.53), channel_id=1, source_target_pairs={{0,6},{1,7},{2,0},{3,1},{4,2},{5,3},{6,4},{7,5},{8,14},{9,15},{10,... | collective-permute-start | bytes 393224 | tf_op jit(solution)/shard_map/ppermute | solution.py:409
  100.1 9.9 %all-to-all-start.3 = ((bf16[8,16,256]{2,1,0:T(8,128)(2,1)}), bf16[8,16,256]{2,1,0:T(8,128)(2,1)S(1)}, u32[]{:S(2)}, u32[]{:S(2)}) async-start(bf16[8,16,256]{2,1,0:T(8,128)(2,1)} %bitcast.2), calls=%async_computation.3 | async-start | bytes 131072 | tf_op jit(solution)/shard_map/all_to_all | solution.py:415
  105.1 0.9 copy-start.16

commit v9 on v7

--- a/solution.py
+++ b/solution.py
@@ -13,7 +13,7 @@
 VMEM_LIMIT = 48 * 1024 * 1024
 ROWS = 18
 CHUNKS = 8
-KEPT = 4
+KEPT = 5
 
 
 def mm(a, b):

time: 94.5 us -> 93.9 us (level)
  no operation moved by 1% of the time
where the time goes in v9:
time: 93.9 us; the launch traced here: 93.5 us
  blocking collectives  69.1 us (74%)
  starting transfers between devices  13.3 us (14%)
  Pallas kernels  9.19 us (10%)
  local copies, waits for them, and re-layouts  1 us (1%)
    all_to_all x1, blocking collectives, local(): lax.all_to_all(msg.reshape(workers, ROWS // 2, 2, size), 'ctx', 0, 0, til...  27.8 us
    all_to_all x1, blocking collectives, local(): back = lax.all_to_all(back, 'ctx', 0, 0, tiled=True)  17.8 us
    all_to_all x1, blocking collectives, local(): lax.all_to_all(part.reshape(chips, piece, out_width + 2 * n), 'tp', 0, 0,...  11.9 us
    all_to_all x1, blocking collectives, local(): lax.all_to_all(jnp.broadcast_to(cotangent[None], (chips, piece, out_width...  11.6 us
    ppermute x1, starting transfers between devices, local(): far = lax.ppermute(near, 'tp', swap)  7.81 us
    ppermute x1, starting transfers between devices, local(): lax.ppermute(theirs, 'tp', swap)  5.45 us
    pallas_call x1, Pallas kernels, local(): call(functools.partial(mid_kernel, heads), [((workers * ROWS, size), BF),...  2.25 us
    pallas_call x1, Pallas kernels, local(): call(functools.partial(fin_kernel, heads, piece), [half, half], 11, range...  2.13 us
  transfers between devices with their start and end apart: 2, of which 0 were waited for; matrix products, arithmetic and copies ran while one was open for 0% of the time, Pallas kernels for 4%

profile of v9, /device:TPU:1, one launch (start us, length us, event | category | flops | bytes accessed | tf_op | source)
XLA Modules:
  0.0 93.5 jit_solution(4299245748584615796)
XLA Ops:
  0.6 0.0 copy-start.2
  0.6 0.0 copy-start.3
  0.7 0.0 copy-start.1
  0.7 0.0 copy-start.4
  0.7 1.0 %broadcast_in_dim.2 = bf16[4,16,4096]{2,1,0:T(8,128)(2,1)S(1)} broadcast(bf16[16,4096]{1,0:T(8,128)(2,1)} %param.13), dimensions={1,2} | broadcast | bytes 655360 | tf_op jit(solution)/shard_map/broadcast_in_dim | solution.py:346
  1.7 11.6 %all_to_all.20.near_ref = bf16[4,16,4096]{2,1,0:T(8,128)(2,1)S(1)} all-to-all(bf16[4,16,4096]{2,1,0:T(8,128)(2,1)S(1)} %broadcast_in_dim.2), channel_id=1, replica_groups={{0,2,4,6},{1,3,5,7},{8,10,12,14},{9,11,13,15},{16,18,20,22},{17,19,21,2..., dimensions={0} | all-to-all | bytes 1048576 | tf_op jit(solution)/shard_map/all_to_all | solution.py:345
  13.2 0.0 copy-start
  13.2 7.8 %collective-permute-start = (bf16[4,16,4096]{2,1,0:T(8,128)(2,1)S(1)}, bf16[4,16,4096]{2,1,0:T(8,128)(2,1)S(1)}, u32[]{:S(2)}, u32[]{:S(2)}) collective-permute-start(bf16[4,16,4096]{2,1,0:T(8,128)(2,1)S(1)} %all_to_all.20.near_ref), channel_id=1, source_target_pairs={{0,1},{1,0},{2,3},{3,2},{4,5},{5,4},{6,7},{7,6},{8,9},{9,8},{10,11... | collective-permute-start | bytes 1572872 | tf_op jit(solution)/shard_map/ppermute | solution.py:349
  21.1 0.0 copy-done.2
  21.1 0.0 copy-done.3
  21.1 0.0 copy-done.1
  21.1 0.0 copy-done.4
  21.1 2.0 %shard_map.118 = (f32[128,512]{1,0:T(8,128)S(1)}, f32[4,8,128]{2,1,0:T(8,128)S(1)}, f32[8,128]{1,0:T(8,128)S(1)}, bf16[4,128,128]{2,1,0:T(8,128)(2,1)S(1)}, f32[...) custom-call(bf16[128,512]{1,0:T(8,128)(2,1)S(1)} %copy-done.1, ...), custom_call_target="tpu_custom_call" | custom-call | tf_op jit(solution)/shard_map/pallas_call | solution.py:350
  23.1 0.0 collective-permute-done.far_ref
  23.1 0.0 copy-done
  23.1 2.2 %shard_map.119 = (bf16[1152,128]{1,0:T(8,128)(2,1)S(1)}, f32[128,512]{1,0:T(8,128)S(1)}) custom-call(bf16[4,16,4096]{2,1,0:T(8,128)(2,1)S(1)} %all_to_all.20.near_ref, bf16[4,16,4096]{2,1,0:T(8,128)(2,1)S(1)} %collective-permute-done.far_ref, bf16[512,4096]{1,0:T(8,128)(2,1)} %w_hbm.5, bf16[128,128]{1,0:T(8,128)(2,1)S(1)} %copy-done.2, ...), custom_call_target="tpu_custom_call" | custom-call | tf_op jit(solution)/shard_map/pallas_call | solution.py:357
  25.4 27.8 %all_to_all.21 = bf16[64,9,2,128]{3,2,1,0:T(2,128)(2,1)S(1)} all-to-all(bf16[64,9,2,128]{3,2,1,0:T(2,128)(2,1)S(1)} %bitcast.4), channel_id=1, replica_groups=mesh['ctx'=64,'tp'=8] {'ctx'}, dimensions={0} | all-to-all | bytes 589824 | tf_op jit(solution)/shard_map/all_to_all | solution.py:364
  53.2 0.3 shard_map.120
  53.5 17.8 %all_to_all.22.back_ref = bf16[64,16,128]{2,1,0:T(8,128)(2,1)S(1)} all-to-all(bf16[64,16,128]{2,1,0:T(8,128)(2,1)S(1)} %shard_map.120), channel_id=1, replica_groups=mesh['ctx'=64,'tp'=8] {'ctx'}, dimensions={0} | all-to-all | bytes 524288 | tf_op jit(solution)/shard_map/all_to_all | solution.py:370
  71.2 2.1 %shard_map.121 = (bf16[64,4352]{1,0:T(8,128)(2,1)S(1)}, bf16[64,4352]{1,0:T(8,128)(2,1)S(1)}) custom-call(bf16[64,16,128]{2,1,0:T(8,128)(2,1)S(1)} %all_to_all.22.back_ref, bf16[128,512]{1,0:T(8,128)(2,1)S(1)} %copy-done.1, bf16[128,128]{1,0:T(8,128)(2,1)S(1)} %copy-done.3, bf16[128,128]{1,0:T(8,128)(2,1)S(1)} %copy-done.2, bf16[512,4096]{1,0:T(8,128)(2,1)} %w_hbm.5, ...), custom_call_target="tpu_custom_call" | custom-call | tf_op jit(solution)/shard_map/pallas_call | solution.py:372
  73.4 5.4 %collective-permute-start.1 = (bf16[64,4352]{1,0:T(8,128)(2,1)S(1)}, bf16[64,4352]{1,0:T(8,128)(2,1)S(1)}, u32[]{:S(2)}, u32[]{:S(2)}) collective-permute-start(bf16[64,4352]{1,0:T(8,128)(2,1)S(1)} %get-tuple-element.35), channel_id=1, source_target_pairs={{0,1},{1,0},{2,3},{3,2},{4,5},{5,4},{6,7},{7,6},{8,9},{9,8},{10,11... | collective-permute-start | bytes 1671176 | tf_op jit(solution)/shard_map/ppermute | solution.py:385
  78.8 1.8 %shard_map.122 = (bf16[128,512]{1,0:T(8,128)(2,1)}, bf16[128,512]{1,0:T(8,128)(2,1)}, f32[4,128]{1,0:T(4,128)}) custom-call(bf16[64,16,128]{2,1,0:T(8,128)(2,1)S(1)} %all_to_all.22.back_ref, bf16[128,512]{1,0:T(8,128)(2,1)S(1)} %copy-done.1, bf16[128,128]{1,0:T(8,128)(2,1)S(1)} %copy-done.3, bf16[128,128]{1,0:T(8,128)(2,1)S(1)} %copy-done.2, ...), custom_call_target="tpu_custom_call" | custom-call | tf_op jit(solution)/shard_map/pallas_call | solution.py:379
  80.7 0.0 collective-permute-done.1
  80.7 0.1 add_convert_fusion
  80.8 11.9 %all_to_all.23.part_ref = bf16[4,16,4352]{2,1,0:T(8,128)(2,1)S(1)} all-to-all(bf16[4,16,4352]{2,1,0:T(8,128)(2,1)S(1)} %bitcast.5), channel_id=1, replica_groups={{0,2,4,6},{1,3,5,7},{8,10,12,14},{9,11,13,15},{16,18,20,22},{17,19,21,2..., dimensions={0} | all-to-all | bytes 1114112 | tf_op jit(solution)/shard_map/all_to_all | solution.py:387
  92.7 0.7 shard_map.123
Async XLA Ops:
  0.6 20.4 %copy-start.2 = (bf16[128,128]{1,0:T(8,128)(2,1)S(1)}, bf16[128,128]{1,0:T(8,128)(2,1)}, u32[]{:S(2)}) copy-start(bf16[128,128]{1,0:T(8,128)(2,1)} %c_hbm.7) | copy-start | bytes 98308
  0.6 20.4 %copy-start.3 = (bf16[128,128]{1,0:T(8,128)(2,1)S(1)}, bf16[128,128]{1,0:T(8,128)(2,1)}, u32[]{:S(2)}) copy-start(bf16[128,128]{1,0:T(8,128)(2,1)} %b_hbm.5) | copy-start | bytes 98308
  0.7 20.4 %copy-start.1 = (bf16[128,512]{1,0:T(8,128)(2,1)S(1)}, bf16[128,512]{1,0:T(8,128)(2,1)}, u32[]{:S(2)}) copy-start(bf16[128,512]{1,0:T(8,128)(2,1)} %x_hbm.5) | copy-start | bytes 393220
  0.7 20.4 %copy-start.4 = (f32[4,128]{1,0:T(4,128)S(1)}, f32[4,128]{1,0:T(4,128)}, u32[]{:S(2)}) copy-start(f32[4,128]{1,0:T(4,128)} %ld_hbm.1) | copy-start | bytes 6148
  13.2 9.9 %copy-start = (bf16[128,512]{1,0:T(8,128)(2,1)S(1)}, bf16[128,512]{1,0:T(8,128)(2,1)}, u32[]{:S(2)}) copy-start(bf16[128,512]{1,0:T(8,128)(2,1)} %gate_hbm.5) | copy-start | bytes 393220
  13.2 9.9 %collective-permute-start = (bf16[4,16,4096]{2,1,0:T(8,128)(2,1)S(1)}, bf16[4,16,4096]{2,1,0:T(8,128)(2,1)S(1)}, u32[]{:S(2)}, u32[]{:S(2)}) collective-permute-start(bf16[4,16,4096]{2,1,0:T(8,128)(2,1)S(1)} %all_to_all.20.near_ref), channel_id=1, source_target_pairs={{0,1},{1,0},{2,3},{3,2},{4,5},{5,4},{6,7},{7,6},{8,9},{9,8},{10,11... | collective-permute-start | bytes 1572872 | tf_op jit(solution)/shard_map/ppermute | solution.py:349
  73.4 7.3 %collective-permute-start.1 = (bf16[64,4352]{1,0:T(8,128)(2,1)S(1)}, bf16[64,4352]{1,0:T(8,128)(2,1)S(1)}, u32[]{:S(2)}, u32[]{:S(2)}) collective-permute-start(bf16[64,4352]{1,0:T(8,128)(2,1)S(1)} %get-tuple-element.35), channel_id=1, source_target_pairs={{0,1},{1,0},{2,3},{3,2},{4,5},{5,4},{6,7},{7,6},{8,9},{9,8},{10,11... | collective-permute-start | bytes 1671176 | tf_op jit(solution)/shard_map/ppermute | solution.py:385

commit v10 on v9

--- a/solution.py
+++ b/solution.py
@@ -13,7 +13,7 @@
 VMEM_LIMIT = 48 * 1024 * 1024
 ROWS = 18
 CHUNKS = 8
-KEPT = 5
+KEPT = 6
 
 
 def mm(a, b):

time: 93.9 us -> 94.1 us (level)
  no operation moved by 1% of the time
where the time goes in v10:
time: 94.1 us; the launch traced here: 93.7 us
  blocking collectives  69.5 us (74%)
  starting transfers between devices  13.3 us (14%)
  Pallas kernels  9.07 us (10%)
  local copies, waits for them, and re-layouts  1 us (1%)
    all_to_all x1, blocking collectives, local(): lax.all_to_all(msg.reshape(workers, ROWS // 2, 2, size), 'ctx', 0, 0, til...  27.8 us
    all_to_all x1, blocking collectives, local(): back = lax.all_to_all(back, 'ctx', 0, 0, tiled=True)  17.8 us
    all_to_all x1, blocking collectives, local(): lax.all_to_all(part.reshape(chips, piece, out_width + 2 * n), 'tp', 0, 0,...  12.3 us
    all_to_all x1, blocking collectives, local(): lax.all_to_all(jnp.broadcast_to(cotangent[None], (chips, piece, out_width...  11.6 us
    ppermute x1, starting transfers between devices, local(): far = lax.ppermute(near, 'tp', swap)  7.81 us
    ppermute x1, starting transfers between devices, local(): lax.ppermute(theirs, 'tp', swap)  5.45 us
    pallas_call x1, Pallas kernels, local(): call(functools.partial(pre_kernel, heads), [((n, full), F32), ((heads, 8,...  2.2 us
    pallas_call x1, Pallas kernels, local(): call(functools.partial(mid_kernel, heads), [((workers * ROWS, size), BF),...  2.11 us
  transfers between devices with their start and end apart: 2, of which 0 were waited for; matrix products, arithmetic and copies ran while one was open for 0% of the time, Pallas kernels for 4%

profile of v10, /device:TPU:1, one launch (start us, length us, event | category | flops | bytes accessed | tf_op | source)
XLA Modules:
  0.0 93.7 jit_solution(2813717617205024104)
XLA Ops:
  0.6 0.0 copy-start.2
  0.6 0.0 copy-start.3
  0.7 0.0 copy-start.1
  0.7 0.0 copy-start.4
  0.7 1.0 %broadcast_in_dim.2 = bf16[4,16,4096]{2,1,0:T(8,128)(2,1)S(1)} broadcast(bf16[16,4096]{1,0:T(8,128)(2,1)} %param.13), dimensions={1,2} | broadcast | bytes 655360 | tf_op jit(solution)/shard_map/broadcast_in_dim | solution.py:346
  1.7 11.6 %all_to_all.20.near_ref = bf16[4,16,4096]{2,1,0:T(8,128)(2,1)S(1)} all-to-all(bf16[4,16,4096]{2,1,0:T(8,128)(2,1)S(1)} %broadcast_in_dim.2), channel_id=1, replica_groups={{0,2,4,6},{1,3,5,7},{8,10,12,14},{9,11,13,15},{16,18,20,22},{17,19,21,2..., dimensions={0} | all-to-all | bytes 1048576 | tf_op jit(solution)/shard_map/all_to_all | solution.py:345
  13.2 0.0 copy-start
  13.2 7.8 %collective-permute-start = (bf16[4,16,4096]{2,1,0:T(8,128)(2,1)S(1)}, bf16[4,16,4096]{2,1,0:T(8,128)(2,1)S(1)}, u32[]{:S(2)}, u32[]{:S(2)}) collective-permute-start(bf16[4,16,4096]{2,1,0:T(8,128)(2,1)S(1)} %all_to_all.20.near_ref), channel_id=1, source_target_pairs={{0,1},{1,0},{2,3},{3,2},{4,5},{5,4},{6,7},{7,6},{8,9},{9,8},{10,11... | collective-permute-start | bytes 1572872 | tf_op jit(solution)/shard_map/ppermute | solution.py:349
  21.1 0.0 copy-done.2
  21.1 0.0 copy-done.3
  21.1 0.0 copy-done.1
  21.1 0.0 copy-done.4
  21.1 2.2 %shard_map.118 = (f32[128,512]{1,0:T(8,128)S(1)}, f32[4,8,128]{2,1,0:T(8,128)S(1)}, f32[8,128]{1,0:T(8,128)S(1)}, bf16[4,128,128]{2,1,0:T(8,128)(2,1)S(1)}, f32[...) custom-call(bf16[128,512]{1,0:T(8,128)(2,1)S(1)} %copy-done.1, ...), custom_call_target="tpu_custom_call" | custom-call | tf_op jit(solution)/shard_map/pallas_call | solution.py:350
  23.3 0.0 collective-permute-done.far_ref
  23.3 0.0 copy-done
  23.3 2.1 %shard_map.119 = (bf16[1152,128]{1,0:T(8,128)(2,1)S(1)}, f32[128,512]{1,0:T(8,128)S(1)}) custom-call(bf16[4,16,4096]{2,1,0:T(8,128)(2,1)S(1)} %all_to_all.20.near_ref, bf16[4,16,4096]{2,1,0:T(8,128)(2,1)S(1)} %collective-permute-done.far_ref, bf16[512,4096]{1,0:T(8,128)(2,1)} %w_hbm.5, bf16[128,128]{1,0:T(8,128)(2,1)S(1)} %copy-done.2, ...), custom_call_target="tpu_custom_call" | custom-call | tf_op jit(solution)/shard_map/pallas_call | solution.py:357
  25.4 27.8 %all_to_all.21 = bf16[64,9,2,128]{3,2,1,0:T(2,128)(2,1)S(1)} all-to-all(bf16[64,9,2,128]{3,2,1,0:T(2,128)(2,1)S(1)} %bitcast.4), channel_id=1, replica_groups=mesh['ctx'=64,'tp'=8] {'ctx'}, dimensions={0} | all-to-all | bytes 589824 | tf_op jit(solution)/shard_map/all_to_all | solution.py:364
  53.2 0.3 shard_map.120
  53.5 17.8 %all_to_all.22.back_ref = bf16[64,16,128]{2,1,0:T(8,128)(2,1)S(1)} all-to-all(bf16[64,16,128]{2,1,0:T(8,128)(2,1)S(1)} %shard_map.120), channel_id=1, replica_groups=mesh['ctx'=64,'tp'=8] {'ctx'}, dimensions={0} | all-to-all | bytes 524288 | tf_op jit(solution)/shard_map/all_to_all | solution.py:370
  71.3 2.0 %shard_map.121 = (bf16[64,4352]{1,0:T(8,128)(2,1)S(1)}, bf16[64,4352]{1,0:T(8,128)(2,1)S(1)}) custom-call(bf16[64,16,128]{2,1,0:T(8,128)(2,1)S(1)} %all_to_all.22.back_ref, bf16[128,512]{1,0:T(8,128)(2,1)S(1)} %copy-done.1, bf16[128,128]{1,0:T(8,128)(2,1)S(1)} %copy-done.3, bf16[128,128]{1,0:T(8,128)(2,1)S(1)} %copy-done.2, bf16[512,4096]{1,0:T(8,128)(2,1)} %w_hbm.5, ...), custom_call_target="tpu_custom_call" | custom-call | tf_op jit(solution)/shard_map/pallas_call | solution.py:372
  73.3 5.4 %collective-permute-start.1 = (bf16[64,4352]{1,0:T(8,128)(2,1)S(1)}, bf16[64,4352]{1,0:T(8,128)(2,1)S(1)}, u32[]{:S(2)}, u32[]{:S(2)}) collective-permute-start(bf16[64,4352]{1,0:T(8,128)(2,1)S(1)} %get-tuple-element.35), channel_id=1, source_target_pairs={{0,1},{1,0},{2,3},{3,2},{4,5},{5,4},{6,7},{7,6},{8,9},{9,8},{10,11... | collective-permute-start | bytes 1671176 | tf_op jit(solution)/shard_map/ppermute | solution.py:385
  78.7 1.8 %shard_map.122 = (bf16[128,512]{1,0:T(8,128)(2,1)}, bf16[128,512]{1,0:T(8,128)(2,1)}, f32[4,128]{1,0:T(4,128)}) custom-call(bf16[64,16,128]{2,1,0:T(8,128)(2,1)S(1)} %all_to_all.22.back_ref, bf16[128,512]{1,0:T(8,128)(2,1)S(1)} %copy-done.1, bf16[128,128]{1,0:T(8,128)(2,1)S(1)} %copy-done.3, bf16[128,128]{1,0:T(8,128)(2,1)S(1)} %copy-done.2, ...), custom_call_target="tpu_custom_call" | custom-call | tf_op jit(solution)/shard_map/pallas_call | solution.py:379
  80.5 0.0 collective-permute-done.1
  80.5 0.1 add_convert_fusion
  80.7 12.3 %all_to_all.23.part_ref = bf16[4,16,4352]{2,1,0:T(8,128)(2,1)S(1)} all-to-all(bf16[4,16,4352]{2,1,0:T(8,128)(2,1)S(1)} %bitcast.5), channel_id=1, replica_groups={{0,2,4,6},{1,3,5,7},{8,10,12,14},{9,11,13,15},{16,18,20,22},{17,19,21,2..., dimensions={0} | all-to-all | bytes 1114112 | tf_op jit(solution)/shard_map/all_to_all | solution.py:387
  93.0 0.7 shard_map.123
Async XLA Ops:
  0.6 20.4 %copy-start.2 = (bf16[128,128]{1,0:T(8,128)(2,1)S(1)}, bf16[128,128]{1,0:T(8,128)(2,1)}, u32[]{:S(2)}) copy-start(bf16[128,128]{1,0:T(8,128)(2,1)} %c_hbm.7) | copy-start | bytes 98308
  0.6 20.4 %copy-start.3 = (bf16[128,128]{1,0:T(8,128)(2,1)S(1)}, bf16[128,128]{1,0:T(8,128)(2,1)}, u32[]{:S(2)}) copy-start(bf16[128,128]{1,0:T(8,128)(2,1)} %b_hbm.5) | copy-start | bytes 98308
  0.7 20.4 %copy-start.1 = (bf16[128,512]{1,0:T(8,128)(2,1)S(1)}, bf16[128,512]{1,0:T(8,128)(2,1)}, u32[]{:S(2)}) copy-start(bf16[128,512]{1,0:T(8,128)(2,1)} %x_hbm.5) | copy-start | bytes 393220
  0.7 20.4 %copy-start.4 = (f32[4,128]{1,0:T(4,128)S(1)}, f32[4,128]{1,0:T(4,128)}, u32[]{:S(2)}) copy-start(f32[4,128]{1,0:T(4,128)} %ld_hbm.1) | copy-start | bytes 6148
  13.2 10.1 %copy-start = (bf16[128,512]{1,0:T(8,128)(2,1)S(1)}, bf16[128,512]{1,0:T(8,128)(2,1)}, u32[]{:S(2)}) copy-start(bf16[128,512]{1,0:T(8,128)(2,1)} %gate_hbm.5) | copy-start | bytes 393220
  13.2 10.1 %collective-permute-start = (bf16[4,16,4096]{2,1,0:T(8,128)(2,1)S(1)}, bf16[4,16,4096]{2,1,0:T(8,128)(2,1)S(1)}, u32[]{:S(2)}, u32[]{:S(2)}) collective-permute-start(bf16[4,16,4096]{2,1,0:T(8,128)(2,1)S(1)} %all_to_all.20.near_ref), channel_id=1, source_target_pairs={{0,1},{1,0},{2,3},{3,2},{4,5},{5,4},{6,7},{7,6},{8,9},{9,8},{10,11... | collective-permute-start | bytes 1572872 | tf_op jit(solution)/shard_map/ppermute | solution.py:349
  73.3 7.3 %collective-permute-start.1 = (bf16[64,4352]{1,0:T(8,128)(2,1)S(1)}, bf16[64,4352]{1,0:T(8,128)(2,1)S(1)}, u32[]{:S(2)}, u32[]{:S(2)}) collective-permute-start(bf16[64,4352]{1,0:T(8,128)(2,1)S(1)} %get-tuple-element.35), channel_id=1, source_target_pairs={{0,1},{1,0},{2,3},{3,2},{4,5},{5,4},{6,7},{7,6},{8,9},{9,8},{10,11... | collective-permute-start | bytes 1671176 | tf_op jit(solution)/shard_map/ppermute | solution.py:385

commit v11 on v9

--- a/solution.py
+++ b/solution.py
@@ -382,8 +382,7 @@
         11, range(1, 5),
         [lanes, lanes, rows, small, small, rows, pltpu.SemaphoreType.DMA((4,))],
     )(back, inputs, b_proj, c_proj, gate_in, dg, cum, mixt, scores, yi, dec)
-    other, grad_inputs = lax.optimization_barrier((lax.ppermute(theirs, "tp", swap), grad_inputs))
-    part = (mine.astype(F32) + other.astype(F32)).astype(BF)
+    part = (mine.astype(F32) + lax.ppermute(theirs, "tp", swap).astype(F32)).astype(BF)
     part = lax.all_to_all(
         part.reshape(chips, piece, out_width + 2 * n),
         "tp", 0, 0, tiled=True, axis_index_groups=across,

time: 93.9 us -> 95.5 us (1.017)
  blocking collectives: 69.1 us -> 57.2 us
  waiting for transfers between devices: 0.01 us -> 9.34 us
  starting transfers between devices: 13.3 us -> 16.7 us
    all_to_all x1 -> x0, blocking collectives: 11.9 us -> none  [local(): lax.all_to_all(part.reshape(chips, piece, out_width + 2 * n), 'tp', 0, 0,...]
    all_to_all x0 -> x1, waiting for transfers between devices: none -> 7.78 us  [local(): lax.all_to_all(part.reshape(chips, piece, out_width + 2 * n), 'tp', 0, 0,...]
    all_to_all x0 -> x1, starting transfers between devices: none -> 3.47 us  [local(): lax.all_to_all(part.reshape(chips, piece, out_width + 2 * n), 'tp', 0, 0,...]
    ppermute x1, waiting for transfers between devices: 0.01 us -> 1.56 us  [local(): lax.ppermute(theirs, 'tp', swap).astype(F32)]
  transfers between devices with their start and end apart: 2 -> 3, of which waited for: 0 -> 2; matrix products, arithmetic and copies ran while one was open for 0% -> 0% of each run, Pallas kernels for 4% -> 4%
where the time goes in v11:
time: 95.5 us; the launch traced here: 95.1 us
  blocking collectives  57.2 us (60%)
  starting transfers between devices  16.7 us (17%)
  waiting for transfers between devices  9.34 us (10%)
  Pallas kernels  9.15 us (10%)
  local copies, waits for them, and re-layouts  1 us (1%)
    all_to_all x1, blocking collectives, local(): lax.all_to_all(msg.reshape(workers, ROWS // 2, 2, size), 'ctx', 0, 0, til...  27.8 us
    all_to_all x1, blocking collectives, local(): back = lax.all_to_all(back, 'ctx', 0, 0, tiled=True)  17.8 us
    all_to_all x1, blocking collectives, local(): lax.all_to_all(jnp.broadcast_to(cotangent[None], (chips, piece, out_width...  11.6 us
    ppermute x1, starting transfers between devices, local(): far = lax.ppermute(near, 'tp', swap)  7.81 us
    all_to_all x1, waiting for transfers between devices, local(): lax.all_to_all(part.reshape(chips, piece, out_width + 2 * n), 'tp', 0, 0,...  7.78 us
    ppermute x1, starting transfers between devices, local(): lax.ppermute(theirs, 'tp', swap).astype(F32)  5.45 us
    all_to_all x1, starting transfers between devices, local(): lax.all_to_all(part.reshape(chips, piece, out_width + 2 * n), 'tp', 0, 0,...  3.47 us
    pallas_call x1, Pallas kernels, local(): call(functools.partial(mid_kernel, heads), [((workers * ROWS, size), BF),...  2.25 us
  transfers between devices with their start and end apart: 3, of which 2 were waited for; matrix products, arithmetic and copies ran while one was open for 0% of the time, Pallas kernels for 4%

profile of v11, /device:TPU:1, one launch (start us, length us, event | category | flops | bytes accessed | tf_op | source)
XLA Modules:
  0.0 95.1 jit_solution(16509193792158751359)
XLA Ops:
  0.6 0.0 copy-start.2
  0.6 0.0 copy-start.3
  0.7 0.0 copy-start.1
  0.7 0.0 copy-start.4
  0.7 1.0 %broadcast_in_dim.2 = bf16[4,16,4096]{2,1,0:T(8,128)(2,1)S(1)} broadcast(bf16[16,4096]{1,0:T(8,128)(2,1)} %param.13), dimensions={1,2} | broadcast | bytes 655360 | tf_op jit(solution)/shard_map/broadcast_in_dim | solution.py:346
  1.7 11.6 %all_to_all.20.near_ref = bf16[4,16,4096]{2,1,0:T(8,128)(2,1)S(1)} all-to-all(bf16[4,16,4096]{2,1,0:T(8,128)(2,1)S(1)} %broadcast_in_dim.2), channel_id=1, replica_groups={{0,2,4,6},{1,3,5,7},{8,10,12,14},{9,11,13,15},{16,18,20,22},{17,19,21,2..., dimensions={0} | all-to-all | bytes 1048576 | tf_op jit(solution)/shard_map/all_to_all | solution.py:345
  13.2 0.0 copy-start
  13.2 7.8 %collective-permute-start = (bf16[4,16,4096]{2,1,0:T(8,128)(2,1)S(1)}, bf16[4,16,4096]{2,1,0:T(8,128)(2,1)S(1)}, u32[]{:S(2)}, u32[]{:S(2)}) collective-permute-start(bf16[4,16,4096]{2,1,0:T(8,128)(2,1)S(1)} %all_to_all.20.near_ref), channel_id=1, source_target_pairs={{0,1},{1,0},{2,3},{3,2},{4,5},{5,4},{6,7},{7,6},{8,9},{9,8},{10,11... | collective-permute-start | bytes 1572872 | tf_op jit(solution)/shard_map/ppermute | solution.py:349
  21.1 0.0 copy-done.2
  21.1 0.0 copy-done.3
  21.1 0.0 copy-done.1
  21.1 0.0 copy-done.4
  21.1 2.0 %shard_map.118 = (f32[128,512]{1,0:T(8,128)S(1)}, f32[4,8,128]{2,1,0:T(8,128)S(1)}, f32[8,128]{1,0:T(8,128)S(1)}, bf16[4,128,128]{2,1,0:T(8,128)(2,1)S(1)}, f32[...) custom-call(bf16[128,512]{1,0:T(8,128)(2,1)S(1)} %copy-done.1, ...), custom_call_target="tpu_custom_call" | custom-call | tf_op jit(solution)/shard_map/pallas_call | solution.py:350
  23.1 0.0 collective-permute-done.far_ref
  23.1 0.0 copy-done
  23.1 2.2 %shard_map.119 = (bf16[1152,128]{1,0:T(8,128)(2,1)S(1)}, f32[128,512]{1,0:T(8,128)S(1)}) custom-call(bf16[4,16,4096]{2,1,0:T(8,128)(2,1)S(1)} %all_to_all.20.near_ref, bf16[4,16,4096]{2,1,0:T(8,128)(2,1)S(1)} %collective-permute-done.far_ref, bf16[512,4096]{1,0:T(8,128)(2,1)} %w_hbm.5, bf16[128,128]{1,0:T(8,128)(2,1)S(1)} %copy-done.2, ...), custom_call_target="tpu_custom_call" | custom-call | tf_op jit(solution)/shard_map/pallas_call | solution.py:357
  25.4 27.8 %all_to_all.21 = bf16[64,9,2,128]{3,2,1,0:T(2,128)(2,1)S(1)} all-to-all(bf16[64,9,2,128]{3,2,1,0:T(2,128)(2,1)S(1)} %bitcast.4), channel_id=1, replica_groups=mesh['ctx'=64,'tp'=8] {'ctx'}, dimensions={0} | all-to-all | bytes 589824 | tf_op jit(solution)/shard_map/all_to_all | solution.py:364
  53.2 0.3 shard_map.120
  53.5 17.8 %all_to_all.22.back_ref = bf16[64,16,128]{2,1,0:T(8,128)(2,1)S(1)} all-to-all(bf16[64,16,128]{2,1,0:T(8,128)(2,1)S(1)} %shard_map.120), channel_id=1, replica_groups=mesh['ctx'=64,'tp'=8] {'ctx'}, dimensions={0} | all-to-all | bytes 524288 | tf_op jit(solution)/shard_map/all_to_all | solution.py:370
  71.2 2.1 %shard_map.121 = (bf16[64,4352]{1,0:T(8,128)(2,1)S(1)}, bf16[64,4352]{1,0:T(8,128)(2,1)S(1)}) custom-call(bf16[64,16,128]{2,1,0:T(8,128)(2,1)S(1)} %all_to_all.22.back_ref, bf16[128,512]{1,0:T(8,128)(2,1)S(1)} %copy-done.1, bf16[128,128]{1,0:T(8,128)(2,1)S(1)} %copy-done.3, bf16[128,128]{1,0:T(8,128)(2,1)S(1)} %copy-done.2, bf16[512,4096]{1,0:T(8,128)(2,1)} %w_hbm.5, ...), custom_call_target="tpu_custom_call" | custom-call | tf_op jit(solution)/shard_map/pallas_call | solution.py:372
  73.4 5.4 %collective-permute-start.1 = (bf16[64,4352]{1,0:T(8,128)(2,1)S(1)}, bf16[64,4352]{1,0:T(8,128)(2,1)S(1)}, u32[]{:S(2)}, u32[]{:S(2)}) collective-permute-start(bf16[64,4352]{1,0:T(8,128)(2,1)S(1)} %get-tuple-element.33), channel_id=1, source_target_pairs={{0,1},{1,0},{2,3},{3,2},{4,5},{5,4},{6,7},{7,6},{8,9},{9,8},{10,11... | collective-permute-start | bytes 1671176 | tf_op jit(solution)/shard_map/ppermute | solution.py:385
  78.8 1.6 %collective-permute-done.1 = bf16[64,4352]{1,0:T(8,128)(2,1)S(1)} collective-permute-done((bf16[64,4352]{1,0:T(8,128)(2,1)S(1)}, bf16[64,4352]{1,0:T(8,128)(2,1)S(1)}, u32[]{:S(2)}, u32[]{:S(2)}) %collective-permute-start.1) | collective-permute-done | bytes 557088 | tf_op jit(solution)/shard_map/ppermute | solution.py:385
  80.4 0.9 add_convert_fusion
  81.3 3.5 %all-to-all-start.3 = ((bf16[4,16,4352]{2,1,0:T(8,128)(2,1)}), bf16[4,16,4352]{2,1,0:T(8,128)(2,1)S(1)}, u32[]{:S(2)}, u32[]{:S(2)}) async-start(bf16[4,16,4352]{2,1,0:T(8,128)(2,1)} %bitcast.2), calls=%async_computation.3 | async-start | bytes 1114112 | tf_op jit(solution)/shard_map/all_to_all | solution.py:386
  84.8 1.8 %shard_map.123 = (bf16[128,512]{1,0:T(8,128)(2,1)}, bf16[128,512]{1,0:T(8,128)(2,1)}, f32[4,128]{1,0:T(4,128)}) custom-call(bf16[64,16,128]{2,1,0:T(8,128)(2,1)S(1)} %all_to_all.22.back_ref, bf16[128,512]{1,0:T(8,128)(2,1)S(1)} %copy-done.1, bf16[128,128]{1,0:T(8,128)(2,1)S(1)} %copy-done.3, bf16[128,128]{1,0:T(8,128)(2,1)S(1)} %copy-done.2, ...), custom_call_target="tpu_custom_call" | custom-call | tf_op jit(solution)/shard_map/pallas_call | solution.py:379
  86.6 7.8 %all-to-all-done.3.part_ref = bf16[4,16,4352]{2,1,0:T(8,128)(2,1)S(1)} async-done(((bf16[4,16,4352]{2,1,0:T(8,128)(2,1)}), bf16[4,16,4352]{2,1,0:T(8,128)(2,1)S(1)}, u32[]{:S(2)}, u32[]{:S(2)}) %all-to-all-start.3) | async-done | bytes 557088 | tf_op jit(solution)/shard_map/all_to_all | solution.py:386
  94.4 0.7 shard_map.122
Async XLA Ops:
  0.6 20.4 %copy-start.2 = (bf16[128,128]{1,0:T(8,128)(2,1)S(1)}, bf16[128,128]{1,0:T(8,128)(2,1)}, u32[]{:S(2)}) copy-start(bf16[128,128]{1,0:T(8,128)(2,1)} %c_hbm.7) | copy-start | bytes 98308
  0.6 20.4 %copy-start.3 = (bf16[128,128]{1,0:T(8,128)(2,1)S(1)}, bf16[128,128]{1,0:T(8,128)(2,1)}, u32[]{:S(2)}) copy-start(bf16[128,128]{1,0:T(8,128)(2,1)} %b_hbm.5) | copy-start | bytes 98308
  0.7 20.4 %copy-start.1 = (bf16[128,512]{1,0:T(8,128)(2,1)S(1)}, bf16[128,512]{1,0:T(8,128)(2,1)}, u32[]{:S(2)}) copy-start(bf16[128,512]{1,0:T(8,128)(2,1)} %x_hbm.5) | copy-start | bytes 393220
  0.7 20.4 %copy-start.4 = (f32[4,128]{1,0:T(4,128)S(1)}, f32[4,128]{1,0:T(4,128)}, u32[]{:S(2)}) copy-start(f32[4,128]{1,0:T(4,128)} %ld_hbm.1) | copy-start | bytes 6148
  13.2 9.9 %copy-start = (bf16[128,512]{1,0:T(8,128)(2,1)S(1)}, bf16[128,512]{1,0:T(8,128)(2,1)}, u32[]{:S(2)}) copy-start(bf16[128,512]{1,0:T(8,128)(2,1)} %gate_hbm.5) | copy-start | bytes 393220
  13.2 9.9 %collective-permute-start = (bf16[4,16,4096]{2,1,0:T(8,128)(2,1)S(1)}, bf16[4,16,4096]{2,1,0:T(8,128)(2,1)S(1)}, u32[]{:S(2)}, u32[]{:S(2)}) collective-permute-start(bf16[4,16,4096]{2,1,0:T(8,128)(2,1)S(1)} %all_to_all.20.near_ref), channel_id=1, source_target_pairs={{0,1},{1,0},{2,3},{3,2},{4,5},{5,4},{6,7},{7,6},{8,9},{9,8},{10,11... | collective-permute-start | bytes 1572872 | tf_op jit(solution)/shard_map/ppermute | solution.py:349
  73.4 7.0 %collective-permute-start.1 = (bf16[64,4352]{1,0:T(8,128)(2,1)S(1)}, bf16[64,4352]{1,0:T(8,128)(2,1)S(1)}, u32[]{:S(2)}, u32[]{:S(2)}) collective-permute-start(bf16[64,4352]{1,0:T(8,128)(2,1)S(1)} %get-tuple-element.33), channel_id=1, source_target_pairs={{0,1},{1,0},{2,3},{3,2},{4,5},{5,4},{6,7},{7,6},{8,9},{9,8},{10,11... | collective-permute-start | bytes 1671176 | tf_op jit(solution)/shard_map/ppermute | solution.py:385
  81.3 13.0 %all-to-all-start.3 = ((bf16[4,16,4352]{2,1,0:T(8,128)(2,1)}), bf16[4,16,4352]{2,1,0:T(8,128)(2,1)S(1)}, u32[]{:S(2)}, u32[]{:S(2)}) async-start(bf16[4,16,4352]{2,1,0:T(8,128)(2,1)} %bitcast.2), calls=%async_computation.3 | async-start | bytes 1114112 | tf_op jit(solution)/shard_map/all_to_all | solution.py:386
